TPU v7x, 32 devices: a whole 2x2x4 slice. The times are simulated.
32 devices in a mesh: row: 4 (over y, x), col: 8 (over z, core).
Axes of the slice: x: 2, y: 2, z: 4, core: 2. Of those that a mesh axis runs over, the one named last changes fastest.
Arguments:
- tiles: float32 [4, 8, 3, 128, 64, 128], P('row', 'col'), may hold values from -0.0625 to 0.0625
- tile_coords: int32 [4, 8, 3, 2, 256], P('row', 'col'), may hold values from 0 to 15, as said below
- tile_count: int32 [4, 8, 3], P('row', 'col'), may hold values from 32 to 256, as said below
- seeds: int32 [128], replicated, may hold values from 0 to 4095
- chain: int32 [3], replicated, may hold values from 0 to 2
Outputs:
- answers: float32 [4096, 128], P(('row', 'col'))
Inputs may be any that keep to these rules, and one draw needn't show every extreme that they name: tile_coords[..., 0, :] is below 8 * 2 and tile_coords[..., 1, :] below 4 * 2; pairs may repeat. `tile_count`: each count is 256 divided by 1, 2, 4 or 8; for every relation some device has all 256 slots live.
All inputs are finite; a program needn't handle non-finite values.
Results may differ from a plain program's by a relative error of at most 0.0003.
Values sent between devices are 32-bit elements; how exact they have to be, the bound alone decides.
No kernel may reach another device: no remote copies, remote signals or barrier semaphores. Data moves between devices by JAX's collectives and lax.ppermute only.
A program may use at most 128 MiB of HBM per device.

v0:
```python
import functools

import jax
import jax.numpy as jnp
from jax import lax
from jax.experimental import pallas as pl
from jax.experimental.pallas import tpu as pltpu
from jax.sharding import PartitionSpec as P

QUERIES = 128
TILE = 64
BLOCKS_DEV = 2
HOPS = 3
ROWS_DEV = BLOCKS_DEV * TILE
LANES = 128
MIN_SHARE = 8


def place_tiles(step, in_pairs, flips, chain, counts, coords, tiles, buf, coord_buf, sems, coord_sem, accs):
    pairs = tiles.shape[1]
    chunk = pairs // MIN_SHARE
    relation = chain[step]
    live_chunks = counts[0, 0, relation] // (2 * chunk)
    row_flip, col_flip = flips[0], flips[1]
    copy_coords = pltpu.make_async_copy(coords.at[relation], coord_buf, coord_sem)
    copy_coords.start()

    def chunk_copy(index):
        span = pl.ds(index * chunk, chunk)
        return pltpu.make_async_copy(tiles.at[relation, span], buf.at[span], sems.at[index])

    for index in range(MIN_SHARE):
        @pl.when(index < live_chunks)
        def _(index=index):
            chunk_copy(index).start()

    acc_even, acc_odd = accs[0], accs[-1]
    blocks = acc_even.shape[0]

    @pl.loop(0, blocks // 4)
    def _(b):
        for u in range(4):
            for acc in accs:
                acc[b * 4 + u] = jnp.zeros((TILE, LANES), jnp.float32)

    half_of_lane = lax.broadcasted_iota(jnp.int32, (TILE, LANES), 1) // TILE
    copy_coords.wait()

    def add_pair(t):
        values = buf[t]
        rolled = pltpu.roll(values, TILE, 1)
        for odd, acc in ((0, acc_even), (1, acc_odd)):
            i = coord_buf[0, 2 * t + odd] ^ row_flip
            j = coord_buf[1, 2 * t + odd] ^ col_flip
            half = j & 1
            at = i * in_pairs + (j >> 1)
            moved = jnp.where(half == odd, values, rolled)
            acc[at] = acc[at] + jnp.where(half_of_lane == half, moved, 0.0)

    @pl.loop(0, live_chunks)
    def _(index):
        chunk_copy(index).wait()

        @pl.loop(0, chunk // 4)
        def _(t):
            for u in range(4):
                add_pair(index * chunk + t * 4 + u)


def split(x):
    high = x.astype(jnp.bfloat16)
    return high, (x - high.astype(jnp.float32)).astype(jnp.bfloat16)


def fold(accs, out_blocks, in_pairs, highs, lows):
    @pl.loop(0, out_blocks)
    def _(i):
        away = (i // BLOCKS_DEV) & 1
        at = pl.multiple_of((i // (2 * BLOCKS_DEV)) * ROWS_DEV + (i & 1) * TILE, TILE)
        for jp in range(in_pairs):
            value = accs[0][i * in_pairs + jp]
            if len(accs) == 2:
                value = value + accs[1][i * in_pairs + jp]
            high, low = split(value)
            highs[away, pl.ds(at, TILE), jp * LANES:(jp + 1) * LANES] = high
            lows[away, pl.ds(at, TILE), jp * LANES:(jp + 1) * LANES] = low


def first_kernel(out_blocks, in_pairs, chain, counts, flips, targets, coords, tiles, keep, send,
                 buf, coord_buf, sems, coord_sem, highs, lows, *accs):
    place_tiles(0, in_pairs, flips, chain, counts, coords, tiles, buf, coord_buf, sems, coord_sem, accs)
    fold(accs, out_blocks, in_pairs, highs, lows)
    depth = in_pairs * LANES
    entity = lax.broadcasted_iota(jnp.int32, (depth, QUERIES), 0)
    states = (entity == targets[...]).astype(jnp.float32).astype(jnp.bfloat16)
    for away, out in ((1, send), (0, keep)):
        out[...] = jnp.dot(highs[away], states, preferred_element_type=jnp.float32) + jnp.dot(
            lows[away], states, preferred_element_type=jnp.float32)


def dense_kernel(step, out_blocks, in_pairs, chain, counts, flips, coords, tiles, highs, lows,
                 buf, coord_buf, sems, coord_sem, *accs):
    place_tiles(step, in_pairs, flips, chain, counts, coords, tiles, buf, coord_buf, sems, coord_sem, accs)
    fold(accs, out_blocks, in_pairs, highs, lows)


def product_kernel(parts, highs, lows, *refs):
    pieces, (keep, send, weights) = refs[:parts], refs[parts:]
    for k, piece in enumerate(pieces):
        high, low = split(piece[...])
        weights[k * ROWS_DEV:(k + 1) * ROWS_DEV, :QUERIES] = high
        weights[k * ROWS_DEV:(k + 1) * ROWS_DEV, QUERIES:] = low
    for away, out in ((1, send), (0, keep)):
        both = jnp.dot(highs[away], weights[...], preferred_element_type=jnp.float32)
        rest = jnp.dot(lows[away], weights[:, :QUERIES], preferred_element_type=jnp.float32)
        out[...] = both[:, :QUERIES] + (both[:, QUERIES:] + rest)


def shards(tiles, tile_coords, tile_count, seeds, chain):
    row_total = lax.axis_size("row")
    col_total = lax.axis_size("col")
    my_row = lax.axis_index("row")
    my_col = lax.axis_index("col")
    out_blocks = col_total * BLOCKS_DEV
    in_pairs = row_total
    depth_total = col_total // 2
    rows_out = depth_total * ROWS_DEV
    rows_in = in_pairs * LANES
    relations, pairs = tiles.shape[2], tiles.shape[3]
    f32, bf16 = jnp.float32, jnp.bfloat16

    tiles = tiles.reshape(relations, pairs, TILE, 2 * TILE)
    coords = tile_coords.reshape(relations, 2, 2 * pairs)
    flips = jnp.stack([my_col * BLOCKS_DEV, my_row * BLOCKS_DEV]).astype(jnp.int32)
    block = seeds // ROWS_DEV
    targets = jnp.where(block % col_total == my_col,
                        ((block // col_total) ^ my_row) * ROWS_DEV + seeds % ROWS_DEV, -1)[None, :]

    small = out_blocks * in_pairs * TILE * LANES * 4 <= 4 << 20
    smem = pl.BlockSpec(memory_space=pltpu.SMEM)
    vmem = pl.BlockSpec(memory_space=pltpu.VMEM)
    hbm = pl.BlockSpec(memory_space=pl.ANY)
    params = pltpu.CompilerParams(vmem_limit_bytes=60 << 20)
    work = [
        pltpu.VMEM((pairs, TILE, 2 * TILE), f32),
        pltpu.SMEM((2, 2 * pairs), jnp.int32),
        pltpu.SemaphoreType.DMA((MIN_SHARE,)),
        pltpu.SemaphoreType.DMA(()),
    ]
    accs = [pltpu.VMEM((out_blocks * in_pairs, TILE, LANES), f32)] * (2 if small else 1)
    dense = jax.ShapeDtypeStruct((2, rows_out, rows_in), bf16)
    partial = jax.ShapeDtypeStruct((rows_out, QUERIES), f32)

    def first():
        return pl.pallas_call(
            functools.partial(first_kernel, out_blocks, in_pairs),
            out_shape=[partial, partial],
            in_specs=[smem, smem, smem, vmem, hbm, hbm],
            out_specs=[vmem, vmem],
            scratch_shapes=work + [pltpu.VMEM(dense.shape, bf16)] * 2 + accs,
            compiler_params=params,
            name="first",
        )(chain, tile_count, flips, targets, coords, tiles)

    def densify(step):
        return pl.pallas_call(
            functools.partial(dense_kernel, step, out_blocks, in_pairs),
            out_shape=[dense, dense],
            in_specs=[smem, smem, smem, hbm, hbm],
            out_specs=[vmem, vmem],
            scratch_shapes=work + accs,
            compiler_params=params,
            cost_estimate=pl.CostEstimate(flops=0, bytes_accessed=8 << 20, transcendentals=0),
            name=f"densify{step}",
        )(chain, tile_count, flips, coords, tiles)

    def product(highs, lows, pieces):
        return pl.pallas_call(
            functools.partial(product_kernel, len(pieces)),
            out_shape=[partial, partial],
            in_specs=[vmem] * (2 + len(pieces)),
            out_specs=[vmem, vmem],
            scratch_shapes=[pltpu.VMEM((rows_in, 2 * QUERIES), bf16)],
            compiler_params=params,
            name="product",
        )(highs, lows, *pieces)

    def swap(x, axis, size, flip):
        return lax.ppermute(x, axis, [(i, i ^ flip) for i in range(size)])

    keep, send = first()
    for step in range(HOPS):
        summed = keep + swap(send, "col", col_total, 1)
        arrived = [
            swap(summed[k * ROWS_DEV:(k + 1) * ROWS_DEV], "col", col_total, 2 * k)
            for k in range(1, depth_total)
        ]
        owned = summed[:ROWS_DEV]
        for part in arrived:
            owned = owned + part
        if step + 1 < HOPS:
            highs, lows = densify(step + 1)
            pieces = [owned] + [swap(owned, "row", row_total, k) for k in range(1, row_total)]
            keep, send = product(highs, lows, pieces)

    squares = jnp.sum(owned * owned, axis=0, keepdims=True)
    devices = row_total * col_total
    shared = lax.all_to_all(
        jnp.broadcast_to(squares, (devices, QUERIES)), ("row", "col"), 0, 0, tiled=True)
    totals = jnp.sum(shared, axis=0)
    return owned * lax.rsqrt(totals / (devices * ROWS_DEV) + 1e-06)


def solution(mesh):
    in_specs = (
        P("row", "col", None, None, None, None),
        P("row", "col", None, None, None),
        P("row", "col", None),
        P(),
        P(),
    )
    out_specs = P(("row", "col"), None)
    return jax.shard_map(shards, mesh=mesh, in_specs=in_specs, out_specs=out_specs, check_vma=False)
```

profile of v0, /device:TPU:0, one launch (start us, length us, event | category | flops | bytes accessed | tf_op | source)
XLA Modules:
  0.0 88.8 jit_solution(13475185859257201969)
XLA Ops:
  0.0 1.2 %fusion.7.targets = s32[1,128]{1,0:T(1,128)} fusion(s32[128]{0:T(128)} %param.8, s32[]{:T(128)S(6)} %axis_index.25, s32[]{:T(128)S(6)} %axis_index.22), kind=kLoop, calls=%fused_computation.25 | loop fusion | flops 5504 | bytes 1032 | tf_op jit(solution)/shard_map/broadcast_in_dim | solution.py:136
  1.8 5.6 %first.1 = (f32[512,128]{1,0:T(8,128)}, f32[512,128]{1,0:T(8,128)}) custom-call(s32[3]{0:T(128)} %chain.5, s32[1,1,3]{2,1,0:T(1,128)} %counts.5, s32[2]{0:T(128)} %pad_add_fusion.flips, s32[1,128]{1,0:T(1,128)} %fusion.7.targets, s32[3,2,256]{2,1,0:T(2,128)} %bitcast.11, f32[3,128,64,128]{3,2,1,0:T(8,128)} %bitcast.7), custom_call_target="tpu_custom_call" | custom-call | tf_op jit(solution)/shard_map/first/pallas_call | solution.py:155
  7.4 2.2 %collective-permute-start = (f32[512,128]{1,0:T(8,128)}, f32[512,128]{1,0:T(8,128)S(1)}, u32[]{:S(2)}, u32[]{:S(2)}) collective-permute-start(f32[512,128]{1,0:T(8,128)} %get-tuple-element.20), channel_id=1, source_target_pairs={{0,1},{1,0},{2,3},{3,2},{4,5},{5,4},{6,7},{7,6},{8,9},{9,8},{10,11... | collective-permute-start | bytes 786440 | tf_op jit(solution)/shard_map/ppermute | solution.py:189
  9.7 1.4 %collective-permute-done = f32[512,128]{1,0:T(8,128)S(1)} collective-permute-done((f32[512,128]{1,0:T(8,128)}, f32[512,128]{1,0:T(8,128)S(1)}, u32[]{:S(2)}, u32[]{:S(2)}) %collective-permute-start) | collective-permute-done | bytes 262176 | tf_op jit(solution)/shard_map/ppermute | solution.py:189
  12.1 2.5 %collective-permute-start.1 = (f32[128,128]{1,0:T(8,128)S(1)}, f32[128,128]{1,0:T(8,128)S(1)}, u32[]{:S(2)}, u32[]{:S(2)}) collective-permute-start(f32[128,128]{1,0:T(8,128)S(1)} %get-tuple-element.33), channel_id=1, source_target_pairs={{0,2},{1,3},{2,0},{3,1},{4,6},{5,7},{6,4},{7,5},{8,10},{9,11},{10,... | collective-permute-start | bytes 196616 | tf_op jit(solution)/shard_map/ppermute | solution.py:189
  14.5 2.5 %collective-permute-start.3 = (f32[128,128]{1,0:T(8,128)S(1)}, f32[128,128]{1,0:T(8,128)S(1)}, u32[]{:S(2)}, u32[]{:S(2)}) collective-permute-start(f32[128,128]{1,0:T(8,128)S(1)} %get-tuple-element.34), channel_id=1, source_target_pairs={{0,6},{1,7},{2,4},{3,5},{4,2},{5,3},{6,0},{7,1},{8,14},{9,15},{10,... | collective-permute-start | bytes 196616 | tf_op jit(solution)/shard_map/ppermute | solution.py:189
  17.1 4.2 %collective-permute-done.3 = f32[128,128]{1,0:T(8,128)S(1)} collective-permute-done((f32[128,128]{1,0:T(8,128)S(1)}, f32[128,128]{1,0:T(8,128)S(1)}, u32[]{:S(2)}, u32[]{:S(2)}) %collective-permute-start.3) | collective-permute-done | bytes 65568 | tf_op jit(solution)/shard_map/ppermute | solution.py:189
  21.4 2.2 %collective-permute-done.2 = f32[128,128]{1,0:T(8,128)S(1)} collective-permute-done((f32[128,128]{1,0:T(8,128)S(1)}, f32[128,128]{1,0:T(8,128)S(1)}, u32[]{:S(2)}, u32[]{:S(2)}) %collective-permute-start.2) | collective-permute-done | bytes 65568 | tf_op jit(solution)/shard_map/ppermute | solution.py:189
  23.6 3.0 %collective-permute-start.6 = (f32[128,128]{1,0:T(8,128)S(1)}, f32[128,128]{1,0:T(8,128)S(1)}, u32[]{:S(2)}, u32[]{:S(2)}) collective-permute-start(f32[128,128]{1,0:T(8,128)S(1)} %fusion.5.refs_0_), channel_id=1, source_target_pairs={{0,24},{8,16},{16,8},{24,0},{1,25},{9,17},{17,9},{25,1},{2,26},{10... | collective-permute-start | bytes 196616 | tf_op jit(solution)/shard_map/ppermute | solution.py:189
  27.2 5.4 %densify1.1 = (bf16[2,512,512]{2,1,0:T(8,128)(2,1)}, bf16[2,512,512]{2,1,0:T(8,128)(2,1)}) custom-call(s32[3]{0:T(128)} %chain.5, s32[1,1,3]{2,1,0:T(1,128)} %counts.5, s32[2]{0:T(128)} %pad_add_fusion.flips, s32[3,2,256]{2,1,0:T(2,128)} %bitcast.12, f32[3,128,64,128]{3,2,1,0:T(8,128)} %bitcast.8), custom_call_target="tpu_custom_call" | custom-call | bytes 8388608 | tf_op jit(solution)/shard_map/densify1/pallas_call | solution.py:166
  33.3 3.0 %product.2 = (f32[512,128]{1,0:T(8,128)}, f32[512,128]{1,0:T(8,128)}) custom-call(bf16[2,512,512]{2,1,0:T(8,128)(2,1)} %get-tuple-element.17.highs, bf16[2,512,512]{2,1,0:T(8,128)(2,1)} %get-tuple-element.18.lows, f32[128,128]{1,0:T(8,128)} %copy-done.1, f32[128,128]{1,0:T(8,128)} %copy-done.7, f32[128,128]{1,0:T(8,128)} %copy-done.5, f32[128,128]{1,0:T(8,128)} %copy-done.3), custom_call_target="tpu_custom_call" | custom-call | tf_op jit(solution)/shard_map/product/pallas_call | solution.py:178
  36.3 1.0 %collective-permute-start.7 = (f32[512,128]{1,0:T(8,128)}, f32[512,128]{1,0:T(8,128)S(1)}, u32[]{:S(2)}, u32[]{:S(2)}) collective-permute-start(f32[512,128]{1,0:T(8,128)} %get-tuple-element.22), channel_id=1, source_target_pairs={{0,1},{1,0},{2,3},{3,2},{4,5},{5,4},{6,7},{7,6},{8,9},{9,8},{10,11... | collective-permute-start | bytes 786440 | tf_op jit(solution)/shard_map/ppermute | solution.py:189
  37.4 1.4 %collective-permute-done.7 = f32[512,128]{1,0:T(8,128)S(1)} collective-permute-done((f32[512,128]{1,0:T(8,128)}, f32[512,128]{1,0:T(8,128)S(1)}, u32[]{:S(2)}, u32[]{:S(2)}) %collective-permute-start.7) | collective-permute-done | bytes 262176 | tf_op jit(solution)/shard_map/ppermute | solution.py:189
  40.8 2.5 %collective-permute-start.9 = (f32[128,128]{1,0:T(8,128)S(1)}, f32[128,128]{1,0:T(8,128)S(1)}, u32[]{:S(2)}, u32[]{:S(2)}) collective-permute-start(f32[128,128]{1,0:T(8,128)S(1)} %get-tuple-element.32), channel_id=1, source_target_pairs={{0,4},{1,5},{2,6},{3,7},{4,0},{5,1},{6,2},{7,3},{8,12},{9,13},{10,... | collective-permute-start | bytes 196616 | tf_op jit(solution)/shard_map/ppermute | solution.py:189
  44.2 2.6 %collective-permute-done.10 = f32[128,128]{1,0:T(8,128)S(1)} collective-permute-done((f32[128,128]{1,0:T(8,128)S(1)}, f32[128,128]{1,0:T(8,128)S(1)}, u32[]{:S(2)}, u32[]{:S(2)}) %collective-permute-start.10) | collective-permute-done | bytes 65568 | tf_op jit(solution)/shard_map/ppermute | solution.py:189
  46.8 2.8 %collective-permute-done.9 = f32[128,128]{1,0:T(8,128)S(1)} collective-permute-done((f32[128,128]{1,0:T(8,128)S(1)}, f32[128,128]{1,0:T(8,128)S(1)}, u32[]{:S(2)}, u32[]{:S(2)}) %collective-permute-start.9) | collective-permute-done | bytes 65568 | tf_op jit(solution)/shard_map/ppermute | solution.py:189
  49.6 3.6 %collective-permute-start.13 = (f32[128,128]{1,0:T(8,128)S(1)}, f32[128,128]{1,0:T(8,128)S(1)}, u32[]{:S(2)}, u32[]{:S(2)}) collective-permute-start(f32[128,128]{1,0:T(8,128)S(1)} %fusion.3.refs_0_), channel_id=1, source_target_pairs={{0,24},{8,16},{16,8},{24,0},{1,25},{9,17},{17,9},{25,1},{2,26},{10... | collective-permute-start | bytes 196616 | tf_op jit(solution)/shard_map/ppermute | solution.py:189
  53.9 4.2 %densify2.1 = (bf16[2,512,512]{2,1,0:T(8,128)(2,1)}, bf16[2,512,512]{2,1,0:T(8,128)(2,1)}) custom-call(s32[3]{0:T(128)} %chain.5, s32[1,1,3]{2,1,0:T(1,128)} %counts.5, s32[2]{0:T(128)} %pad_add_fusion.flips, s32[3,2,256]{2,1,0:T(2,128)} %bitcast.13, f32[3,128,64,128]{3,2,1,0:T(8,128)} %bitcast.9), custom_call_target="tpu_custom_call" | custom-call | bytes 8388608 | tf_op jit(solution)/shard_map/densify2/pallas_call | solution.py:166
  58.8 3.0 %product.3 = (f32[512,128]{1,0:T(8,128)}, f32[512,128]{1,0:T(8,128)}) custom-call(bf16[2,512,512]{2,1,0:T(8,128)(2,1)} %get-tuple-element.15.highs, bf16[2,512,512]{2,1,0:T(8,128)(2,1)} %get-tuple-element.16.lows, f32[128,128]{1,0:T(8,128)} %copy-done, f32[128,128]{1,0:T(8,128)} %copy-done.6, f32[128,128]{1,0:T(8,128)} %copy-done.4, f32[128,128]{1,0:T(8,128)} %copy-done.2), custom_call_target="tpu_custom_call" | custom-call | tf_op jit(solution)/shard_map/product/pallas_call | solution.py:178
  61.8 1.7 %collective-permute-done.14 = f32[512,128]{1,0:T(8,128)S(1)} collective-permute-done((f32[512,128]{1,0:T(8,128)}, f32[512,128]{1,0:T(8,128)S(1)}, u32[]{:S(2)}, u32[]{:S(2)}) %collective-permute-start.14) | collective-permute-done | bytes 262176 | tf_op jit(solution)/shard_map/ppermute | solution.py:189
  64.6 2.9 %collective-permute-start.17 = (f32[128,128]{1,0:T(8,128)S(1)}, f32[128,128]{1,0:T(8,128)S(1)}, u32[]{:S(2)}, u32[]{:S(2)}) collective-permute-start(f32[128,128]{1,0:T(8,128)S(1)} %get-tuple-element.28), channel_id=1, source_target_pairs={{0,6},{1,7},{2,4},{3,5},{4,2},{5,3},{6,0},{7,1},{8,14},{9,15},{10,... | collective-permute-start | bytes 196616 | tf_op jit(solution)/shard_map/ppermute | solution.py:189
  68.9 2.7 %collective-permute-done.17 = f32[128,128]{1,0:T(8,128)S(1)} collective-permute-done((f32[128,128]{1,0:T(8,128)S(1)}, f32[128,128]{1,0:T(8,128)S(1)}, u32[]{:S(2)}, u32[]{:S(2)}) %collective-permute-start.17) | collective-permute-done | bytes 65568 | tf_op jit(solution)/shard_map/ppermute | solution.py:189
  71.6 2.8 %collective-permute-done.16 = f32[128,128]{1,0:T(8,128)S(1)} collective-permute-done((f32[128,128]{1,0:T(8,128)S(1)}, f32[128,128]{1,0:T(8,128)S(1)}, u32[]{:S(2)}, u32[]{:S(2)}) %collective-permute-start.16) | collective-permute-done | bytes 65568 | tf_op jit(solution)/shard_map/ppermute | solution.py:189
  74.4 13.7 %all_to_all.6 = f32[32,1,128]{2,1,0:T(1,128)S(1)} all-to-all(f32[32,1,128]{2,1,0:T(1,128)S(1)} %broadcast_in_dim.7), channel_id=1, replica_groups=mesh['row'=4,'col'=8] {'row','col'}, dimensions={0} | all-to-all | bytes 32768 | tf_op jit(solution)/shard_map/all_to_all | solution.py:208
  (49 shorter events, 10.5 us)
Async XLA Ops:
  7.4 3.6 %collective-permute-start = (f32[512,128]{1,0:T(8,128)}, f32[512,128]{1,0:T(8,128)S(1)}, u32[]{:S(2)}, u32[]{:S(2)}) collective-permute-start(f32[512,128]{1,0:T(8,128)} %get-tuple-element.20), channel_id=1, source_target_pairs={{0,1},{1,0},{2,3},{3,2},{4,5},{5,4},{6,7},{7,6},{8,9},{9,8},{10,11... | collective-permute-start | bytes 786440 | tf_op jit(solution)/shard_map/ppermute | solution.py:189
  12.1 5.1 %collective-permute-start.1 = (f32[128,128]{1,0:T(8,128)S(1)}, f32[128,128]{1,0:T(8,128)S(1)}, u32[]{:S(2)}, u32[]{:S(2)}) collective-permute-start(f32[128,128]{1,0:T(8,128)S(1)} %get-tuple-element.33), channel_id=1, source_target_pairs={{0,2},{1,3},{2,0},{3,1},{4,6},{5,7},{6,4},{7,5},{8,10},{9,11},{10,... | collective-permute-start | bytes 196616 | tf_op jit(solution)/shard_map/ppermute | solution.py:189
  14.5 6.9 %collective-permute-start.3 = (f32[128,128]{1,0:T(8,128)S(1)}, f32[128,128]{1,0:T(8,128)S(1)}, u32[]{:S(2)}, u32[]{:S(2)}) collective-permute-start(f32[128,128]{1,0:T(8,128)S(1)} %get-tuple-element.34), channel_id=1, source_target_pairs={{0,6},{1,7},{2,4},{3,5},{4,2},{5,3},{6,0},{7,1},{8,14},{9,15},{10,... | collective-permute-start | bytes 196616 | tf_op jit(solution)/shard_map/ppermute | solution.py:189
  17.0 6.6 %collective-permute-start.2 = (f32[128,128]{1,0:T(8,128)S(1)}, f32[128,128]{1,0:T(8,128)S(1)}, u32[]{:S(2)}, u32[]{:S(2)}) collective-permute-start(f32[128,128]{1,0:T(8,128)S(1)} %get-tuple-element.35), channel_id=1, source_target_pairs={{0,4},{1,5},{2,6},{3,7},{4,0},{5,1},{6,2},{7,3},{8,12},{9,13},{10,... | collective-permute-start | bytes 196616 | tf_op jit(solution)/shard_map/ppermute | solution.py:189
  23.6 9.1 %copy-start.1 = (f32[128,128]{1,0:T(8,128)}, f32[128,128]{1,0:T(8,128)S(1)}, u32[]{:S(2)}) copy-start(f32[128,128]{1,0:T(8,128)S(1)} %fusion.5.refs_0_) | copy-start | bytes 196612
  23.6 9.1 %collective-permute-start.6 = (f32[128,128]{1,0:T(8,128)S(1)}, f32[128,128]{1,0:T(8,128)S(1)}, u32[]{:S(2)}, u32[]{:S(2)}) collective-permute-start(f32[128,128]{1,0:T(8,128)S(1)} %fusion.5.refs_0_), channel_id=1, source_target_pairs={{0,24},{8,16},{16,8},{24,0},{1,25},{9,17},{17,9},{25,1},{2,26},{10... | collective-permute-start | bytes 196616 | tf_op jit(solution)/shard_map/ppermute | solution.py:189
  26.6 6.1 %collective-permute-start.5 = (f32[128,128]{1,0:T(8,128)S(1)}, f32[128,128]{1,0:T(8,128)S(1)}, u32[]{:S(2)}, u32[]{:S(2)}) collective-permute-start(f32[128,128]{1,0:T(8,128)S(1)} %fusion.5.refs_0_), channel_id=1, source_target_pairs={{0,16},{8,24},{16,0},{24,8},{1,17},{9,25},{17,1},{25,9},{2,18},{10... | collective-permute-start | bytes 196616 | tf_op jit(solution)/shard_map/ppermute | solution.py:189
  26.9 5.8 %collective-permute-start.4 = (f32[128,128]{1,0:T(8,128)S(1)}, f32[128,128]{1,0:T(8,128)S(1)}, u32[]{:S(2)}, u32[]{:S(2)}) collective-permute-start(f32[128,128]{1,0:T(8,128)S(1)} %fusion.5.refs_0_), channel_id=1, source_target_pairs={{0,8},{8,0},{16,24},{24,16},{1,9},{9,1},{17,25},{25,17},{2,10},{10... | collective-permute-start | bytes 196616 | tf_op jit(solution)/shard_map/ppermute | solution.py:189
  32.7 0.6 copy-start.5
  32.7 0.6 copy-start.7
  36.3 2.4 %collective-permute-start.7 = (f32[512,128]{1,0:T(8,128)}, f32[512,128]{1,0:T(8,128)S(1)}, u32[]{:S(2)}, u32[]{:S(2)}) collective-permute-start(f32[512,128]{1,0:T(8,128)} %get-tuple-element.22), channel_id=1, source_target_pairs={{0,1},{1,0},{2,3},{3,2},{4,5},{5,4},{6,7},{7,6},{8,9},{9,8},{10,11... | collective-permute-start | bytes 786440 | tf_op jit(solution)/shard_map/ppermute | solution.py:189
  39.8 4.4 %collective-permute-start.8 = (f32[128,128]{1,0:T(8,128)S(1)}, f32[128,128]{1,0:T(8,128)S(1)}, u32[]{:S(2)}, u32[]{:S(2)}) collective-permute-start(f32[128,128]{1,0:T(8,128)S(1)} %get-tuple-element.30), channel_id=1, source_target_pairs={{0,2},{1,3},{2,0},{3,1},{4,6},{5,7},{6,4},{7,5},{8,10},{9,11},{10,... | collective-permute-start | bytes 196616 | tf_op jit(solution)/shard_map/ppermute | solution.py:189
  39.8 6.9 %collective-permute-start.10 = (f32[128,128]{1,0:T(8,128)S(1)}, f32[128,128]{1,0:T(8,128)S(1)}, u32[]{:S(2)}, u32[]{:S(2)}) collective-permute-start(f32[128,128]{1,0:T(8,128)S(1)} %get-tuple-element.31), channel_id=1, source_target_pairs={{0,6},{1,7},{2,4},{3,5},{4,2},{5,3},{6,0},{7,1},{8,14},{9,15},{10,... | collective-permute-start | bytes 196616 | tf_op jit(solution)/shard_map/ppermute | solution.py:189
  40.8 8.8 %collective-permute-start.9 = (f32[128,128]{1,0:T(8,128)S(1)}, f32[128,128]{1,0:T(8,128)S(1)}, u32[]{:S(2)}, u32[]{:S(2)}) collective-permute-start(f32[128,128]{1,0:T(8,128)S(1)} %get-tuple-element.32), channel_id=1, source_target_pairs={{0,4},{1,5},{2,6},{3,7},{4,0},{5,1},{6,2},{7,3},{8,12},{9,13},{10,... | collective-permute-start | bytes 196616 | tf_op jit(solution)/shard_map/ppermute | solution.py:189
  49.6 8.5 %copy-start = (f32[128,128]{1,0:T(8,128)}, f32[128,128]{1,0:T(8,128)S(1)}, u32[]{:S(2)}) copy-start(f32[128,128]{1,0:T(8,128)S(1)} %fusion.3.refs_0_) | copy-start | bytes 196612
  49.6 8.5 %collective-permute-start.13 = (f32[128,128]{1,0:T(8,128)S(1)}, f32[128,128]{1,0:T(8,128)S(1)}, u32[]{:S(2)}, u32[]{:S(2)}) collective-permute-start(f32[128,128]{1,0:T(8,128)S(1)} %fusion.3.refs_0_), channel_id=1, source_target_pairs={{0,24},{8,16},{16,8},{24,0},{1,25},{9,17},{17,9},{25,1},{2,26},{10... | collective-permute-start | bytes 196616 | tf_op jit(solution)/shard_map/ppermute | solution.py:189
  53.3 4.8 %collective-permute-start.12 = (f32[128,128]{1,0:T(8,128)S(1)}, f32[128,128]{1,0:T(8,128)S(1)}, u32[]{:S(2)}, u32[]{:S(2)}) collective-permute-start(f32[128,128]{1,0:T(8,128)S(1)} %fusion.3.refs_0_), channel_id=1, source_target_pairs={{0,16},{8,24},{16,0},{24,8},{1,17},{9,25},{17,1},{25,9},{2,18},{10... | collective-permute-start | bytes 196616 | tf_op jit(solution)/shard_map/ppermute | solution.py:189
  53.3 4.9 %collective-permute-start.11 = (f32[128,128]{1,0:T(8,128)S(1)}, f32[128,128]{1,0:T(8,128)S(1)}, u32[]{:S(2)}, u32[]{:S(2)}) collective-permute-start(f32[128,128]{1,0:T(8,128)S(1)} %fusion.3.refs_0_), channel_id=1, source_target_pairs={{0,8},{8,0},{16,24},{24,16},{1,9},{9,1},{17,25},{25,17},{2,10},{10... | collective-permute-start | bytes 196616 | tf_op jit(solution)/shard_map/ppermute | solution.py:189
  58.1 0.6 copy-start.4
  58.1 0.6 copy-start.6
  61.8 1.7 %collective-permute-start.14 = (f32[512,128]{1,0:T(8,128)}, f32[512,128]{1,0:T(8,128)S(1)}, u32[]{:S(2)}, u32[]{:S(2)}) collective-permute-start(f32[512,128]{1,0:T(8,128)} %get-tuple-element.24), channel_id=1, source_target_pairs={{0,1},{1,0},{2,3},{3,2},{4,5},{5,4},{6,7},{7,6},{8,9},{9,8},{10,11... | collective-permute-start | bytes 786440 | tf_op jit(solution)/shard_map/ppermute | solution.py:189
  64.6 4.3 %collective-permute-start.15 = (f32[128,128]{1,0:T(8,128)S(1)}, f32[128,128]{1,0:T(8,128)S(1)}, u32[]{:S(2)}, u32[]{:S(2)}) collective-permute-start(f32[128,128]{1,0:T(8,128)S(1)} %get-tuple-element.27), channel_id=1, source_target_pairs={{0,2},{1,3},{2,0},{3,1},{4,6},{5,7},{6,4},{7,5},{8,10},{9,11},{10,... | collective-permute-start | bytes 196616 | tf_op jit(solution)/shard_map/ppermute | solution.py:189
  64.6 7.0 %collective-permute-start.17 = (f32[128,128]{1,0:T(8,128)S(1)}, f32[128,128]{1,0:T(8,128)S(1)}, u32[]{:S(2)}, u32[]{:S(2)}) collective-permute-start(f32[128,128]{1,0:T(8,128)S(1)} %get-tuple-element.28), channel_id=1, source_target_pairs={{0,6},{1,7},{2,4},{3,5},{4,2},{5,3},{6,0},{7,1},{8,14},{9,15},{10,... | collective-permute-start | bytes 196616 | tf_op jit(solution)/shard_map/ppermute | solution.py:189
  67.6 6.8 %collective-permute-start.16 = (f32[128,128]{1,0:T(8,128)S(1)}, f32[128,128]{1,0:T(8,128)S(1)}, u32[]{:S(2)}, u32[]{:S(2)}) collective-permute-start(f32[128,128]{1,0:T(8,128)S(1)} %get-tuple-element.29), channel_id=1, source_target_pairs={{0,4},{1,5},{2,6},{3,7},{4,0},{5,1},{6,2},{7,3},{8,12},{9,13},{10,... | collective-permute-start | bytes 196616 | tf_op jit(solution)/shard_map/ppermute | solution.py:189
  (2 other events, 1.2 us)
where the time goes:
time: 88.8 us
  waiting for transfers between devices  23.6 us (27%)
  starting transfers between devices  23.2 us (26%)
  Pallas kernels  21.2 us (24%)
  blocking collectives  13.7 us (15%)
  other arithmetic  5.53 us (6%)
  local copies, waits for them, and re-layouts  1.33 us (1%)
    ppermute x18, waiting for transfers between devices, swap(): return lax.ppermute(x, axis, [(i, i ^ flip) for i in range(size)])  23.6 us
    ppermute x18, starting transfers between devices, swap(): return lax.ppermute(x, axis, [(i, i ^ flip) for i in range(size)])  23.2 us
    all_to_all x1, blocking collectives, shards(): lax.all_to_all(jnp.broadcast_to(squares, (devices, QUERIES)), ('row', 'co...  13.7 us
    pallas_call x2, Pallas kernels, densify(): pl.pallas_call(functools.partial(dense_kernel, step, out_blocks, in_pairs...  9.6 us
    pallas_call x2, Pallas kernels, product(): pl.pallas_call(functools.partial(product_kernel, len(pieces)), out_shape=...  6.02 us
    pallas_call x1, Pallas kernels, first(): pl.pallas_call(functools.partial(first_kernel, out_blocks, in_pairs), out...  5.6 us
    add x3, other arithmetic, shards(): summed = keep + swap(send, 'col', col_total, 1)  2.97 us
  transfers between devices with their start and end apart: 18, of which 12 were waited for; matrix products, arithmetic and copies ran while one was open for 0% of the time, Pallas kernels for 11%

commit v1 on v0

--- a/solution.py
+++ b/solution.py
@@ -6,6 +6,7 @@
 from jax.experimental import pallas as pl
 from jax.experimental.pallas import tpu as pltpu
 from jax.sharding import PartitionSpec as P
+
 
 QUERIES = 128
 TILE = 64
@@ -16,12 +17,13 @@
 MIN_SHARE = 8
 
 
-def place_tiles(step, in_pairs, flips, chain, counts, coords, tiles, buf, coord_buf, sems, coord_sem, accs):
+def place_tiles(step, in_pairs, chain, counts, coords, tiles, buf, coord_buf, sems, coord_sem, accs):
     pairs = tiles.shape[1]
     chunk = pairs // MIN_SHARE
     relation = chain[step]
     live_chunks = counts[0, 0, relation] // (2 * chunk)
-    row_flip, col_flip = flips[0], flips[1]
+    row_flip = lax.axis_index("col") * BLOCKS_DEV
+    col_flip = lax.axis_index("row") * BLOCKS_DEV
     copy_coords = pltpu.make_async_copy(coords.at[relation], coord_buf, coord_sem)
     copy_coords.start()
 
@@ -86,21 +88,25 @@
             lows[away, pl.ds(at, TILE), jp * LANES:(jp + 1) * LANES] = low
 
 
-def first_kernel(out_blocks, in_pairs, chain, counts, flips, targets, coords, tiles, keep, send,
+def first_kernel(out_blocks, in_pairs, chain, counts, seeds, coords, tiles, keep, send,
                  buf, coord_buf, sems, coord_sem, highs, lows, *accs):
-    place_tiles(0, in_pairs, flips, chain, counts, coords, tiles, buf, coord_buf, sems, coord_sem, accs)
+    place_tiles(0, in_pairs, chain, counts, coords, tiles, buf, coord_buf, sems, coord_sem, accs)
     fold(accs, out_blocks, in_pairs, highs, lows)
     depth = in_pairs * LANES
+    cols = out_blocks // BLOCKS_DEV
+    block = seeds[...] // ROWS_DEV
+    target = ((block // cols) ^ lax.axis_index("row")) * ROWS_DEV + seeds[...] % ROWS_DEV
+    target = jnp.where(block % cols == lax.axis_index("col"), target, -1)
     entity = lax.broadcasted_iota(jnp.int32, (depth, QUERIES), 0)
-    states = (entity == targets[...]).astype(jnp.float32).astype(jnp.bfloat16)
+    states = (entity == target).astype(jnp.float32).astype(jnp.bfloat16)
     for away, out in ((1, send), (0, keep)):
         out[...] = jnp.dot(highs[away], states, preferred_element_type=jnp.float32) + jnp.dot(
             lows[away], states, preferred_element_type=jnp.float32)
 
 
-def dense_kernel(step, out_blocks, in_pairs, chain, counts, flips, coords, tiles, highs, lows,
+def dense_kernel(step, out_blocks, in_pairs, chain, counts, coords, tiles, highs, lows,
                  buf, coord_buf, sems, coord_sem, *accs):
-    place_tiles(step, in_pairs, flips, chain, counts, coords, tiles, buf, coord_buf, sems, coord_sem, accs)
+    place_tiles(step, in_pairs, chain, counts, coords, tiles, buf, coord_buf, sems, coord_sem, accs)
     fold(accs, out_blocks, in_pairs, highs, lows)
 
 
@@ -119,8 +125,6 @@
 def shards(tiles, tile_coords, tile_count, seeds, chain):
     row_total = lax.axis_size("row")
     col_total = lax.axis_size("col")
-    my_row = lax.axis_index("row")
-    my_col = lax.axis_index("col")
     out_blocks = col_total * BLOCKS_DEV
     in_pairs = row_total
     depth_total = col_total // 2
@@ -131,16 +135,16 @@
 
     tiles = tiles.reshape(relations, pairs, TILE, 2 * TILE)
     coords = tile_coords.reshape(relations, 2, 2 * pairs)
-    flips = jnp.stack([my_col * BLOCKS_DEV, my_row * BLOCKS_DEV]).astype(jnp.int32)
-    block = seeds // ROWS_DEV
-    targets = jnp.where(block % col_total == my_col,
-                        ((block // col_total) ^ my_row) * ROWS_DEV + seeds % ROWS_DEV, -1)[None, :]
+    seeds = seeds[None, :]
 
     small = out_blocks * in_pairs * TILE * LANES * 4 <= 4 << 20
     smem = pl.BlockSpec(memory_space=pltpu.SMEM)
     vmem = pl.BlockSpec(memory_space=pltpu.VMEM)
-    hbm = pl.BlockSpec(memory_space=pl.ANY)
-    params = pltpu.CompilerParams(vmem_limit_bytes=60 << 20)
+    hbm = pl.BlockSpec(memory_space=pltpu.HBM)
+    dense_bytes = out_blocks * in_pairs * TILE * LANES * 4
+    params = pltpu.CompilerParams(
+        vmem_limit_bytes=(3 if small else 2) * dense_bytes + pairs * TILE * LANES * 4 + (6 << 20))
+    product_params = pltpu.CompilerParams(vmem_limit_bytes=dense_bytes + (8 << 20))
     work = [
         pltpu.VMEM((pairs, TILE, 2 * TILE), f32),
         pltpu.SMEM((2, 2 * pairs), jnp.int32),
@@ -148,31 +152,38 @@
         pltpu.SemaphoreType.DMA(()),
     ]
     accs = [pltpu.VMEM((out_blocks * in_pairs, TILE, LANES), f32)] * (2 if small else 1)
-    dense = jax.ShapeDtypeStruct((2, rows_out, rows_in), bf16)
-    partial = jax.ShapeDtypeStruct((rows_out, QUERIES), f32)
+    dense = pltpu.VMEM((2, rows_out, rows_in), bf16)
+    partial = pltpu.VMEM((rows_out, QUERIES), f32)
+
+    def local(x):
+        return pltpu.with_memory_space_constraint(x, pltpu.VMEM)
+
+    def remain(x):
+        return pltpu.with_memory_space_constraint(x, pltpu.HBM)
+
+    given = [remain(x) for x in (chain, tile_count, seeds, coords, tiles)]
 
     def first():
         return pl.pallas_call(
             functools.partial(first_kernel, out_blocks, in_pairs),
             out_shape=[partial, partial],
-            in_specs=[smem, smem, smem, vmem, hbm, hbm],
+            in_specs=[smem, smem, vmem, hbm, hbm],
             out_specs=[vmem, vmem],
             scratch_shapes=work + [pltpu.VMEM(dense.shape, bf16)] * 2 + accs,
             compiler_params=params,
             name="first",
-        )(chain, tile_count, flips, targets, coords, tiles)
+        )(*given)
 
     def densify(step):
         return pl.pallas_call(
             functools.partial(dense_kernel, step, out_blocks, in_pairs),
             out_shape=[dense, dense],
-            in_specs=[smem, smem, smem, hbm, hbm],
+            in_specs=[smem, smem, hbm, hbm],
             out_specs=[vmem, vmem],
             scratch_shapes=work + accs,
             compiler_params=params,
             cost_estimate=pl.CostEstimate(flops=0, bytes_accessed=8 << 20, transcendentals=0),
-            name=f"densify{step}",
-        )(chain, tile_count, flips, coords, tiles)
+        )(*given[:2], *given[3:])
 
     def product(highs, lows, pieces):
         return pl.pallas_call(
@@ -181,9 +192,9 @@
             in_specs=[vmem] * (2 + len(pieces)),
             out_specs=[vmem, vmem],
             scratch_shapes=[pltpu.VMEM((rows_in, 2 * QUERIES), bf16)],
-            compiler_params=params,
+            compiler_params=product_params,
             name="product",
-        )(highs, lows, *pieces)
+        )(local(highs), local(lows), *map(local, pieces))
 
     def swap(x, axis, size, flip):
         return lax.ppermute(x, axis, [(i, i ^ flip) for i in range(size)])
@@ -195,11 +206,12 @@
             swap(summed[k * ROWS_DEV:(k + 1) * ROWS_DEV], "col", col_total, 2 * k)
             for k in range(1, depth_total)
         ]
+        if step + 1 < HOPS:
+            highs, lows = densify(step + 1)
         owned = summed[:ROWS_DEV]
         for part in arrived:
             owned = owned + part
         if step + 1 < HOPS:
-            highs, lows = densify(step + 1)
             pieces = [owned] + [swap(owned, "row", row_total, k) for k in range(1, row_total)]
             keep, send = product(highs, lows, pieces)
 

time: 88.8 us -> 72.7 us (0.82)
  Pallas kernels: 21.2 us -> 13.2 us
  other arithmetic: 5.53 us -> 0.86 us
  blocking collectives: 13.7 us -> 11 us
  local copies, waits for them, and re-layouts: 1.33 us -> 0.06 us
    pallas_call x2, Pallas kernels: 6.02 us -> 1.48 us  [product(): pl.pallas_call(functools.partial(product_kernel, len(pieces)), out_shape=...]
    add x3, other arithmetic: 2.97 us -> 0.12 us  [shards(): summed = keep + swap(send, 'col', col_total, 1)]
    all_to_all x1, blocking collectives: 13.7 us -> 11 us  [shards(): lax.all_to_all(jnp.broadcast_to(squares, (devices, QUERIES)), ('row', 'co...]
    pallas_call x2, Pallas kernels: 9.6 us -> 6.89 us  [densify(): pl.pallas_call(functools.partial(dense_kernel, step, out_blocks, in_pairs...]
    unnamed x16 -> x0, local copies, waits for them, and re-layouts: 1.28 us -> none
    broadcast_in_dim x1 -> x0, other arithmetic: 1.19 us -> none  [shards(): jnp.where(block % col_total == my_col, (block // col_total ^ my_row) * RO...]
  transfers between devices with their start and end apart: 18 -> 18, of which waited for: 12 -> 14; matrix products, arithmetic and copies ran while one was open for 0% -> 0% of each run, Pallas kernels for 11% -> 10%
where the time goes in v1:
time: 72.7 us; the launch traced here: 72.5 us
  waiting for transfers between devices  24.4 us (34%)
  starting transfers between devices  22.8 us (31%)
  Pallas kernels  13.2 us (18%)
  blocking collectives  11 us (15%)
  other arithmetic  0.86 us (1%)
    ppermute x18, waiting for transfers between devices, swap(): return lax.ppermute(x, axis, [(i, i ^ flip) for i in range(size)])  24.4 us
    ppermute x18, starting transfers between devices, swap(): return lax.ppermute(x, axis, [(i, i ^ flip) for i in range(size)])  22.8 us
    all_to_all x1, blocking collectives, shards(): lax.all_to_all(jnp.broadcast_to(squares, (devices, QUERIES)), ('row', 'co...  11 us
    pallas_call x2, Pallas kernels, densify(): pl.pallas_call(functools.partial(dense_kernel, step, out_blocks, in_pairs...  6.89 us
    pallas_call x1, Pallas kernels, first(): pl.pallas_call(functools.partial(first_kernel, out_blocks, in_pairs), out...  4.8 us
    pallas_call x2, Pallas kernels, product(): pl.pallas_call(functools.partial(product_kernel, len(pieces)), out_shape=...  1.48 us
  transfers between devices with their start and end apart: 18, of which 14 were waited for; matrix products, arithmetic and copies ran while one was open for 0% of the time, Pallas kernels for 10%

profile of v1, /device:TPU:0, one launch (start us, length us, event | category | flops | bytes accessed | tf_op | source)
XLA Modules:
  0.0 72.5 jit_solution(2155318662102726539)
XLA Ops:
  0.0 4.8 %first.1 = (f32[512,128]{1,0:T(8,128)S(1)}, f32[512,128]{1,0:T(8,128)S(1)}) custom-call(s32[3]{0:T(128)} %chain.5, s32[1,1,3]{2,1,0:T(1,128)} %counts.5, s32[1,128]{1,0:T(1,128)} %bitcast.11, s32[3,2,256]{2,1,0:T(2,128)} %bitcast.8, f32[3,128,64,128]{3,2,1,0:T(8,128)} %bitcast.4), custom_call_target="tpu_custom_call" | custom-call | tf_op jit(solution)/shard_map/first/pallas_call | solution.py:167
  4.9 1.5 %collective-permute-done = f32[512,128]{1,0:T(8,128)S(1)} collective-permute-done((f32[512,128]{1,0:T(8,128)S(1)}, f32[512,128]{1,0:T(8,128)S(1)}, u32[]{:S(2)}, u32[]{:S(2)}) %collective-permute-start) | collective-permute-done | bytes 262176 | tf_op jit(solution)/shard_map/ppermute | solution.py:200
  6.5 3.1 %collective-permute-start.1 = (f32[128,128]{1,0:T(8,128)S(1)}, f32[128,128]{1,0:T(8,128)S(1)}, u32[]{:S(2)}, u32[]{:S(2)}) collective-permute-start(f32[128,128]{1,0:T(8,128)S(1)} %get-tuple-element.33), channel_id=1, source_target_pairs={{0,2},{1,3},{2,0},{3,1},{4,6},{5,7},{6,4},{7,5},{8,10},{9,11},{10,... | collective-permute-start | bytes 196616 | tf_op jit(solution)/shard_map/ppermute | solution.py:200
  9.6 3.6 %collective-permute-start.3 = (f32[128,128]{1,0:T(8,128)S(1)}, f32[128,128]{1,0:T(8,128)S(1)}, u32[]{:S(2)}, u32[]{:S(2)}) collective-permute-start(f32[128,128]{1,0:T(8,128)S(1)} %get-tuple-element.34), channel_id=1, source_target_pairs={{0,6},{1,7},{2,4},{3,5},{4,2},{5,3},{6,0},{7,1},{8,14},{9,15},{10,... | collective-permute-start | bytes 196616 | tf_op jit(solution)/shard_map/ppermute | solution.py:200
  13.2 4.4 %collective-permute-done.3 = f32[128,128]{1,0:T(8,128)S(1)} collective-permute-done((f32[128,128]{1,0:T(8,128)S(1)}, f32[128,128]{1,0:T(8,128)S(1)}, u32[]{:S(2)}, u32[]{:S(2)}) %collective-permute-start.3) | collective-permute-done | bytes 65568 | tf_op jit(solution)/shard_map/ppermute | solution.py:200
  17.7 2.1 %collective-permute-done.2 = f32[128,128]{1,0:T(8,128)S(1)} collective-permute-done((f32[128,128]{1,0:T(8,128)S(1)}, f32[128,128]{1,0:T(8,128)S(1)}, u32[]{:S(2)}, u32[]{:S(2)}) %collective-permute-start.2) | collective-permute-done | bytes 65568 | tf_op jit(solution)/shard_map/ppermute | solution.py:200
  19.8 2.4 %collective-permute-start.6 = (f32[128,128]{1,0:T(8,128)S(1)}, f32[128,128]{1,0:T(8,128)S(1)}, u32[]{:S(2)}, u32[]{:S(2)}) collective-permute-start(f32[128,128]{1,0:T(8,128)S(1)} %fusion.5.refs_0_), channel_id=1, source_target_pairs={{0,24},{8,16},{16,8},{24,0},{1,25},{9,17},{17,9},{25,1},{2,26},{10... | collective-permute-start | bytes 196616 | tf_op jit(solution)/shard_map/ppermute | solution.py:200
  22.2 0.9 %collective-permute-start.5 = (f32[128,128]{1,0:T(8,128)S(1)}, f32[128,128]{1,0:T(8,128)S(1)}, u32[]{:S(2)}, u32[]{:S(2)}) collective-permute-start(f32[128,128]{1,0:T(8,128)S(1)} %fusion.5.refs_0_), channel_id=1, source_target_pairs={{0,16},{8,24},{16,0},{24,8},{1,17},{9,25},{17,1},{25,9},{2,18},{10... | collective-permute-start | bytes 196616 | tf_op jit(solution)/shard_map/ppermute | solution.py:200
  23.3 2.8 %shard_map.56 = (bf16[2,512,512]{2,1,0:T(8,128)(2,1)S(1)}, bf16[2,512,512]{2,1,0:T(8,128)(2,1)S(1)}) custom-call(s32[3]{0:T(128)} %chain.5, s32[1,1,3]{2,1,0:T(1,128)} %counts.5, s32[3,2,256]{2,1,0:T(2,128)} %bitcast.9, f32[3,128,64,128]{3,2,1,0:T(8,128)} %bitcast.5), custom_call_target="tpu_custom_call" | custom-call | bytes 8388608 | tf_op jit(solution)/shard_map/pallas_call | solution.py:178
  28.1 1.1 %collective-permute-start.7 = (f32[512,128]{1,0:T(8,128)S(1)}, f32[512,128]{1,0:T(8,128)S(1)}, u32[]{:S(2)}, u32[]{:S(2)}) collective-permute-start(f32[512,128]{1,0:T(8,128)S(1)} %get-tuple-element.22), channel_id=1, source_target_pairs={{0,1},{1,0},{2,3},{3,2},{4,5},{5,4},{6,7},{7,6},{8,9},{9,8},{10,11... | collective-permute-start | bytes 786440 | tf_op jit(solution)/shard_map/ppermute | solution.py:200
  29.2 1.2 %collective-permute-done.7 = f32[512,128]{1,0:T(8,128)S(1)} collective-permute-done((f32[512,128]{1,0:T(8,128)S(1)}, f32[512,128]{1,0:T(8,128)S(1)}, u32[]{:S(2)}, u32[]{:S(2)}) %collective-permute-start.7) | collective-permute-done | bytes 262176 | tf_op jit(solution)/shard_map/ppermute | solution.py:200
  30.5 2.5 %collective-permute-start.10 = (f32[128,128]{1,0:T(8,128)S(1)}, f32[128,128]{1,0:T(8,128)S(1)}, u32[]{:S(2)}, u32[]{:S(2)}) collective-permute-start(f32[128,128]{1,0:T(8,128)S(1)} %get-tuple-element.31), channel_id=1, source_target_pairs={{0,6},{1,7},{2,4},{3,5},{4,2},{5,3},{6,0},{7,1},{8,14},{9,15},{10,... | collective-permute-start | bytes 196616 | tf_op jit(solution)/shard_map/ppermute | solution.py:200
  33.0 0.9 %collective-permute-start.9 = (f32[128,128]{1,0:T(8,128)S(1)}, f32[128,128]{1,0:T(8,128)S(1)}, u32[]{:S(2)}, u32[]{:S(2)}) collective-permute-start(f32[128,128]{1,0:T(8,128)S(1)} %get-tuple-element.32), channel_id=1, source_target_pairs={{0,4},{1,5},{2,6},{3,7},{4,0},{5,1},{6,2},{7,3},{8,12},{9,13},{10,... | collective-permute-start | bytes 196616 | tf_op jit(solution)/shard_map/ppermute | solution.py:200
  34.8 2.6 %collective-permute-done.10 = f32[128,128]{1,0:T(8,128)S(1)} collective-permute-done((f32[128,128]{1,0:T(8,128)S(1)}, f32[128,128]{1,0:T(8,128)S(1)}, u32[]{:S(2)}, u32[]{:S(2)}) %collective-permute-start.10) | collective-permute-done | bytes 65568 | tf_op jit(solution)/shard_map/ppermute | solution.py:200
  37.4 2.8 %collective-permute-done.9 = f32[128,128]{1,0:T(8,128)S(1)} collective-permute-done((f32[128,128]{1,0:T(8,128)S(1)}, f32[128,128]{1,0:T(8,128)S(1)}, u32[]{:S(2)}, u32[]{:S(2)}) %collective-permute-start.9) | collective-permute-done | bytes 65568 | tf_op jit(solution)/shard_map/ppermute | solution.py:200
  40.2 2.1 %collective-permute-start.13 = (f32[128,128]{1,0:T(8,128)S(1)}, f32[128,128]{1,0:T(8,128)S(1)}, u32[]{:S(2)}, u32[]{:S(2)}) collective-permute-start(f32[128,128]{1,0:T(8,128)S(1)} %fusion.3.refs_0_), channel_id=1, source_target_pairs={{0,24},{8,16},{16,8},{24,0},{1,25},{9,17},{17,9},{25,1},{2,26},{10... | collective-permute-start | bytes 196616 | tf_op jit(solution)/shard_map/ppermute | solution.py:200
  42.4 2.1 %collective-permute-start.12 = (f32[128,128]{1,0:T(8,128)S(1)}, f32[128,128]{1,0:T(8,128)S(1)}, u32[]{:S(2)}, u32[]{:S(2)}) collective-permute-start(f32[128,128]{1,0:T(8,128)S(1)} %fusion.3.refs_0_), channel_id=1, source_target_pairs={{0,16},{8,24},{16,0},{24,8},{1,17},{9,25},{17,1},{25,9},{2,18},{10... | collective-permute-start | bytes 196616 | tf_op jit(solution)/shard_map/ppermute | solution.py:200
  44.5 4.1 %shard_map.55 = (bf16[2,512,512]{2,1,0:T(8,128)(2,1)S(1)}, bf16[2,512,512]{2,1,0:T(8,128)(2,1)S(1)}) custom-call(s32[3]{0:T(128)} %chain.5, s32[1,1,3]{2,1,0:T(1,128)} %counts.5, s32[3,2,256]{2,1,0:T(2,128)} %bitcast.10, f32[3,128,64,128]{3,2,1,0:T(8,128)} %bitcast.6), custom_call_target="tpu_custom_call" | custom-call | bytes 8388608 | tf_op jit(solution)/shard_map/pallas_call | solution.py:178
  49.6 1.5 %collective-permute-done.14 = f32[512,128]{1,0:T(8,128)S(1)} collective-permute-done((f32[512,128]{1,0:T(8,128)S(1)}, f32[512,128]{1,0:T(8,128)S(1)}, u32[]{:S(2)}, u32[]{:S(2)}) %collective-permute-start.14) | collective-permute-done | bytes 262176 | tf_op jit(solution)/shard_map/ppermute | solution.py:200
  51.2 1.2 %collective-permute-start.17 = (f32[128,128]{1,0:T(8,128)S(1)}, f32[128,128]{1,0:T(8,128)S(1)}, u32[]{:S(2)}, u32[]{:S(2)}) collective-permute-start(f32[128,128]{1,0:T(8,128)S(1)} %get-tuple-element.28), channel_id=1, source_target_pairs={{0,6},{1,7},{2,4},{3,5},{4,2},{5,3},{6,0},{7,1},{8,14},{9,15},{10,... | collective-permute-start | bytes 196616 | tf_op jit(solution)/shard_map/ppermute | solution.py:200
  52.5 2.2 %collective-permute-start.16 = (f32[128,128]{1,0:T(8,128)S(1)}, f32[128,128]{1,0:T(8,128)S(1)}, u32[]{:S(2)}, u32[]{:S(2)}) collective-permute-start(f32[128,128]{1,0:T(8,128)S(1)} %get-tuple-element.29), channel_id=1, source_target_pairs={{0,4},{1,5},{2,6},{3,7},{4,0},{5,1},{6,2},{7,3},{8,12},{9,13},{10,... | collective-permute-start | bytes 196616 | tf_op jit(solution)/shard_map/ppermute | solution.py:200
  55.5 2.5 %collective-permute-done.17 = f32[128,128]{1,0:T(8,128)S(1)} collective-permute-done((f32[128,128]{1,0:T(8,128)S(1)}, f32[128,128]{1,0:T(8,128)S(1)}, u32[]{:S(2)}, u32[]{:S(2)}) %collective-permute-start.17) | collective-permute-done | bytes 65568 | tf_op jit(solution)/shard_map/ppermute | solution.py:200
  58.0 2.7 %collective-permute-done.16 = f32[128,128]{1,0:T(8,128)S(1)} collective-permute-done((f32[128,128]{1,0:T(8,128)S(1)}, f32[128,128]{1,0:T(8,128)S(1)}, u32[]{:S(2)}, u32[]{:S(2)}) %collective-permute-start.16) | collective-permute-done | bytes 65568 | tf_op jit(solution)/shard_map/ppermute | solution.py:200
  60.8 11.0 %all_to_all.6 = f32[32,1,128]{2,1,0:T(1,128)S(1)} all-to-all(f32[32,1,128]{2,1,0:T(1,128)S(1)} %broadcast_in_dim.5), channel_id=1, replica_groups=mesh['row'=4,'col'=8] {'row','col'}, dimensions={0} | all-to-all | bytes 32768 | tf_op jit(solution)/shard_map/all_to_all | solution.py:220
  (31 shorter events, 5.9 us)
Async XLA Ops:
  4.8 1.6 %collective-permute-start = (f32[512,128]{1,0:T(8,128)S(1)}, f32[512,128]{1,0:T(8,128)S(1)}, u32[]{:S(2)}, u32[]{:S(2)}) collective-permute-start(f32[512,128]{1,0:T(8,128)S(1)} %get-tuple-element.20), channel_id=1, source_target_pairs={{0,1},{1,0},{2,3},{3,2},{4,5},{5,4},{6,7},{7,6},{8,9},{9,8},{10,11... | collective-permute-start | bytes 786440 | tf_op jit(solution)/shard_map/ppermute | solution.py:200
  6.5 6.7 %collective-permute-start.1 = (f32[128,128]{1,0:T(8,128)S(1)}, f32[128,128]{1,0:T(8,128)S(1)}, u32[]{:S(2)}, u32[]{:S(2)}) collective-permute-start(f32[128,128]{1,0:T(8,128)S(1)} %get-tuple-element.33), channel_id=1, source_target_pairs={{0,2},{1,3},{2,0},{3,1},{4,6},{5,7},{6,4},{7,5},{8,10},{9,11},{10,... | collective-permute-start | bytes 196616 | tf_op jit(solution)/shard_map/ppermute | solution.py:200
  9.6 8.1 %collective-permute-start.3 = (f32[128,128]{1,0:T(8,128)S(1)}, f32[128,128]{1,0:T(8,128)S(1)}, u32[]{:S(2)}, u32[]{:S(2)}) collective-permute-start(f32[128,128]{1,0:T(8,128)S(1)} %get-tuple-element.34), channel_id=1, source_target_pairs={{0,6},{1,7},{2,4},{3,5},{4,2},{5,3},{6,0},{7,1},{8,14},{9,15},{10,... | collective-permute-start | bytes 196616 | tf_op jit(solution)/shard_map/ppermute | solution.py:200
  13.2 6.6 %collective-permute-start.2 = (f32[128,128]{1,0:T(8,128)S(1)}, f32[128,128]{1,0:T(8,128)S(1)}, u32[]{:S(2)}, u32[]{:S(2)}) collective-permute-start(f32[128,128]{1,0:T(8,128)S(1)} %get-tuple-element.35), channel_id=1, source_target_pairs={{0,4},{1,5},{2,6},{3,7},{4,0},{5,1},{6,2},{7,3},{8,12},{9,13},{10,... | collective-permute-start | bytes 196616 | tf_op jit(solution)/shard_map/ppermute | solution.py:200
  19.8 6.4 %collective-permute-start.6 = (f32[128,128]{1,0:T(8,128)S(1)}, f32[128,128]{1,0:T(8,128)S(1)}, u32[]{:S(2)}, u32[]{:S(2)}) collective-permute-start(f32[128,128]{1,0:T(8,128)S(1)} %fusion.5.refs_0_), channel_id=1, source_target_pairs={{0,24},{8,16},{16,8},{24,0},{1,25},{9,17},{17,9},{25,1},{2,26},{10... | collective-permute-start | bytes 196616 | tf_op jit(solution)/shard_map/ppermute | solution.py:200
  22.2 4.3 %collective-permute-start.5 = (f32[128,128]{1,0:T(8,128)S(1)}, f32[128,128]{1,0:T(8,128)S(1)}, u32[]{:S(2)}, u32[]{:S(2)}) collective-permute-start(f32[128,128]{1,0:T(8,128)S(1)} %fusion.5.refs_0_), channel_id=1, source_target_pairs={{0,16},{8,24},{16,0},{24,8},{1,17},{9,25},{17,1},{25,9},{2,18},{10... | collective-permute-start | bytes 196616 | tf_op jit(solution)/shard_map/ppermute | solution.py:200
  23.1 4.3 %collective-permute-start.4 = (f32[128,128]{1,0:T(8,128)S(1)}, f32[128,128]{1,0:T(8,128)S(1)}, u32[]{:S(2)}, u32[]{:S(2)}) collective-permute-start(f32[128,128]{1,0:T(8,128)S(1)} %fusion.5.refs_0_), channel_id=1, source_target_pairs={{0,8},{8,0},{16,24},{24,16},{1,9},{9,1},{17,25},{25,17},{2,10},{10... | collective-permute-start | bytes 196616 | tf_op jit(solution)/shard_map/ppermute | solution.py:200
  28.1 2.2 %collective-permute-start.7 = (f32[512,128]{1,0:T(8,128)S(1)}, f32[512,128]{1,0:T(8,128)S(1)}, u32[]{:S(2)}, u32[]{:S(2)}) collective-permute-start(f32[512,128]{1,0:T(8,128)S(1)} %get-tuple-element.22), channel_id=1, source_target_pairs={{0,1},{1,0},{2,3},{3,2},{4,5},{5,4},{6,7},{7,6},{8,9},{9,8},{10,11... | collective-permute-start | bytes 786440 | tf_op jit(solution)/shard_map/ppermute | solution.py:200
  30.4 4.4 %collective-permute-start.8 = (f32[128,128]{1,0:T(8,128)S(1)}, f32[128,128]{1,0:T(8,128)S(1)}, u32[]{:S(2)}, u32[]{:S(2)}) collective-permute-start(f32[128,128]{1,0:T(8,128)S(1)} %get-tuple-element.30), channel_id=1, source_target_pairs={{0,2},{1,3},{2,0},{3,1},{4,6},{5,7},{6,4},{7,5},{8,10},{9,11},{10,... | collective-permute-start | bytes 196616 | tf_op jit(solution)/shard_map/ppermute | solution.py:200
  30.5 6.9 %collective-permute-start.10 = (f32[128,128]{1,0:T(8,128)S(1)}, f32[128,128]{1,0:T(8,128)S(1)}, u32[]{:S(2)}, u32[]{:S(2)}) collective-permute-start(f32[128,128]{1,0:T(8,128)S(1)} %get-tuple-element.31), channel_id=1, source_target_pairs={{0,6},{1,7},{2,4},{3,5},{4,2},{5,3},{6,0},{7,1},{8,14},{9,15},{10,... | collective-permute-start | bytes 196616 | tf_op jit(solution)/shard_map/ppermute | solution.py:200
  33.0 7.2 %collective-permute-start.9 = (f32[128,128]{1,0:T(8,128)S(1)}, f32[128,128]{1,0:T(8,128)S(1)}, u32[]{:S(2)}, u32[]{:S(2)}) collective-permute-start(f32[128,128]{1,0:T(8,128)S(1)} %get-tuple-element.32), channel_id=1, source_target_pairs={{0,4},{1,5},{2,6},{3,7},{4,0},{5,1},{6,2},{7,3},{8,12},{9,13},{10,... | collective-permute-start | bytes 196616 | tf_op jit(solution)/shard_map/ppermute | solution.py:200
  40.2 8.3 %collective-permute-start.13 = (f32[128,128]{1,0:T(8,128)S(1)}, f32[128,128]{1,0:T(8,128)S(1)}, u32[]{:S(2)}, u32[]{:S(2)}) collective-permute-start(f32[128,128]{1,0:T(8,128)S(1)} %fusion.3.refs_0_), channel_id=1, source_target_pairs={{0,24},{8,16},{16,8},{24,0},{1,25},{9,17},{17,9},{25,1},{2,26},{10... | collective-permute-start | bytes 196616 | tf_op jit(solution)/shard_map/ppermute | solution.py:200
  42.4 6.2 %collective-permute-start.12 = (f32[128,128]{1,0:T(8,128)S(1)}, f32[128,128]{1,0:T(8,128)S(1)}, u32[]{:S(2)}, u32[]{:S(2)}) collective-permute-start(f32[128,128]{1,0:T(8,128)S(1)} %fusion.3.refs_0_), channel_id=1, source_target_pairs={{0,16},{8,24},{16,0},{24,8},{1,17},{9,25},{17,1},{25,9},{2,18},{10... | collective-permute-start | bytes 196616 | tf_op jit(solution)/shard_map/ppermute | solution.py:200
  44.5 4.3 %collective-permute-start.11 = (f32[128,128]{1,0:T(8,128)S(1)}, f32[128,128]{1,0:T(8,128)S(1)}, u32[]{:S(2)}, u32[]{:S(2)}) collective-permute-start(f32[128,128]{1,0:T(8,128)S(1)} %fusion.3.refs_0_), channel_id=1, source_target_pairs={{0,8},{8,0},{16,24},{24,16},{1,9},{9,1},{17,25},{25,17},{2,10},{10... | collective-permute-start | bytes 196616 | tf_op jit(solution)/shard_map/ppermute | solution.py:200
  49.5 1.6 %collective-permute-start.14 = (f32[512,128]{1,0:T(8,128)S(1)}, f32[512,128]{1,0:T(8,128)S(1)}, u32[]{:S(2)}, u32[]{:S(2)}) collective-permute-start(f32[512,128]{1,0:T(8,128)S(1)} %get-tuple-element.24), channel_id=1, source_target_pairs={{0,1},{1,0},{2,3},{3,2},{4,5},{5,4},{6,7},{7,6},{8,9},{9,8},{10,11... | collective-permute-start | bytes 786440 | tf_op jit(solution)/shard_map/ppermute | solution.py:200
  51.2 4.3 %collective-permute-start.15 = (f32[128,128]{1,0:T(8,128)S(1)}, f32[128,128]{1,0:T(8,128)S(1)}, u32[]{:S(2)}, u32[]{:S(2)}) collective-permute-start(f32[128,128]{1,0:T(8,128)S(1)} %get-tuple-element.27), channel_id=1, source_target_pairs={{0,2},{1,3},{2,0},{3,1},{4,6},{5,7},{6,4},{7,5},{8,10},{9,11},{10,... | collective-permute-start | bytes 196616 | tf_op jit(solution)/shard_map/ppermute | solution.py:200
  51.2 6.8 %collective-permute-start.17 = (f32[128,128]{1,0:T(8,128)S(1)}, f32[128,128]{1,0:T(8,128)S(1)}, u32[]{:S(2)}, u32[]{:S(2)}) collective-permute-start(f32[128,128]{1,0:T(8,128)S(1)} %get-tuple-element.28), channel_id=1, source_target_pairs={{0,6},{1,7},{2,4},{3,5},{4,2},{5,3},{6,0},{7,1},{8,14},{9,15},{10,... | collective-permute-start | bytes 196616 | tf_op jit(solution)/shard_map/ppermute | solution.py:200
  52.5 8.3 %collective-permute-start.16 = (f32[128,128]{1,0:T(8,128)S(1)}, f32[128,128]{1,0:T(8,128)S(1)}, u32[]{:S(2)}, u32[]{:S(2)}) collective-permute-start(f32[128,128]{1,0:T(8,128)S(1)} %get-tuple-element.29), channel_id=1, source_target_pairs={{0,4},{1,5},{2,6},{3,7},{4,0},{5,1},{6,2},{7,3},{8,12},{9,13},{10,... | collective-permute-start | bytes 196616 | tf_op jit(solution)/shard_map/ppermute | solution.py:200

commit v2 on v1

--- a/solution.py
+++ b/solution.py
@@ -17,14 +17,13 @@
 MIN_SHARE = 8
 
 
-def place_tiles(step, in_pairs, chain, counts, coords, tiles, buf, coord_buf, sems, coord_sem, accs):
+def place_tiles(step, in_pairs, chain, counts, coords, tiles, buf, coord_buf, spots, sems, acc):
     pairs = tiles.shape[1]
     chunk = pairs // MIN_SHARE
+    blocks = acc.shape[0] // 2
     relation = chain[step]
     live_chunks = counts[0, 0, relation] // (2 * chunk)
-    row_flip = lax.axis_index("col") * BLOCKS_DEV
-    col_flip = lax.axis_index("row") * BLOCKS_DEV
-    copy_coords = pltpu.make_async_copy(coords.at[relation], coord_buf, coord_sem)
+    copy_coords = pltpu.make_async_copy(coords.at[relation], coord_buf, sems.at[MIN_SHARE])
     copy_coords.start()
 
     def chunk_copy(index):
@@ -36,28 +35,29 @@
         def _(index=index):
             chunk_copy(index).start()
 
-    acc_even, acc_odd = accs[0], accs[-1]
-    blocks = acc_even.shape[0]
-
-    @pl.loop(0, blocks // 4)
+    copy_coords.wait()
+    slot = lax.broadcasted_iota(jnp.int32, (1, 2 * pairs), 1)
+    i = coord_buf[0:1, :] ^ (lax.axis_index("col") * BLOCKS_DEV)
+    j = coord_buf[1:2, :] ^ (lax.axis_index("row") * BLOCKS_DEV)
+    coord_buf[0:1, :] = ((j ^ slot) & 1) * blocks + i * in_pairs + (j >> 1)
+    copy_spots = pltpu.make_async_copy(coord_buf.at[pl.ds(0, 1)], spots, sems.at[MIN_SHARE])
+    copy_spots.start()
+
+    @pl.loop(0, 2 * blocks // 8)
     def _(b):
-        for u in range(4):
-            for acc in accs:
-                acc[b * 4 + u] = jnp.zeros((TILE, LANES), jnp.float32)
-
-    half_of_lane = lax.broadcasted_iota(jnp.int32, (TILE, LANES), 1) // TILE
-    copy_coords.wait()
+        for u in range(8):
+            acc[b * 8 + u] = jnp.zeros((TILE, LANES), jnp.float32)
+
+    left = lax.broadcasted_iota(jnp.int32, (TILE, LANES), 1) < TILE
+    copy_spots.wait()
 
     def add_pair(t):
+        even, odd = spots[0, 2 * t], spots[0, 2 * t + 1]
         values = buf[t]
-        rolled = pltpu.roll(values, TILE, 1)
-        for odd, acc in ((0, acc_even), (1, acc_odd)):
-            i = coord_buf[0, 2 * t + odd] ^ row_flip
-            j = coord_buf[1, 2 * t + odd] ^ col_flip
-            half = j & 1
-            at = i * in_pairs + (j >> 1)
-            moved = jnp.where(half == odd, values, rolled)
-            acc[at] = acc[at] + jnp.where(half_of_lane == half, moved, 0.0)
+        new_even = acc[even] + values
+        new_odd = acc[odd] + values
+        pltpu.store(acc.at[even], new_even, mask=left)
+        pltpu.store(acc.at[odd], new_odd, mask=jnp.logical_not(left))
 
     @pl.loop(0, live_chunks)
     def _(index):
@@ -74,40 +74,41 @@
     return high, (x - high.astype(jnp.float32)).astype(jnp.bfloat16)
 
 
-def fold(accs, out_blocks, in_pairs, highs, lows):
-    @pl.loop(0, out_blocks)
-    def _(i):
-        away = (i // BLOCKS_DEV) & 1
-        at = pl.multiple_of((i // (2 * BLOCKS_DEV)) * ROWS_DEV + (i & 1) * TILE, TILE)
-        for jp in range(in_pairs):
-            value = accs[0][i * in_pairs + jp]
-            if len(accs) == 2:
-                value = value + accs[1][i * in_pairs + jp]
-            high, low = split(value)
-            highs[away, pl.ds(at, TILE), jp * LANES:(jp + 1) * LANES] = high
-            lows[away, pl.ds(at, TILE), jp * LANES:(jp + 1) * LANES] = low
+def fold(acc, in_pairs, highs, lows):
+    blocks = acc.shape[0] // 2
+    group = 2 * BLOCKS_DEV
+
+    @pl.loop(0, blocks // in_pairs // group)
+    def _(chip):
+        for inner in range(group):
+            away, k = inner // BLOCKS_DEV, inner % BLOCKS_DEV
+            at = pl.multiple_of(chip * ROWS_DEV + k * TILE, TILE)
+            for jp in range(in_pairs):
+                block = (chip * group + inner) * in_pairs + jp
+                high, low = split(acc[block] + pltpu.roll(acc[blocks + block], TILE, 1))
+                highs[away, pl.ds(at, TILE), jp * LANES:(jp + 1) * LANES] = high
+                lows[away, pl.ds(at, TILE), jp * LANES:(jp + 1) * LANES] = low
 
 
 def first_kernel(out_blocks, in_pairs, chain, counts, seeds, coords, tiles, keep, send,
-                 buf, coord_buf, sems, coord_sem, highs, lows, *accs):
-    place_tiles(0, in_pairs, chain, counts, coords, tiles, buf, coord_buf, sems, coord_sem, accs)
-    fold(accs, out_blocks, in_pairs, highs, lows)
-    depth = in_pairs * LANES
+                 buf, coord_buf, spots, sems, acc, highs, lows, states):
     cols = out_blocks // BLOCKS_DEV
     block = seeds[...] // ROWS_DEV
     target = ((block // cols) ^ lax.axis_index("row")) * ROWS_DEV + seeds[...] % ROWS_DEV
     target = jnp.where(block % cols == lax.axis_index("col"), target, -1)
-    entity = lax.broadcasted_iota(jnp.int32, (depth, QUERIES), 0)
-    states = (entity == target).astype(jnp.float32).astype(jnp.bfloat16)
+    entity = lax.broadcasted_iota(jnp.int32, states.shape, 0)
+    states[...] = (entity == target).astype(jnp.float32).astype(jnp.bfloat16)
+    place_tiles(0, in_pairs, chain, counts, coords, tiles, buf, coord_buf, spots, sems, acc)
+    fold(acc, in_pairs, highs, lows)
     for away, out in ((1, send), (0, keep)):
-        out[...] = jnp.dot(highs[away], states, preferred_element_type=jnp.float32) + jnp.dot(
-            lows[away], states, preferred_element_type=jnp.float32)
-
-
-def dense_kernel(step, out_blocks, in_pairs, chain, counts, coords, tiles, highs, lows,
-                 buf, coord_buf, sems, coord_sem, *accs):
-    place_tiles(step, in_pairs, chain, counts, coords, tiles, buf, coord_buf, sems, coord_sem, accs)
-    fold(accs, out_blocks, in_pairs, highs, lows)
+        out[...] = jnp.dot(highs[away], states[...], preferred_element_type=jnp.float32) + jnp.dot(
+            lows[away], states[...], preferred_element_type=jnp.float32)
+
+
+def dense_kernel(step, in_pairs, chain, counts, coords, tiles, highs, lows,
+                 buf, coord_buf, spots, sems, acc):
+    place_tiles(step, in_pairs, chain, counts, coords, tiles, buf, coord_buf, spots, sems, acc)
+    fold(acc, in_pairs, highs, lows)
 
 
 def product_kernel(parts, highs, lows, *refs):
@@ -137,21 +138,20 @@
     coords = tile_coords.reshape(relations, 2, 2 * pairs)
     seeds = seeds[None, :]
 
-    small = out_blocks * in_pairs * TILE * LANES * 4 <= 4 << 20
     smem = pl.BlockSpec(memory_space=pltpu.SMEM)
     vmem = pl.BlockSpec(memory_space=pltpu.VMEM)
     hbm = pl.BlockSpec(memory_space=pltpu.HBM)
     dense_bytes = out_blocks * in_pairs * TILE * LANES * 4
-    params = pltpu.CompilerParams(
-        vmem_limit_bytes=(3 if small else 2) * dense_bytes + pairs * TILE * LANES * 4 + (6 << 20))
-    product_params = pltpu.CompilerParams(vmem_limit_bytes=dense_bytes + (8 << 20))
+    dense_params = pltpu.CompilerParams(vmem_limit_bytes=2 * dense_bytes + pairs * TILE * LANES * 4 + (2 << 20))
+    first_params = pltpu.CompilerParams(vmem_limit_bytes=3 * dense_bytes + pairs * TILE * LANES * 4 + (4 << 20))
+    product_params = pltpu.CompilerParams(vmem_limit_bytes=rows_in * rows_out + (8 << 20))
     work = [
         pltpu.VMEM((pairs, TILE, 2 * TILE), f32),
-        pltpu.SMEM((2, 2 * pairs), jnp.int32),
-        pltpu.SemaphoreType.DMA((MIN_SHARE,)),
-        pltpu.SemaphoreType.DMA(()),
+        pltpu.VMEM((2, 2 * pairs), jnp.int32),
+        pltpu.SMEM((1, 2 * pairs), jnp.int32),
+        pltpu.SemaphoreType.DMA((MIN_SHARE + 1,)),
+        pltpu.VMEM((2 * out_blocks * in_pairs, TILE, LANES), f32),
     ]
-    accs = [pltpu.VMEM((out_blocks * in_pairs, TILE, LANES), f32)] * (2 if small else 1)
     dense = pltpu.VMEM((2, rows_out, rows_in), bf16)
     partial = pltpu.VMEM((rows_out, QUERIES), f32)
 
@@ -169,19 +169,19 @@
             out_shape=[partial, partial],
             in_specs=[smem, smem, vmem, hbm, hbm],
             out_specs=[vmem, vmem],
-            scratch_shapes=work + [pltpu.VMEM(dense.shape, bf16)] * 2 + accs,
-            compiler_params=params,
+            scratch_shapes=work + [pltpu.VMEM(dense.shape, bf16)] * 2 + [pltpu.VMEM((rows_in, QUERIES), bf16)],
+            compiler_params=first_params,
             name="first",
         )(*given)
 
     def densify(step):
         return pl.pallas_call(
-            functools.partial(dense_kernel, step, out_blocks, in_pairs),
+            functools.partial(dense_kernel, step, in_pairs),
             out_shape=[dense, dense],
             in_specs=[smem, smem, hbm, hbm],
             out_specs=[vmem, vmem],
-            scratch_shapes=work + accs,
-            compiler_params=params,
+            scratch_shapes=work,
+            compiler_params=dense_params,
             cost_estimate=pl.CostEstimate(flops=0, bytes_accessed=8 << 20, transcendentals=0),
         )(*given[:2], *given[3:])
 

time: 72.7 us -> 68.8 us (0.946)
  starting transfers between devices: 22.8 us -> 20.2 us
  Pallas kernels: 13.2 us -> 12 us
    ppermute x18, starting transfers between devices: 22.8 us -> 20.2 us  [swap(): return lax.ppermute(x, axis, [(i, i ^ flip) for i in range(size)])]
  transfers between devices with their start and end apart: 18 -> 18, of which waited for: 14 -> 14; matrix products, arithmetic and copies ran while one was open for 0% -> 0% of each run, Pallas kernels for 10% -> 9%
where the time goes in v2:
time: 68.8 us; the launch traced here: 68.5 us
  waiting for transfers between devices  24.7 us (36%)
  starting transfers between devices  20.2 us (29%)
  Pallas kernels  12 us (17%)
  blocking collectives  10.6 us (15%)
  other arithmetic  0.86 us (1%)
    ppermute x18, waiting for transfers between devices, swap(): return lax.ppermute(x, axis, [(i, i ^ flip) for i in range(size)])  24.7 us
    ppermute x18, starting transfers between devices, swap(): return lax.ppermute(x, axis, [(i, i ^ flip) for i in range(size)])  20.2 us
    all_to_all x1, blocking collectives, shards(): lax.all_to_all(jnp.broadcast_to(squares, (devices, QUERIES)), ('row', 'co...  10.6 us
    pallas_call x2, Pallas kernels, densify(): pl.pallas_call(functools.partial(dense_kernel, step, in_pairs), out_shape...  6.38 us
    pallas_call x1, Pallas kernels, first(): pl.pallas_call(functools.partial(first_kernel, out_blocks, in_pairs), out...  4.11 us
    pallas_call x2, Pallas kernels, product(): pl.pallas_call(functools.partial(product_kernel, len(pieces)), out_shape=...  1.48 us
  transfers between devices with their start and end apart: 18, of which 14 were waited for; matrix products, arithmetic and copies ran while one was open for 0% of the time, Pallas kernels for 9%

profile of v2, /device:TPU:0, one launch (start us, length us, event | category | flops | bytes accessed | tf_op | source)
XLA Modules:
  0.0 68.5 jit_solution(15086014112336421423)
XLA Ops:
  0.0 4.1 %first.1 = (f32[512,128]{1,0:T(8,128)S(1)}, f32[512,128]{1,0:T(8,128)S(1)}) custom-call(s32[3]{0:T(128)} %chain.5, s32[1,1,3]{2,1,0:T(1,128)} %counts.5, s32[1,128]{1,0:T(1,128)} %bitcast.11, s32[3,2,256]{2,1,0:T(2,128)} %bitcast.8, f32[3,128,64,128]{3,2,1,0:T(8,128)} %bitcast.4), custom_call_target="tpu_custom_call" | custom-call | tf_op jit(solution)/shard_map/first/pallas_call | solution.py:167
  4.4 1.3 %collective-permute-done = f32[512,128]{1,0:T(8,128)S(1)} collective-permute-done((f32[512,128]{1,0:T(8,128)S(1)}, f32[512,128]{1,0:T(8,128)S(1)}, u32[]{:S(2)}, u32[]{:S(2)}) %collective-permute-start) | collective-permute-done | bytes 262176 | tf_op jit(solution)/shard_map/ppermute | solution.py:200
  5.8 3.1 %collective-permute-start.1 = (f32[128,128]{1,0:T(8,128)S(1)}, f32[128,128]{1,0:T(8,128)S(1)}, u32[]{:S(2)}, u32[]{:S(2)}) collective-permute-start(f32[128,128]{1,0:T(8,128)S(1)} %get-tuple-element.33), channel_id=1, source_target_pairs={{0,2},{1,3},{2,0},{3,1},{4,6},{5,7},{6,4},{7,5},{8,10},{9,11},{10,... | collective-permute-start | bytes 196616 | tf_op jit(solution)/shard_map/ppermute | solution.py:200
  8.9 2.5 %collective-permute-start.3 = (f32[128,128]{1,0:T(8,128)S(1)}, f32[128,128]{1,0:T(8,128)S(1)}, u32[]{:S(2)}, u32[]{:S(2)}) collective-permute-start(f32[128,128]{1,0:T(8,128)S(1)} %get-tuple-element.34), channel_id=1, source_target_pairs={{0,6},{1,7},{2,4},{3,5},{4,2},{5,3},{6,0},{7,1},{8,14},{9,15},{10,... | collective-permute-start | bytes 196616 | tf_op jit(solution)/shard_map/ppermute | solution.py:200
  11.4 4.4 %collective-permute-done.3 = f32[128,128]{1,0:T(8,128)S(1)} collective-permute-done((f32[128,128]{1,0:T(8,128)S(1)}, f32[128,128]{1,0:T(8,128)S(1)}, u32[]{:S(2)}, u32[]{:S(2)}) %collective-permute-start.3) | collective-permute-done | bytes 65568 | tf_op jit(solution)/shard_map/ppermute | solution.py:200
  15.9 2.1 %collective-permute-done.2 = f32[128,128]{1,0:T(8,128)S(1)} collective-permute-done((f32[128,128]{1,0:T(8,128)S(1)}, f32[128,128]{1,0:T(8,128)S(1)}, u32[]{:S(2)}, u32[]{:S(2)}) %collective-permute-start.2) | collective-permute-done | bytes 65568 | tf_op jit(solution)/shard_map/ppermute | solution.py:200
  18.0 2.4 %collective-permute-start.6 = (f32[128,128]{1,0:T(8,128)S(1)}, f32[128,128]{1,0:T(8,128)S(1)}, u32[]{:S(2)}, u32[]{:S(2)}) collective-permute-start(f32[128,128]{1,0:T(8,128)S(1)} %fusion.5.refs_0_), channel_id=1, source_target_pairs={{0,24},{8,16},{16,8},{24,0},{1,25},{9,17},{17,9},{25,1},{2,26},{10... | collective-permute-start | bytes 196616 | tf_op jit(solution)/shard_map/ppermute | solution.py:200
  20.4 0.9 %collective-permute-start.5 = (f32[128,128]{1,0:T(8,128)S(1)}, f32[128,128]{1,0:T(8,128)S(1)}, u32[]{:S(2)}, u32[]{:S(2)}) collective-permute-start(f32[128,128]{1,0:T(8,128)S(1)} %fusion.5.refs_0_), channel_id=1, source_target_pairs={{0,16},{8,24},{16,0},{24,8},{1,17},{9,25},{17,1},{25,9},{2,18},{10... | collective-permute-start | bytes 196616 | tf_op jit(solution)/shard_map/ppermute | solution.py:200
  21.6 3.0 %shard_map.56 = (bf16[2,512,512]{2,1,0:T(8,128)(2,1)S(1)}, bf16[2,512,512]{2,1,0:T(8,128)(2,1)S(1)}) custom-call(s32[3]{0:T(128)} %chain.5, s32[1,1,3]{2,1,0:T(1,128)} %counts.5, s32[3,2,256]{2,1,0:T(2,128)} %bitcast.9, f32[3,128,64,128]{3,2,1,0:T(8,128)} %bitcast.5), custom_call_target="tpu_custom_call" | custom-call | bytes 8388608 | tf_op jit(solution)/shard_map/pallas_call | solution.py:178
  24.6 0.9 %collective-permute-done.4.refs_1_ = f32[128,128]{1,0:T(8,128)S(1)} collective-permute-done((f32[128,128]{1,0:T(8,128)S(1)}, f32[128,128]{1,0:T(8,128)S(1)}, u32[]{:S(2)}, u32[]{:S(2)}) %collective-permute-start.4) | collective-permute-done | bytes 65568 | tf_op jit(solution)/shard_map/ppermute | solution.py:200
  26.4 1.5 %collective-permute-done.7 = f32[512,128]{1,0:T(8,128)S(1)} collective-permute-done((f32[512,128]{1,0:T(8,128)S(1)}, f32[512,128]{1,0:T(8,128)S(1)}, u32[]{:S(2)}, u32[]{:S(2)}) %collective-permute-start.7) | collective-permute-done | bytes 262176 | tf_op jit(solution)/shard_map/ppermute | solution.py:200
  28.1 2.2 %collective-permute-start.10 = (f32[128,128]{1,0:T(8,128)S(1)}, f32[128,128]{1,0:T(8,128)S(1)}, u32[]{:S(2)}, u32[]{:S(2)}) collective-permute-start(f32[128,128]{1,0:T(8,128)S(1)} %get-tuple-element.31), channel_id=1, source_target_pairs={{0,6},{1,7},{2,4},{3,5},{4,2},{5,3},{6,0},{7,1},{8,14},{9,15},{10,... | collective-permute-start | bytes 196616 | tf_op jit(solution)/shard_map/ppermute | solution.py:200
  30.3 1.2 %collective-permute-start.9 = (f32[128,128]{1,0:T(8,128)S(1)}, f32[128,128]{1,0:T(8,128)S(1)}, u32[]{:S(2)}, u32[]{:S(2)}) collective-permute-start(f32[128,128]{1,0:T(8,128)S(1)} %get-tuple-element.32), channel_id=1, source_target_pairs={{0,4},{1,5},{2,6},{3,7},{4,0},{5,1},{6,2},{7,3},{8,12},{9,13},{10,... | collective-permute-start | bytes 196616 | tf_op jit(solution)/shard_map/ppermute | solution.py:200
  32.3 2.2 %collective-permute-done.10 = f32[128,128]{1,0:T(8,128)S(1)} collective-permute-done((f32[128,128]{1,0:T(8,128)S(1)}, f32[128,128]{1,0:T(8,128)S(1)}, u32[]{:S(2)}, u32[]{:S(2)}) %collective-permute-start.10) | collective-permute-done | bytes 65568 | tf_op jit(solution)/shard_map/ppermute | solution.py:200
  34.5 3.1 %collective-permute-done.9 = f32[128,128]{1,0:T(8,128)S(1)} collective-permute-done((f32[128,128]{1,0:T(8,128)S(1)}, f32[128,128]{1,0:T(8,128)S(1)}, u32[]{:S(2)}, u32[]{:S(2)}) %collective-permute-start.9) | collective-permute-done | bytes 65568 | tf_op jit(solution)/shard_map/ppermute | solution.py:200
  37.6 2.1 %collective-permute-start.13 = (f32[128,128]{1,0:T(8,128)S(1)}, f32[128,128]{1,0:T(8,128)S(1)}, u32[]{:S(2)}, u32[]{:S(2)}) collective-permute-start(f32[128,128]{1,0:T(8,128)S(1)} %fusion.3.refs_0_), channel_id=1, source_target_pairs={{0,24},{8,16},{16,8},{24,0},{1,25},{9,17},{17,9},{25,1},{2,26},{10... | collective-permute-start | bytes 196616 | tf_op jit(solution)/shard_map/ppermute | solution.py:200
  39.7 1.2 %collective-permute-start.12 = (f32[128,128]{1,0:T(8,128)S(1)}, f32[128,128]{1,0:T(8,128)S(1)}, u32[]{:S(2)}, u32[]{:S(2)}) collective-permute-start(f32[128,128]{1,0:T(8,128)S(1)} %fusion.3.refs_0_), channel_id=1, source_target_pairs={{0,16},{8,24},{16,0},{24,8},{1,17},{9,25},{17,1},{25,9},{2,18},{10... | collective-permute-start | bytes 196616 | tf_op jit(solution)/shard_map/ppermute | solution.py:200
  41.2 3.4 %shard_map.55 = (bf16[2,512,512]{2,1,0:T(8,128)(2,1)S(1)}, bf16[2,512,512]{2,1,0:T(8,128)(2,1)S(1)}) custom-call(s32[3]{0:T(128)} %chain.5, s32[1,1,3]{2,1,0:T(1,128)} %counts.5, s32[3,2,256]{2,1,0:T(2,128)} %bitcast.10, f32[3,128,64,128]{3,2,1,0:T(8,128)} %bitcast.6), custom_call_target="tpu_custom_call" | custom-call | bytes 8388608 | tf_op jit(solution)/shard_map/pallas_call | solution.py:178
  46.0 1.5 %collective-permute-done.14 = f32[512,128]{1,0:T(8,128)S(1)} collective-permute-done((f32[512,128]{1,0:T(8,128)S(1)}, f32[512,128]{1,0:T(8,128)S(1)}, u32[]{:S(2)}, u32[]{:S(2)}) %collective-permute-start.14) | collective-permute-done | bytes 262176 | tf_op jit(solution)/shard_map/ppermute | solution.py:200
  47.7 1.6 %collective-permute-start.17 = (f32[128,128]{1,0:T(8,128)S(1)}, f32[128,128]{1,0:T(8,128)S(1)}, u32[]{:S(2)}, u32[]{:S(2)}) collective-permute-start(f32[128,128]{1,0:T(8,128)S(1)} %get-tuple-element.28), channel_id=1, source_target_pairs={{0,6},{1,7},{2,4},{3,5},{4,2},{5,3},{6,0},{7,1},{8,14},{9,15},{10,... | collective-permute-start | bytes 196616 | tf_op jit(solution)/shard_map/ppermute | solution.py:200
  49.3 1.8 %collective-permute-start.16 = (f32[128,128]{1,0:T(8,128)S(1)}, f32[128,128]{1,0:T(8,128)S(1)}, u32[]{:S(2)}, u32[]{:S(2)}) collective-permute-start(f32[128,128]{1,0:T(8,128)S(1)} %get-tuple-element.29), channel_id=1, source_target_pairs={{0,4},{1,5},{2,6},{3,7},{4,0},{5,1},{6,2},{7,3},{8,12},{9,13},{10,... | collective-permute-start | bytes 196616 | tf_op jit(solution)/shard_map/ppermute | solution.py:200
  51.9 2.5 %collective-permute-done.17 = f32[128,128]{1,0:T(8,128)S(1)} collective-permute-done((f32[128,128]{1,0:T(8,128)S(1)}, f32[128,128]{1,0:T(8,128)S(1)}, u32[]{:S(2)}, u32[]{:S(2)}) %collective-permute-start.17) | collective-permute-done | bytes 65568 | tf_op jit(solution)/shard_map/ppermute | solution.py:200
  54.5 2.7 %collective-permute-done.16 = f32[128,128]{1,0:T(8,128)S(1)} collective-permute-done((f32[128,128]{1,0:T(8,128)S(1)}, f32[128,128]{1,0:T(8,128)S(1)}, u32[]{:S(2)}, u32[]{:S(2)}) %collective-permute-start.16) | collective-permute-done | bytes 65568 | tf_op jit(solution)/shard_map/ppermute | solution.py:200
  57.3 10.6 %all_to_all.6 = f32[32,1,128]{2,1,0:T(1,128)S(1)} all-to-all(f32[32,1,128]{2,1,0:T(1,128)S(1)} %broadcast_in_dim.5), channel_id=1, replica_groups=mesh['row'=4,'col'=8] {'row','col'}, dimensions={0} | all-to-all | bytes 32768 | tf_op jit(solution)/shard_map/all_to_all | solution.py:220
  (31 shorter events, 5.7 us)
Async XLA Ops:
  4.1 1.6 %collective-permute-start = (f32[512,128]{1,0:T(8,128)S(1)}, f32[512,128]{1,0:T(8,128)S(1)}, u32[]{:S(2)}, u32[]{:S(2)}) collective-permute-start(f32[512,128]{1,0:T(8,128)S(1)} %get-tuple-element.20), channel_id=1, source_target_pairs={{0,1},{1,0},{2,3},{3,2},{4,5},{5,4},{6,7},{7,6},{8,9},{9,8},{10,11... | collective-permute-start | bytes 786440 | tf_op jit(solution)/shard_map/ppermute | solution.py:200
  5.8 5.6 %collective-permute-start.1 = (f32[128,128]{1,0:T(8,128)S(1)}, f32[128,128]{1,0:T(8,128)S(1)}, u32[]{:S(2)}, u32[]{:S(2)}) collective-permute-start(f32[128,128]{1,0:T(8,128)S(1)} %get-tuple-element.33), channel_id=1, source_target_pairs={{0,2},{1,3},{2,0},{3,1},{4,6},{5,7},{6,4},{7,5},{8,10},{9,11},{10,... | collective-permute-start | bytes 196616 | tf_op jit(solution)/shard_map/ppermute | solution.py:200
  8.9 7.0 %collective-permute-start.3 = (f32[128,128]{1,0:T(8,128)S(1)}, f32[128,128]{1,0:T(8,128)S(1)}, u32[]{:S(2)}, u32[]{:S(2)}) collective-permute-start(f32[128,128]{1,0:T(8,128)S(1)} %get-tuple-element.34), channel_id=1, source_target_pairs={{0,6},{1,7},{2,4},{3,5},{4,2},{5,3},{6,0},{7,1},{8,14},{9,15},{10,... | collective-permute-start | bytes 196616 | tf_op jit(solution)/shard_map/ppermute | solution.py:200
  11.4 6.6 %collective-permute-start.2 = (f32[128,128]{1,0:T(8,128)S(1)}, f32[128,128]{1,0:T(8,128)S(1)}, u32[]{:S(2)}, u32[]{:S(2)}) collective-permute-start(f32[128,128]{1,0:T(8,128)S(1)} %get-tuple-element.35), channel_id=1, source_target_pairs={{0,4},{1,5},{2,6},{3,7},{4,0},{5,1},{6,2},{7,3},{8,12},{9,13},{10,... | collective-permute-start | bytes 196616 | tf_op jit(solution)/shard_map/ppermute | solution.py:200
  18.0 6.5 %collective-permute-start.6 = (f32[128,128]{1,0:T(8,128)S(1)}, f32[128,128]{1,0:T(8,128)S(1)}, u32[]{:S(2)}, u32[]{:S(2)}) collective-permute-start(f32[128,128]{1,0:T(8,128)S(1)} %fusion.5.refs_0_), channel_id=1, source_target_pairs={{0,24},{8,16},{16,8},{24,0},{1,25},{9,17},{17,9},{25,1},{2,26},{10... | collective-permute-start | bytes 196616 | tf_op jit(solution)/shard_map/ppermute | solution.py:200
  20.4 4.3 %collective-permute-start.5 = (f32[128,128]{1,0:T(8,128)S(1)}, f32[128,128]{1,0:T(8,128)S(1)}, u32[]{:S(2)}, u32[]{:S(2)}) collective-permute-start(f32[128,128]{1,0:T(8,128)S(1)} %fusion.5.refs_0_), channel_id=1, source_target_pairs={{0,16},{8,24},{16,0},{24,8},{1,17},{9,25},{17,1},{25,9},{2,18},{10... | collective-permute-start | bytes 196616 | tf_op jit(solution)/shard_map/ppermute | solution.py:200
  21.3 4.3 %collective-permute-start.4 = (f32[128,128]{1,0:T(8,128)S(1)}, f32[128,128]{1,0:T(8,128)S(1)}, u32[]{:S(2)}, u32[]{:S(2)}) collective-permute-start(f32[128,128]{1,0:T(8,128)S(1)} %fusion.5.refs_0_), channel_id=1, source_target_pairs={{0,8},{8,0},{16,24},{24,16},{1,9},{9,1},{17,25},{25,17},{2,10},{10... | collective-permute-start | bytes 196616 | tf_op jit(solution)/shard_map/ppermute | solution.py:200
  26.3 1.6 %collective-permute-start.7 = (f32[512,128]{1,0:T(8,128)S(1)}, f32[512,128]{1,0:T(8,128)S(1)}, u32[]{:S(2)}, u32[]{:S(2)}) collective-permute-start(f32[512,128]{1,0:T(8,128)S(1)} %get-tuple-element.22), channel_id=1, source_target_pairs={{0,1},{1,0},{2,3},{3,2},{4,5},{5,4},{6,7},{7,6},{8,9},{9,8},{10,11... | collective-permute-start | bytes 786440 | tf_op jit(solution)/shard_map/ppermute | solution.py:200
  28.0 4.3 %collective-permute-start.8 = (f32[128,128]{1,0:T(8,128)S(1)}, f32[128,128]{1,0:T(8,128)S(1)}, u32[]{:S(2)}, u32[]{:S(2)}) collective-permute-start(f32[128,128]{1,0:T(8,128)S(1)} %get-tuple-element.30), channel_id=1, source_target_pairs={{0,2},{1,3},{2,0},{3,1},{4,6},{5,7},{6,4},{7,5},{8,10},{9,11},{10,... | collective-permute-start | bytes 196616 | tf_op jit(solution)/shard_map/ppermute | solution.py:200
  28.1 6.5 %collective-permute-start.10 = (f32[128,128]{1,0:T(8,128)S(1)}, f32[128,128]{1,0:T(8,128)S(1)}, u32[]{:S(2)}, u32[]{:S(2)}) collective-permute-start(f32[128,128]{1,0:T(8,128)S(1)} %get-tuple-element.31), channel_id=1, source_target_pairs={{0,6},{1,7},{2,4},{3,5},{4,2},{5,3},{6,0},{7,1},{8,14},{9,15},{10,... | collective-permute-start | bytes 196616 | tf_op jit(solution)/shard_map/ppermute | solution.py:200
  30.3 7.3 %collective-permute-start.9 = (f32[128,128]{1,0:T(8,128)S(1)}, f32[128,128]{1,0:T(8,128)S(1)}, u32[]{:S(2)}, u32[]{:S(2)}) collective-permute-start(f32[128,128]{1,0:T(8,128)S(1)} %get-tuple-element.32), channel_id=1, source_target_pairs={{0,4},{1,5},{2,6},{3,7},{4,0},{5,1},{6,2},{7,3},{8,12},{9,13},{10,... | collective-permute-start | bytes 196616 | tf_op jit(solution)/shard_map/ppermute | solution.py:200
  37.6 7.0 %collective-permute-start.13 = (f32[128,128]{1,0:T(8,128)S(1)}, f32[128,128]{1,0:T(8,128)S(1)}, u32[]{:S(2)}, u32[]{:S(2)}) collective-permute-start(f32[128,128]{1,0:T(8,128)S(1)} %fusion.3.refs_0_), channel_id=1, source_target_pairs={{0,24},{8,16},{16,8},{24,0},{1,25},{9,17},{17,9},{25,1},{2,26},{10... | collective-permute-start | bytes 196616 | tf_op jit(solution)/shard_map/ppermute | solution.py:200
  39.7 4.8 %collective-permute-start.12 = (f32[128,128]{1,0:T(8,128)S(1)}, f32[128,128]{1,0:T(8,128)S(1)}, u32[]{:S(2)}, u32[]{:S(2)}) collective-permute-start(f32[128,128]{1,0:T(8,128)S(1)} %fusion.3.refs_0_), channel_id=1, source_target_pairs={{0,16},{8,24},{16,0},{24,8},{1,17},{9,25},{17,1},{25,9},{2,18},{10... | collective-permute-start | bytes 196616 | tf_op jit(solution)/shard_map/ppermute | solution.py:200
  40.9 4.3 %collective-permute-start.11 = (f32[128,128]{1,0:T(8,128)S(1)}, f32[128,128]{1,0:T(8,128)S(1)}, u32[]{:S(2)}, u32[]{:S(2)}) collective-permute-start(f32[128,128]{1,0:T(8,128)S(1)} %fusion.3.refs_0_), channel_id=1, source_target_pairs={{0,8},{8,0},{16,24},{24,16},{1,9},{9,1},{17,25},{25,17},{2,10},{10... | collective-permute-start | bytes 196616 | tf_op jit(solution)/shard_map/ppermute | solution.py:200
  45.9 1.6 %collective-permute-start.14 = (f32[512,128]{1,0:T(8,128)S(1)}, f32[512,128]{1,0:T(8,128)S(1)}, u32[]{:S(2)}, u32[]{:S(2)}) collective-permute-start(f32[512,128]{1,0:T(8,128)S(1)} %get-tuple-element.24), channel_id=1, source_target_pairs={{0,1},{1,0},{2,3},{3,2},{4,5},{5,4},{6,7},{7,6},{8,9},{9,8},{10,11... | collective-permute-start | bytes 786440 | tf_op jit(solution)/shard_map/ppermute | solution.py:200
  47.6 4.3 %collective-permute-start.15 = (f32[128,128]{1,0:T(8,128)S(1)}, f32[128,128]{1,0:T(8,128)S(1)}, u32[]{:S(2)}, u32[]{:S(2)}) collective-permute-start(f32[128,128]{1,0:T(8,128)S(1)} %get-tuple-element.27), channel_id=1, source_target_pairs={{0,2},{1,3},{2,0},{3,1},{4,6},{5,7},{6,4},{7,5},{8,10},{9,11},{10,... | collective-permute-start | bytes 196616 | tf_op jit(solution)/shard_map/ppermute | solution.py:200
  47.7 6.8 %collective-permute-start.17 = (f32[128,128]{1,0:T(8,128)S(1)}, f32[128,128]{1,0:T(8,128)S(1)}, u32[]{:S(2)}, u32[]{:S(2)}) collective-permute-start(f32[128,128]{1,0:T(8,128)S(1)} %get-tuple-element.28), channel_id=1, source_target_pairs={{0,6},{1,7},{2,4},{3,5},{4,2},{5,3},{6,0},{7,1},{8,14},{9,15},{10,... | collective-permute-start | bytes 196616 | tf_op jit(solution)/shard_map/ppermute | solution.py:200
  49.3 7.9 %collective-permute-start.16 = (f32[128,128]{1,0:T(8,128)S(1)}, f32[128,128]{1,0:T(8,128)S(1)}, u32[]{:S(2)}, u32[]{:S(2)}) collective-permute-start(f32[128,128]{1,0:T(8,128)S(1)} %get-tuple-element.29), channel_id=1, source_target_pairs={{0,4},{1,5},{2,6},{3,7},{4,0},{5,1},{6,2},{7,3},{8,12},{9,13},{10,... | collective-permute-start | bytes 196616 | tf_op jit(solution)/shard_map/ppermute | solution.py:200

commit v3 on v2

v3 whole, which is shorter than its diff:
```python
import functools

import jax
import jax.numpy as jnp
from jax import lax
from jax.experimental import pallas as pl
from jax.experimental.pallas import tpu as pltpu
from jax.sharding import PartitionSpec as P


QUERIES = 128
TILE = 64
BLOCKS_DEV = 2
HOPS = 3
ROWS_DEV = BLOCKS_DEV * TILE
LANES = 128
MIN_SHARE = 8


def place_tiles(step, in_pairs, chain, counts, coords, tiles, buf, coord_buf, spots, sems, acc):
    pairs = tiles.shape[1]
    chunk = pairs // MIN_SHARE
    blocks = acc.shape[0] // 2
    relation = chain[step]
    live_chunks = counts[0, 0, relation] // (2 * chunk)
    copy_coords = pltpu.make_async_copy(coords.at[relation], coord_buf, sems.at[MIN_SHARE])
    copy_coords.start()

    def chunk_copy(index):
        span = pl.ds(index * chunk, chunk)
        return pltpu.make_async_copy(tiles.at[relation, span], buf.at[span], sems.at[index])

    for index in range(MIN_SHARE):
        @pl.when(index < live_chunks)
        def _(index=index):
            chunk_copy(index).start()

    copy_coords.wait()
    slot = lax.broadcasted_iota(jnp.int32, (1, 2 * pairs), 1)
    i = coord_buf[0:1, :] ^ (lax.axis_index("col") * BLOCKS_DEV)
    j = coord_buf[1:2, :] ^ (lax.axis_index("row") * BLOCKS_DEV)
    coord_buf[0:1, :] = ((j ^ slot) & 1) * blocks + i * in_pairs + (j >> 1)
    copy_spots = pltpu.make_async_copy(coord_buf.at[pl.ds(0, 1)], spots, sems.at[MIN_SHARE])
    copy_spots.start()

    @pl.loop(0, 2 * blocks // 8)
    def _(b):
        for u in range(8):
            acc[b * 8 + u] = jnp.zeros((TILE, LANES), jnp.float32)

    left = lax.broadcasted_iota(jnp.int32, (TILE, LANES), 1) < TILE
    copy_spots.wait()

    def add_pair(t):
        even, odd = spots[0, 2 * t], spots[0, 2 * t + 1]
        values = buf[t]
        new_even = acc[even] + values
        new_odd = acc[odd] + values
        pltpu.store(acc.at[even], new_even, mask=left)
        pltpu.store(acc.at[odd], new_odd, mask=jnp.logical_not(left))

    @pl.loop(0, live_chunks)
    def _(index):
        chunk_copy(index).wait()

        @pl.loop(0, chunk // 4)
        def _(t):
            for u in range(4):
                add_pair(index * chunk + t * 4 + u)


def split(x):
    high = x.astype(jnp.bfloat16)
    return high, (x - high.astype(jnp.float32)).astype(jnp.bfloat16)


def block_rows(acc, in_pairs, first, high, low, at):
    blocks = acc.shape[0] // 2
    for k in range(BLOCKS_DEV):
        for jp in range(in_pairs):
            block = (first + k) * in_pairs + jp
            span = (pl.ds(at + k * TILE, TILE), pl.ds(jp * LANES, LANES))
            high[span], low[span] = split(acc[block] + pltpu.roll(acc[blocks + block], TILE, 1))


def one_hot_product(acc, states, in_pairs, away, high, low, out):
    for chip in range(out.shape[0] // ROWS_DEV):
        span = pl.ds(chip * ROWS_DEV, ROWS_DEV)
        block_rows(acc, in_pairs, (2 * chip + away) * BLOCKS_DEV, high, low, chip * ROWS_DEV)
        out[span] = jnp.dot(high[span], states[...], preferred_element_type=jnp.float32) + jnp.dot(
            low[span], states[...], preferred_element_type=jnp.float32)


def first_send_kernel(in_pairs, chain, counts, seeds, coords, tiles, send, acc, states,
                      buf, coord_buf, spots, sems, high, low):
    cols = send.shape[0] // ROWS_DEV * 2
    block = seeds[...] // ROWS_DEV
    target = ((block // cols) ^ lax.axis_index("row")) * ROWS_DEV + seeds[...] % ROWS_DEV
    target = jnp.where(block % cols == lax.axis_index("col"), target, -1)
    entity = lax.broadcasted_iota(jnp.int32, states.shape, 0)
    states[...] = (entity == target).astype(jnp.float32).astype(jnp.bfloat16)
    place_tiles(0, in_pairs, chain, counts, coords, tiles, buf, coord_buf, spots, sems, acc)
    one_hot_product(acc, states, in_pairs, 1, high, low, send)


def first_keep_kernel(in_pairs, acc, states, keep, high, low):
    one_hot_product(acc, states, in_pairs, 0, high, low, keep)


def dense_kernel(step, in_pairs, chain, counts, coords, tiles, keep_high, keep_low, send_high, send_low,
                 buf, coord_buf, spots, sems, acc):
    place_tiles(step, in_pairs, chain, counts, coords, tiles, buf, coord_buf, spots, sems, acc)

    @pl.loop(0, keep_high.shape[0] // ROWS_DEV)
    def _(chip):
        at = pl.multiple_of(chip * ROWS_DEV, ROWS_DEV)
        block_rows(acc, in_pairs, 2 * chip * BLOCKS_DEV, keep_high, keep_low, at)
        block_rows(acc, in_pairs, (2 * chip + 1) * BLOCKS_DEV, send_high, send_low, at)


def product_kernel(parts, high, low, *refs):
    pieces, (out, weights) = refs[:parts], refs[parts:]
    for k, piece in enumerate(pieces):
        above, below = split(piece[...])
        weights[k * ROWS_DEV:(k + 1) * ROWS_DEV, :QUERIES] = above
        weights[k * ROWS_DEV:(k + 1) * ROWS_DEV, QUERIES:] = below
    both = jnp.dot(high[...], weights[...], preferred_element_type=jnp.float32)
    rest = jnp.dot(low[...], weights[:, :QUERIES], preferred_element_type=jnp.float32)
    out[...] = both[:, :QUERIES] + (both[:, QUERIES:] + rest)


def shards(tiles, tile_coords, tile_count, seeds, chain):
    row_total = lax.axis_size("row")
    col_total = lax.axis_size("col")
    out_blocks = col_total * BLOCKS_DEV
    in_pairs = row_total
    depth_total = col_total // 2
    rows_out = depth_total * ROWS_DEV
    rows_in = in_pairs * LANES
    relations, pairs = tiles.shape[2], tiles.shape[3]
    f32, bf16 = jnp.float32, jnp.bfloat16

    tiles = tiles.reshape(relations, pairs, TILE, 2 * TILE)
    coords = tile_coords.reshape(relations, 2, 2 * pairs)
    seeds = seeds[None, :]

    smem = pl.BlockSpec(memory_space=pltpu.SMEM)
    vmem = pl.BlockSpec(memory_space=pltpu.VMEM)
    hbm = pl.BlockSpec(memory_space=pltpu.HBM)
    dense_bytes = out_blocks * in_pairs * TILE * LANES * 4
    tile_bytes = pairs * TILE * LANES * 4
    work = [
        pltpu.VMEM((pairs, TILE, 2 * TILE), f32),
        pltpu.VMEM((2, 2 * pairs), jnp.int32),
        pltpu.SMEM((1, 2 * pairs), jnp.int32),
        pltpu.SemaphoreType.DMA((MIN_SHARE + 1,)),
    ]
    sums = pltpu.VMEM((2 * out_blocks * in_pairs, TILE, LANES), f32)
    half = pltpu.VMEM((rows_out, rows_in), bf16)
    partial = pltpu.VMEM((rows_out, QUERIES), f32)
    one_hot = pltpu.VMEM((rows_in, QUERIES), bf16)

    def limit(size):
        return pltpu.CompilerParams(vmem_limit_bytes=size + (2 << 20))

    def cost(flops):
        return pl.CostEstimate(flops=flops, bytes_accessed=1 << 20, transcendentals=0)

    def local(x):
        return pltpu.with_memory_space_constraint(x, pltpu.VMEM)

    def remain(x):
        return pltpu.with_memory_space_constraint(x, pltpu.HBM)

    given = [remain(x) for x in (chain, tile_count, seeds, coords, tiles)]

    def first_send():
        return pl.pallas_call(
            functools.partial(first_send_kernel, in_pairs),
            out_shape=[partial, sums, one_hot],
            in_specs=[smem, smem, vmem, hbm, hbm],
            out_specs=[vmem] * 3,
            scratch_shapes=work + [half] * 2,
            compiler_params=limit(tile_bytes + dense_bytes // 2),
            name="first_send",
        )(*given)

    def first_keep(acc, states):
        return pl.pallas_call(
            functools.partial(first_keep_kernel, in_pairs),
            out_shape=partial,
            in_specs=[vmem] * 2,
            out_specs=vmem,
            scratch_shapes=[half] * 2,
            compiler_params=limit(dense_bytes // 2),
            cost_estimate=cost(4 * rows_out * rows_in * QUERIES),
            name="first_keep",
        )(local(acc), local(states))

    def densify(step):
        return pl.pallas_call(
            functools.partial(dense_kernel, step, in_pairs),
            out_shape=[half] * 4,
            in_specs=[smem, smem, hbm, hbm],
            out_specs=[vmem] * 4,
            scratch_shapes=work + [sums],
            compiler_params=limit(tile_bytes + 2 * dense_bytes),
            cost_estimate=pl.CostEstimate(flops=0, bytes_accessed=8 << 20, transcendentals=0),
        )(*given[:2], *given[3:])

    def product(high, low, pieces):
        return pl.pallas_call(
            functools.partial(product_kernel, len(pieces)),
            out_shape=partial,
            in_specs=[vmem] * (2 + len(pieces)),
            out_specs=vmem,
            scratch_shapes=[pltpu.VMEM((rows_in, 2 * QUERIES), bf16)],
            compiler_params=limit(4 << 20),
            cost_estimate=cost(6 * rows_out * rows_in * QUERIES),
            name="product",
        )(local(high), local(low), *map(local, pieces))

    def swap(x, axis, size, flip):
        return lax.ppermute(x, axis, [(i, i ^ flip) for i in range(size)])

    for step in range(HOPS):
        if step == 0:
            send, acc, states = first_send()
        else:
            send = product(*relation[2:], pieces)
        crossing = swap(send, "col", col_total, 1)
        keep = first_keep(acc, states) if step == 0 else product(*relation[:2], pieces)
        summed = keep + crossing
        arrived = [
            swap(summed[k * ROWS_DEV:(k + 1) * ROWS_DEV], "col", col_total, 2 * k)
            for k in range(1, depth_total)
        ]
        if step + 1 < HOPS:
            relation = densify(step + 1)
        owned = summed[:ROWS_DEV]
        for part in arrived:
            owned = owned + part
        if step + 1 < HOPS:
            pieces = [owned] + [swap(owned, "row", row_total, k) for k in range(1, row_total)]

    squares = jnp.sum(owned * owned, axis=0, keepdims=True)
    devices = row_total * col_total
    shared = lax.all_to_all(
        jnp.broadcast_to(squares, (devices, QUERIES)), ("row", "col"), 0, 0, tiled=True)
    totals = jnp.sum(shared, axis=0)
    return owned * lax.rsqrt(totals / (devices * ROWS_DEV) + 1e-06)


def solution(mesh):
    in_specs = (
        P("row", "col", None, None, None, None),
        P("row", "col", None, None, None),
        P("row", "col", None),
        P(),
        P(),
    )
    out_specs = P(("row", "col"), None)
    return jax.shard_map(shards, mesh=mesh, in_specs=in_specs, out_specs=out_specs, check_vma=False)
```

time: 68.8 us -> 65.5 us (0.952)
  waiting for transfers between devices: 24.7 us -> 20 us
  starting transfers between devices: 20.2 us -> 22.1 us
    ppermute x18, waiting for transfers between devices: 24.7 us -> 20 us  [swap(): return lax.ppermute(x, axis, [(i, i ^ flip) for i in range(size)])]
    ppermute x18, starting transfers between devices: 20.2 us -> 22.1 us  [swap(): return lax.ppermute(x, axis, [(i, i ^ flip) for i in range(size)])]
    pallas_call x2 -> x4, Pallas kernels: 1.48 us -> 1.88 us  [product(): pl.pallas_call(functools.partial(product_kernel, len(pieces)), out_shape=...]
    pallas_call x1 -> x2, Pallas kernels: 4.11 us -> 3.76 us  [the longest x1 3.17 us: first_send(): pl.pallas_call(functools.partial(first_send_kernel, in_pairs), out_shape=...]
  transfers between devices with their start and end apart: 18 -> 18, of which waited for: 14 -> 10; matrix products, arithmetic and copies ran while one was open for 0% -> 0% of each run, Pallas kernels for 9% -> 12%
where the time goes in v3:
time: 65.5 us; the launch traced here: 65.2 us
  starting transfers between devices  22.1 us (34%)
  waiting for transfers between devices  20 us (31%)
  Pallas kernels  12 us (18%)
  blocking collectives  10.1 us (15%)
  other arithmetic  0.82 us (1%)
    ppermute x18, starting transfers between devices, swap(): return lax.ppermute(x, axis, [(i, i ^ flip) for i in range(size)])  22.1 us
    ppermute x18, waiting for transfers between devices, swap(): return lax.ppermute(x, axis, [(i, i ^ flip) for i in range(size)])  20 us
    all_to_all x1, blocking collectives, shards(): lax.all_to_all(jnp.broadcast_to(squares, (devices, QUERIES)), ('row', 'co...  10.1 us
    pallas_call x2, Pallas kernels, densify(): pl.pallas_call(functools.partial(dense_kernel, step, in_pairs), out_shape...  6.38 us
    pallas_call x1, Pallas kernels, first_send(): pl.pallas_call(functools.partial(first_send_kernel, in_pairs), out_shape=...  3.17 us
    pallas_call x4, Pallas kernels, product(): pl.pallas_call(functools.partial(product_kernel, len(pieces)), out_shape=...  1.88 us
  transfers between devices with their start and end apart: 18, of which 10 were waited for; matrix products, arithmetic and copies ran while one was open for 0% of the time, Pallas kernels for 12%

profile of v3, /device:TPU:0, one launch (start us, length us, event | category | flops | bytes accessed | tf_op | source)
XLA Modules:
  0.0 65.2 jit_solution(12579459123587703648)
XLA Ops:
  0.0 3.2 %first_send.1 = (f32[512,128]{1,0:T(8,128)S(1)}, f32[128,64,128]{2,1,0:T(8,128)S(1)}, bf16[512,128]{1,0:T(8,128)(2,1)S(1)}) custom-call(s32[3]{0:T(128)} %chain.5, s32[1,1,3]{2,1,0:T(1,128)} %counts.5, s32[1,128]{1,0:T(1,128)} %bitcast.11, s32[3,2,256]{2,1,0:T(2,128)} %bitcast.8, f32[3,128,64,128]{3,2,1,0:T(8,128)} %bitcast.4), custom_call_target="tpu_custom_call" | custom-call | tf_op jit(solution)/shard_map/first_send/pallas_call | solution.py:178
  4.0 0.7 %collective-permute-done = f32[512,128]{1,0:T(8,128)S(1)} collective-permute-done((f32[512,128]{1,0:T(8,128)S(1)}, f32[512,128]{1,0:T(8,128)S(1)}, u32[]{:S(2)}, u32[]{:S(2)}) %collective-permute-start) | collective-permute-done | bytes 262176 | tf_op jit(solution)/shard_map/ppermute | solution.py:224
  4.8 3.1 %collective-permute-start.1 = (f32[128,128]{1,0:T(8,128)S(1)}, f32[128,128]{1,0:T(8,128)S(1)}, u32[]{:S(2)}, u32[]{:S(2)}) collective-permute-start(f32[128,128]{1,0:T(8,128)S(1)} %get-tuple-element.35), channel_id=1, source_target_pairs={{0,2},{1,3},{2,0},{3,1},{4,6},{5,7},{6,4},{7,5},{8,10},{9,11},{10,... | collective-permute-start | bytes 196616 | tf_op jit(solution)/shard_map/ppermute | solution.py:224
  8.0 2.1 %collective-permute-start.2 = (f32[128,128]{1,0:T(8,128)S(1)}, f32[128,128]{1,0:T(8,128)S(1)}, u32[]{:S(2)}, u32[]{:S(2)}) collective-permute-start(f32[128,128]{1,0:T(8,128)S(1)} %get-tuple-element.37), channel_id=1, source_target_pairs={{0,4},{1,5},{2,6},{3,7},{4,0},{5,1},{6,2},{7,3},{8,12},{9,13},{10,... | collective-permute-start | bytes 196616 | tf_op jit(solution)/shard_map/ppermute | solution.py:224
  10.5 5.8 %collective-permute-done.2 = f32[128,128]{1,0:T(8,128)S(1)} collective-permute-done((f32[128,128]{1,0:T(8,128)S(1)}, f32[128,128]{1,0:T(8,128)S(1)}, u32[]{:S(2)}, u32[]{:S(2)}) %collective-permute-start.2) | collective-permute-done | bytes 65568 | tf_op jit(solution)/shard_map/ppermute | solution.py:224
  16.3 2.0 %collective-permute-start.4 = (f32[128,128]{1,0:T(8,128)S(1)}, f32[128,128]{1,0:T(8,128)S(1)}, u32[]{:S(2)}, u32[]{:S(2)}) collective-permute-start(f32[128,128]{1,0:T(8,128)S(1)} %fusion.5.refs_0_), channel_id=1, source_target_pairs={{0,8},{8,0},{16,24},{24,16},{1,9},{9,1},{17,25},{25,17},{2,10},{10... | collective-permute-start | bytes 196616 | tf_op jit(solution)/shard_map/ppermute | solution.py:224
  18.3 1.2 %collective-permute-start.5 = (f32[128,128]{1,0:T(8,128)S(1)}, f32[128,128]{1,0:T(8,128)S(1)}, u32[]{:S(2)}, u32[]{:S(2)}) collective-permute-start(f32[128,128]{1,0:T(8,128)S(1)} %fusion.5.refs_0_), channel_id=1, source_target_pairs={{0,16},{8,24},{16,0},{24,8},{1,17},{9,25},{17,1},{25,9},{2,18},{10... | collective-permute-start | bytes 196616 | tf_op jit(solution)/shard_map/ppermute | solution.py:224
  19.9 3.0 %shard_map.56 = (bf16[512,512]{1,0:T(8,128)(2,1)S(1)}, bf16[512,512]{1,0:T(8,128)(2,1)S(1)}, bf16[512,512]{1,0:T(8,128)(2,1)S(1)}, bf16[512,512]{1,0:T(8,128)(2,1)S(1)}) custom-call(s32[3]{0:T(128)} %chain.5, s32[1,1,3]{2,1,0:T(1,128)} %counts.5, s32[3,2,256]{2,1,0:T(2,128)} %bitcast.9, f32[3,128,64,128]{3,2,1,0:T(8,128)} %bitcast.5), custom_call_target="tpu_custom_call" | custom-call | bytes 8388608 | tf_op jit(solution)/shard_map/pallas_call | solution.py:201
  22.9 1.8 %collective-permute-done.6.refs_3_ = f32[128,128]{1,0:T(8,128)S(1)} collective-permute-done((f32[128,128]{1,0:T(8,128)S(1)}, f32[128,128]{1,0:T(8,128)S(1)}, u32[]{:S(2)}, u32[]{:S(2)}) %collective-permute-start.6) | collective-permute-done | bytes 65568 | tf_op jit(solution)/shard_map/ppermute | solution.py:224
  25.7 1.0 %collective-permute-done.7 = f32[512,128]{1,0:T(8,128)S(1)} collective-permute-done((f32[512,128]{1,0:T(8,128)S(1)}, f32[512,128]{1,0:T(8,128)S(1)}, u32[]{:S(2)}, u32[]{:S(2)}) %collective-permute-start.7) | collective-permute-done | bytes 262176 | tf_op jit(solution)/shard_map/ppermute | solution.py:224
  26.8 2.1 %collective-permute-start.10 = (f32[128,128]{1,0:T(8,128)S(1)}, f32[128,128]{1,0:T(8,128)S(1)}, u32[]{:S(2)}, u32[]{:S(2)}) collective-permute-start(f32[128,128]{1,0:T(8,128)S(1)} %get-tuple-element.33), channel_id=1, source_target_pairs={{0,6},{1,7},{2,4},{3,5},{4,2},{5,3},{6,0},{7,1},{8,14},{9,15},{10,... | collective-permute-start | bytes 196616 | tf_op jit(solution)/shard_map/ppermute | solution.py:224
  29.3 2.0 %collective-permute-start.9 = (f32[128,128]{1,0:T(8,128)S(1)}, f32[128,128]{1,0:T(8,128)S(1)}, u32[]{:S(2)}, u32[]{:S(2)}) collective-permute-start(f32[128,128]{1,0:T(8,128)S(1)} %get-tuple-element.34), channel_id=1, source_target_pairs={{0,4},{1,5},{2,6},{3,7},{4,0},{5,1},{6,2},{7,3},{8,12},{9,13},{10,... | collective-permute-start | bytes 196616 | tf_op jit(solution)/shard_map/ppermute | solution.py:224
  31.3 2.3 %collective-permute-done.10 = f32[128,128]{1,0:T(8,128)S(1)} collective-permute-done((f32[128,128]{1,0:T(8,128)S(1)}, f32[128,128]{1,0:T(8,128)S(1)}, u32[]{:S(2)}, u32[]{:S(2)}) %collective-permute-start.10) | collective-permute-done | bytes 65568 | tf_op jit(solution)/shard_map/ppermute | solution.py:224
  33.6 1.5 %collective-permute-done.8 = f32[128,128]{1,0:T(8,128)S(1)} collective-permute-done((f32[128,128]{1,0:T(8,128)S(1)}, f32[128,128]{1,0:T(8,128)S(1)}, u32[]{:S(2)}, u32[]{:S(2)}) %collective-permute-start.8) | collective-permute-done | bytes 65568 | tf_op jit(solution)/shard_map/ppermute | solution.py:224
  35.1 1.1 %collective-permute-done.9 = f32[128,128]{1,0:T(8,128)S(1)} collective-permute-done((f32[128,128]{1,0:T(8,128)S(1)}, f32[128,128]{1,0:T(8,128)S(1)}, u32[]{:S(2)}, u32[]{:S(2)}) %collective-permute-start.9) | collective-permute-done | bytes 65568 | tf_op jit(solution)/shard_map/ppermute | solution.py:224
  36.2 1.1 %collective-permute-start.11 = (f32[128,128]{1,0:T(8,128)S(1)}, f32[128,128]{1,0:T(8,128)S(1)}, u32[]{:S(2)}, u32[]{:S(2)}) collective-permute-start(f32[128,128]{1,0:T(8,128)S(1)} %fusion.3.refs_0_), channel_id=1, source_target_pairs={{0,8},{8,0},{16,24},{24,16},{1,9},{9,1},{17,25},{25,17},{2,10},{10... | collective-permute-start | bytes 196616 | tf_op jit(solution)/shard_map/ppermute | solution.py:224
  37.3 2.4 %collective-permute-start.13 = (f32[128,128]{1,0:T(8,128)S(1)}, f32[128,128]{1,0:T(8,128)S(1)}, u32[]{:S(2)}, u32[]{:S(2)}) collective-permute-start(f32[128,128]{1,0:T(8,128)S(1)} %fusion.3.refs_0_), channel_id=1, source_target_pairs={{0,24},{8,16},{16,8},{24,0},{1,25},{9,17},{17,9},{25,1},{2,26},{10... | collective-permute-start | bytes 196616 | tf_op jit(solution)/shard_map/ppermute | solution.py:224
  39.7 3.4 %shard_map.55 = (bf16[512,512]{1,0:T(8,128)(2,1)S(1)}, bf16[512,512]{1,0:T(8,128)(2,1)S(1)}, bf16[512,512]{1,0:T(8,128)(2,1)S(1)}, bf16[512,512]{1,0:T(8,128)(2,1)S(1)}) custom-call(s32[3]{0:T(128)} %chain.5, s32[1,1,3]{2,1,0:T(1,128)} %counts.5, s32[3,2,256]{2,1,0:T(2,128)} %bitcast.10, f32[3,128,64,128]{3,2,1,0:T(8,128)} %bitcast.6), custom_call_target="tpu_custom_call" | custom-call | bytes 8388608 | tf_op jit(solution)/shard_map/pallas_call | solution.py:201
  44.2 1.0 %collective-permute-done.14 = f32[512,128]{1,0:T(8,128)S(1)} collective-permute-done((f32[512,128]{1,0:T(8,128)S(1)}, f32[512,128]{1,0:T(8,128)S(1)}, u32[]{:S(2)}, u32[]{:S(2)}) %collective-permute-start.14) | collective-permute-done | bytes 262176 | tf_op jit(solution)/shard_map/ppermute | solution.py:224
  45.9 2.2 %collective-permute-start.16 = (f32[128,128]{1,0:T(8,128)S(1)}, f32[128,128]{1,0:T(8,128)S(1)}, u32[]{:S(2)}, u32[]{:S(2)}) collective-permute-start(f32[128,128]{1,0:T(8,128)S(1)} %get-tuple-element.31), channel_id=1, source_target_pairs={{0,4},{1,5},{2,6},{3,7},{4,0},{5,1},{6,2},{7,3},{8,12},{9,13},{10,... | collective-permute-start | bytes 196616 | tf_op jit(solution)/shard_map/ppermute | solution.py:224
  48.1 1.7 %collective-permute-start.17 = (f32[128,128]{1,0:T(8,128)S(1)}, f32[128,128]{1,0:T(8,128)S(1)}, u32[]{:S(2)}, u32[]{:S(2)}) collective-permute-start(f32[128,128]{1,0:T(8,128)S(1)} %get-tuple-element.30), channel_id=1, source_target_pairs={{0,6},{1,7},{2,4},{3,5},{4,2},{5,3},{6,0},{7,1},{8,14},{9,15},{10,... | collective-permute-start | bytes 196616 | tf_op jit(solution)/shard_map/ppermute | solution.py:224
  50.3 4.1 %collective-permute-done.16 = f32[128,128]{1,0:T(8,128)S(1)} collective-permute-done((f32[128,128]{1,0:T(8,128)S(1)}, f32[128,128]{1,0:T(8,128)S(1)}, u32[]{:S(2)}, u32[]{:S(2)}) %collective-permute-start.16) | collective-permute-done | bytes 65568 | tf_op jit(solution)/shard_map/ppermute | solution.py:224
  54.4 10.1 %all_to_all.6 = f32[32,1,128]{2,1,0:T(1,128)S(1)} all-to-all(f32[32,1,128]{2,1,0:T(1,128)S(1)} %broadcast_in_dim.5), channel_id=1, replica_groups=mesh['row'=4,'col'=8] {'row','col'}, dimensions={0} | all-to-all | bytes 32768 | tf_op jit(solution)/shard_map/all_to_all | solution.py:248
  64.6 0.6 broadcast_multiply_fusion
  (34 shorter events, 5.4 us)
Async XLA Ops:
  3.2 1.6 %collective-permute-start = (f32[512,128]{1,0:T(8,128)S(1)}, f32[512,128]{1,0:T(8,128)S(1)}, u32[]{:S(2)}, u32[]{:S(2)}) collective-permute-start(f32[512,128]{1,0:T(8,128)S(1)} %get-tuple-element.22), channel_id=1, source_target_pairs={{0,1},{1,0},{2,3},{3,2},{4,5},{5,4},{6,7},{7,6},{8,9},{9,8},{10,11... | collective-permute-start | bytes 786440 | tf_op jit(solution)/shard_map/ppermute | solution.py:224
  4.8 5.6 %collective-permute-start.1 = (f32[128,128]{1,0:T(8,128)S(1)}, f32[128,128]{1,0:T(8,128)S(1)}, u32[]{:S(2)}, u32[]{:S(2)}) collective-permute-start(f32[128,128]{1,0:T(8,128)S(1)} %get-tuple-element.35), channel_id=1, source_target_pairs={{0,2},{1,3},{2,0},{3,1},{4,6},{5,7},{6,4},{7,5},{8,10},{9,11},{10,... | collective-permute-start | bytes 196616 | tf_op jit(solution)/shard_map/ppermute | solution.py:224
  8.0 8.3 %collective-permute-start.2 = (f32[128,128]{1,0:T(8,128)S(1)}, f32[128,128]{1,0:T(8,128)S(1)}, u32[]{:S(2)}, u32[]{:S(2)}) collective-permute-start(f32[128,128]{1,0:T(8,128)S(1)} %get-tuple-element.37), channel_id=1, source_target_pairs={{0,4},{1,5},{2,6},{3,7},{4,0},{5,1},{6,2},{7,3},{8,12},{9,13},{10,... | collective-permute-start | bytes 196616 | tf_op jit(solution)/shard_map/ppermute | solution.py:224
  10.1 6.2 %collective-permute-start.3 = (f32[128,128]{1,0:T(8,128)S(1)}, f32[128,128]{1,0:T(8,128)S(1)}, u32[]{:S(2)}, u32[]{:S(2)}) collective-permute-start(f32[128,128]{1,0:T(8,128)S(1)} %get-tuple-element.36), channel_id=1, source_target_pairs={{0,6},{1,7},{2,4},{3,5},{4,2},{5,3},{6,0},{7,1},{8,14},{9,15},{10,... | collective-permute-start | bytes 196616 | tf_op jit(solution)/shard_map/ppermute | solution.py:224
  16.3 6.5 %collective-permute-start.4 = (f32[128,128]{1,0:T(8,128)S(1)}, f32[128,128]{1,0:T(8,128)S(1)}, u32[]{:S(2)}, u32[]{:S(2)}) collective-permute-start(f32[128,128]{1,0:T(8,128)S(1)} %fusion.5.refs_0_), channel_id=1, source_target_pairs={{0,8},{8,0},{16,24},{24,16},{1,9},{9,1},{17,25},{25,17},{2,10},{10... | collective-permute-start | bytes 196616 | tf_op jit(solution)/shard_map/ppermute | solution.py:224
  18.3 4.6 %collective-permute-start.5 = (f32[128,128]{1,0:T(8,128)S(1)}, f32[128,128]{1,0:T(8,128)S(1)}, u32[]{:S(2)}, u32[]{:S(2)}) collective-permute-start(f32[128,128]{1,0:T(8,128)S(1)} %fusion.5.refs_0_), channel_id=1, source_target_pairs={{0,16},{8,24},{16,0},{24,8},{1,17},{9,25},{17,1},{25,9},{2,18},{10... | collective-permute-start | bytes 196616 | tf_op jit(solution)/shard_map/ppermute | solution.py:224
  19.5 5.2 %collective-permute-start.6 = (f32[128,128]{1,0:T(8,128)S(1)}, f32[128,128]{1,0:T(8,128)S(1)}, u32[]{:S(2)}, u32[]{:S(2)}) collective-permute-start(f32[128,128]{1,0:T(8,128)S(1)} %fusion.5.refs_0_), channel_id=1, source_target_pairs={{0,24},{8,16},{16,8},{24,0},{1,25},{9,17},{17,9},{25,1},{2,26},{10... | collective-permute-start | bytes 196616 | tf_op jit(solution)/shard_map/ppermute | solution.py:224
  25.2 1.6 %collective-permute-start.7 = (f32[512,128]{1,0:T(8,128)S(1)}, f32[512,128]{1,0:T(8,128)S(1)}, u32[]{:S(2)}, u32[]{:S(2)}) collective-permute-start(f32[512,128]{1,0:T(8,128)S(1)} %product.5), channel_id=1, source_target_pairs={{0,1},{1,0},{2,3},{3,2},{4,5},{5,4},{6,7},{7,6},{8,9},{9,8},{10,11... | collective-permute-start | bytes 786440 | tf_op jit(solution)/shard_map/ppermute | solution.py:224
  26.8 6.8 %collective-permute-start.10 = (f32[128,128]{1,0:T(8,128)S(1)}, f32[128,128]{1,0:T(8,128)S(1)}, u32[]{:S(2)}, u32[]{:S(2)}) collective-permute-start(f32[128,128]{1,0:T(8,128)S(1)} %get-tuple-element.33), channel_id=1, source_target_pairs={{0,6},{1,7},{2,4},{3,5},{4,2},{5,3},{6,0},{7,1},{8,14},{9,15},{10,... | collective-permute-start | bytes 196616 | tf_op jit(solution)/shard_map/ppermute | solution.py:224
  28.9 6.1 %collective-permute-start.8 = (f32[128,128]{1,0:T(8,128)S(1)}, f32[128,128]{1,0:T(8,128)S(1)}, u32[]{:S(2)}, u32[]{:S(2)}) collective-permute-start(f32[128,128]{1,0:T(8,128)S(1)} %get-tuple-element.32), channel_id=1, source_target_pairs={{0,2},{1,3},{2,0},{3,1},{4,6},{5,7},{6,4},{7,5},{8,10},{9,11},{10,... | collective-permute-start | bytes 196616 | tf_op jit(solution)/shard_map/ppermute | solution.py:224
  29.3 6.9 %collective-permute-start.9 = (f32[128,128]{1,0:T(8,128)S(1)}, f32[128,128]{1,0:T(8,128)S(1)}, u32[]{:S(2)}, u32[]{:S(2)}) collective-permute-start(f32[128,128]{1,0:T(8,128)S(1)} %get-tuple-element.34), channel_id=1, source_target_pairs={{0,4},{1,5},{2,6},{3,7},{4,0},{5,1},{6,2},{7,3},{8,12},{9,13},{10,... | collective-permute-start | bytes 196616 | tf_op jit(solution)/shard_map/ppermute | solution.py:224
  36.2 7.0 %collective-permute-start.11 = (f32[128,128]{1,0:T(8,128)S(1)}, f32[128,128]{1,0:T(8,128)S(1)}, u32[]{:S(2)}, u32[]{:S(2)}) collective-permute-start(f32[128,128]{1,0:T(8,128)S(1)} %fusion.3.refs_0_), channel_id=1, source_target_pairs={{0,8},{8,0},{16,24},{24,16},{1,9},{9,1},{17,25},{25,17},{2,10},{10... | collective-permute-start | bytes 196616 | tf_op jit(solution)/shard_map/ppermute | solution.py:224
  37.3 5.9 %collective-permute-start.12 = (f32[128,128]{1,0:T(8,128)S(1)}, f32[128,128]{1,0:T(8,128)S(1)}, u32[]{:S(2)}, u32[]{:S(2)}) collective-permute-start(f32[128,128]{1,0:T(8,128)S(1)} %fusion.3.refs_0_), channel_id=1, source_target_pairs={{0,16},{8,24},{16,0},{24,8},{1,17},{9,25},{17,1},{25,9},{2,18},{10... | collective-permute-start | bytes 196616 | tf_op jit(solution)/shard_map/ppermute | solution.py:224
  37.3 5.9 %collective-permute-start.13 = (f32[128,128]{1,0:T(8,128)S(1)}, f32[128,128]{1,0:T(8,128)S(1)}, u32[]{:S(2)}, u32[]{:S(2)}) collective-permute-start(f32[128,128]{1,0:T(8,128)S(1)} %fusion.3.refs_0_), channel_id=1, source_target_pairs={{0,24},{8,16},{16,8},{24,0},{1,25},{9,17},{17,9},{25,1},{2,26},{10... | collective-permute-start | bytes 196616 | tf_op jit(solution)/shard_map/ppermute | solution.py:224
  43.6 1.6 %collective-permute-start.14 = (f32[512,128]{1,0:T(8,128)S(1)}, f32[512,128]{1,0:T(8,128)S(1)}, u32[]{:S(2)}, u32[]{:S(2)}) collective-permute-start(f32[512,128]{1,0:T(8,128)S(1)} %product.7), channel_id=1, source_target_pairs={{0,1},{1,0},{2,3},{3,2},{4,5},{5,4},{6,7},{7,6},{8,9},{9,8},{10,11... | collective-permute-start | bytes 786440 | tf_op jit(solution)/shard_map/ppermute | solution.py:224
  45.3 5.0 %collective-permute-start.15 = (f32[128,128]{1,0:T(8,128)S(1)}, f32[128,128]{1,0:T(8,128)S(1)}, u32[]{:S(2)}, u32[]{:S(2)}) collective-permute-start(f32[128,128]{1,0:T(8,128)S(1)} %get-tuple-element.29), channel_id=1, source_target_pairs={{0,2},{1,3},{2,0},{3,1},{4,6},{5,7},{6,4},{7,5},{8,10},{9,11},{10,... | collective-permute-start | bytes 196616 | tf_op jit(solution)/shard_map/ppermute | solution.py:224
  45.9 8.5 %collective-permute-start.16 = (f32[128,128]{1,0:T(8,128)S(1)}, f32[128,128]{1,0:T(8,128)S(1)}, u32[]{:S(2)}, u32[]{:S(2)}) collective-permute-start(f32[128,128]{1,0:T(8,128)S(1)} %get-tuple-element.31), channel_id=1, source_target_pairs={{0,4},{1,5},{2,6},{3,7},{4,0},{5,1},{6,2},{7,3},{8,12},{9,13},{10,... | collective-permute-start | bytes 196616 | tf_op jit(solution)/shard_map/ppermute | solution.py:224
  48.1 6.3 %collective-permute-start.17 = (f32[128,128]{1,0:T(8,128)S(1)}, f32[128,128]{1,0:T(8,128)S(1)}, u32[]{:S(2)}, u32[]{:S(2)}) collective-permute-start(f32[128,128]{1,0:T(8,128)S(1)} %get-tuple-element.30), channel_id=1, source_target_pairs={{0,6},{1,7},{2,4},{3,5},{4,2},{5,3},{6,0},{7,1},{8,14},{9,15},{10,... | collective-permute-start | bytes 196616 | tf_op jit(solution)/shard_map/ppermute | solution.py:224

commit v4 on v3

--- a/solution.py
+++ b/solution.py
@@ -15,6 +15,10 @@
 ROWS_DEV = BLOCKS_DEV * TILE
 LANES = 128
 MIN_SHARE = 8
+
+
+def visits(chips):
+    return [0, *range(2, chips), 1], [0, 2, 1, *range(3, chips)]
 
 
 def place_tiles(step, in_pairs, chain, counts, coords, tiles, buf, coord_buf, spots, sems, acc):
@@ -38,6 +42,14 @@
     copy_coords.wait()
     slot = lax.broadcasted_iota(jnp.int32, (1, 2 * pairs), 1)
     i = coord_buf[0:1, :] ^ (lax.axis_index("col") * BLOCKS_DEV)
+    group = 2 * BLOCKS_DEV
+    owner = (lax.axis_index("col") ^ (i // BLOCKS_DEV)) & 1
+    chip = i // group
+    turn = jnp.zeros_like(i)
+    for core, order in enumerate(visits(blocks // in_pairs // group)):
+        for place, flip in enumerate(order):
+            turn = jnp.where((owner == core) & (chip == flip), place, turn)
+    i = turn * group + i % group
     j = coord_buf[1:2, :] ^ (lax.axis_index("row") * BLOCKS_DEV)
     coord_buf[0:1, :] = ((j ^ slot) & 1) * blocks + i * in_pairs + (j >> 1)
     copy_spots = pltpu.make_async_copy(coord_buf.at[pl.ds(0, 1)], spots, sems.at[MIN_SHARE])
@@ -231,10 +243,13 @@
         crossing = swap(send, "col", col_total, 1)
         keep = first_keep(acc, states) if step == 0 else product(*relation[:2], pieces)
         summed = keep + crossing
-        arrived = [
-            swap(summed[k * ROWS_DEV:(k + 1) * ROWS_DEV], "col", col_total, 2 * k)
-            for k in range(1, depth_total)
-        ]
+        arrived = []
+        for turn, flips in enumerate(zip(*visits(depth_total))):
+            if turn:
+                pairs_there = [(2 * z + core, 2 * (z ^ flips[core]) + core)
+                               for z in range(depth_total) for core in range(2)]
+                arrived.append(
+                    lax.ppermute(summed[turn * ROWS_DEV:(turn + 1) * ROWS_DEV], "col", pairs_there))
         if step + 1 < HOPS:
             relation = densify(step + 1)
         owned = summed[:ROWS_DEV]

time: 65.5 us -> 65.2 us (level)
  starting transfers between devices: 22.1 us -> 21 us
    ppermute x0 -> x9, waiting for transfers between devices: none -> 15.3 us  [shards(): lax.ppermute(summed[turn * ROWS_DEV:(turn + 1) * ROWS_DEV], 'col', pairs_...]
    ppermute x18 -> x9, waiting for transfers between devices: 20 us -> 5.06 us  [swap(): return lax.ppermute(x, axis, [(i, i ^ flip) for i in range(size)])]
    ppermute x18 -> x9, starting transfers between devices: 22.1 us -> 7.51 us  [swap(): return lax.ppermute(x, axis, [(i, i ^ flip) for i in range(size)])]
    ppermute x0 -> x9, starting transfers between devices: none -> 13.5 us  [shards(): lax.ppermute(summed[turn * ROWS_DEV:(turn + 1) * ROWS_DEV], 'col', pairs_...]
  transfers between devices with their start and end apart: 18 -> 18, of which waited for: 10 -> 11; matrix products, arithmetic and copies ran while one was open for 0% -> 0% of each run, Pallas kernels for 12% -> 12%
where the time goes in v4:
time: 65.2 us; the launch traced here: 65 us
  starting transfers between devices  21 us (32%)
  waiting for transfers between devices  20.3 us (31%)
  Pallas kernels  12.1 us (19%)
  blocking collectives  10.5 us (16%)
  other arithmetic  0.82 us (1%)
    ppermute x9, waiting for transfers between devices, shards(): lax.ppermute(summed[turn * ROWS_DEV:(turn + 1) * ROWS_DEV], 'col', pairs_...  15.3 us
    ppermute x9, starting transfers between devices, shards(): lax.ppermute(summed[turn * ROWS_DEV:(turn + 1) * ROWS_DEV], 'col', pairs_...  13.5 us
    all_to_all x1, blocking collectives, shards(): lax.all_to_all(jnp.broadcast_to(squares, (devices, QUERIES)), ('row', 'co...  10.5 us
    ppermute x9, starting transfers between devices, swap(): return lax.ppermute(x, axis, [(i, i ^ flip) for i in range(size)])  7.51 us
    pallas_call x2, Pallas kernels, densify(): pl.pallas_call(functools.partial(dense_kernel, step, in_pairs), out_shape...  6.41 us
    ppermute x9, waiting for transfers between devices, swap(): return lax.ppermute(x, axis, [(i, i ^ flip) for i in range(size)])  5.06 us
    pallas_call x1, Pallas kernels, first_send(): pl.pallas_call(functools.partial(first_send_kernel, in_pairs), out_shape=...  3.18 us
    pallas_call x4, Pallas kernels, product(): pl.pallas_call(functools.partial(product_kernel, len(pieces)), out_shape=...  1.88 us
  transfers between devices with their start and end apart: 18, of which 11 were waited for; matrix products, arithmetic and copies ran while one was open for 0% of the time, Pallas kernels for 12%

profile of v4, /device:TPU:0, one launch (start us, length us, event | category | flops | bytes accessed | tf_op | source)
XLA Modules:
  0.0 65.0 jit_solution(13980943632131871286)
XLA Ops:
  0.0 3.2 %first_send.1 = (f32[512,128]{1,0:T(8,128)S(1)}, f32[128,64,128]{2,1,0:T(8,128)S(1)}, bf16[512,128]{1,0:T(8,128)(2,1)S(1)}) custom-call(s32[3]{0:T(128)} %chain.5, s32[1,1,3]{2,1,0:T(1,128)} %counts.5, s32[1,128]{1,0:T(1,128)} %bitcast.11, s32[3,2,256]{2,1,0:T(2,128)} %bitcast.8, f32[3,128,64,128]{3,2,1,0:T(8,128)} %bitcast.4), custom_call_target="tpu_custom_call" | custom-call | tf_op jit(solution)/shard_map/first_send/pallas_call | solution.py:190
  4.1 0.7 %collective-permute-done = f32[512,128]{1,0:T(8,128)S(1)} collective-permute-done((f32[512,128]{1,0:T(8,128)S(1)}, f32[512,128]{1,0:T(8,128)S(1)}, u32[]{:S(2)}, u32[]{:S(2)}) %collective-permute-start) | collective-permute-done | bytes 262176 | tf_op jit(solution)/shard_map/ppermute | solution.py:236
  4.8 4.2 %collective-permute-start.1 = (f32[128,128]{1,0:T(8,128)S(1)}, f32[128,128]{1,0:T(8,128)S(1)}, u32[]{:S(2)}, u32[]{:S(2)}) collective-permute-start(f32[128,128]{1,0:T(8,128)S(1)} %get-tuple-element.35), channel_id=1, source_target_pairs={{0,4},{1,5},{2,6},{3,7},{4,0},{5,1},{6,2},{7,3},{8,12},{9,13},{10,... | collective-permute-start | bytes 196616 | tf_op jit(solution)/shard_map/ppermute | solution.py:252
  9.0 1.3 %collective-permute-start.2 = (f32[128,128]{1,0:T(8,128)S(1)}, f32[128,128]{1,0:T(8,128)S(1)}, u32[]{:S(2)}, u32[]{:S(2)}) collective-permute-start(f32[128,128]{1,0:T(8,128)S(1)} %get-tuple-element.37), channel_id=1, source_target_pairs={{0,6},{1,3},{2,4},{3,1},{4,2},{5,7},{6,0},{7,5},{8,14},{9,11},{10,... | collective-permute-start | bytes 196616 | tf_op jit(solution)/shard_map/ppermute | solution.py:252
  10.3 2.5 %collective-permute-done.1 = f32[128,128]{1,0:T(8,128)S(1)} collective-permute-done((f32[128,128]{1,0:T(8,128)S(1)}, f32[128,128]{1,0:T(8,128)S(1)}, u32[]{:S(2)}, u32[]{:S(2)}) %collective-permute-start.1) | collective-permute-done | bytes 65568 | tf_op jit(solution)/shard_map/ppermute | solution.py:252
  12.9 2.7 %collective-permute-done.2 = f32[128,128]{1,0:T(8,128)S(1)} collective-permute-done((f32[128,128]{1,0:T(8,128)S(1)}, f32[128,128]{1,0:T(8,128)S(1)}, u32[]{:S(2)}, u32[]{:S(2)}) %collective-permute-start.2) | collective-permute-done | bytes 65568 | tf_op jit(solution)/shard_map/ppermute | solution.py:252
  16.0 1.6 %collective-permute-start.4 = (f32[128,128]{1,0:T(8,128)S(1)}, f32[128,128]{1,0:T(8,128)S(1)}, u32[]{:S(2)}, u32[]{:S(2)}) collective-permute-start(f32[128,128]{1,0:T(8,128)S(1)} %fusion.5.refs_0_), channel_id=1, source_target_pairs={{0,8},{8,0},{16,24},{24,16},{1,9},{9,1},{17,25},{25,17},{2,10},{10... | collective-permute-start | bytes 196616 | tf_op jit(solution)/shard_map/ppermute | solution.py:236
  17.6 1.6 %collective-permute-start.5 = (f32[128,128]{1,0:T(8,128)S(1)}, f32[128,128]{1,0:T(8,128)S(1)}, u32[]{:S(2)}, u32[]{:S(2)}) collective-permute-start(f32[128,128]{1,0:T(8,128)S(1)} %fusion.5.refs_0_), channel_id=1, source_target_pairs={{0,16},{8,24},{16,0},{24,8},{1,17},{9,25},{17,1},{25,9},{2,18},{10... | collective-permute-start | bytes 196616 | tf_op jit(solution)/shard_map/ppermute | solution.py:236
  19.6 3.0 %shard_map.56 = (bf16[512,512]{1,0:T(8,128)(2,1)S(1)}, bf16[512,512]{1,0:T(8,128)(2,1)S(1)}, bf16[512,512]{1,0:T(8,128)(2,1)S(1)}, bf16[512,512]{1,0:T(8,128)(2,1)S(1)}) custom-call(s32[3]{0:T(128)} %chain.5, s32[1,1,3]{2,1,0:T(1,128)} %counts.5, s32[3,2,256]{2,1,0:T(2,128)} %bitcast.9, f32[3,128,64,128]{3,2,1,0:T(8,128)} %bitcast.5), custom_call_target="tpu_custom_call" | custom-call | bytes 8388608 | tf_op jit(solution)/shard_map/pallas_call | solution.py:213
  22.6 1.8 %collective-permute-done.6.refs_3_ = f32[128,128]{1,0:T(8,128)S(1)} collective-permute-done((f32[128,128]{1,0:T(8,128)S(1)}, f32[128,128]{1,0:T(8,128)S(1)}, u32[]{:S(2)}, u32[]{:S(2)}) %collective-permute-start.6) | collective-permute-done | bytes 65568 | tf_op jit(solution)/shard_map/ppermute | solution.py:236
  25.4 1.0 %collective-permute-done.7 = f32[512,128]{1,0:T(8,128)S(1)} collective-permute-done((f32[512,128]{1,0:T(8,128)S(1)}, f32[512,128]{1,0:T(8,128)S(1)}, u32[]{:S(2)}, u32[]{:S(2)}) %collective-permute-start.7) | collective-permute-done | bytes 262176 | tf_op jit(solution)/shard_map/ppermute | solution.py:236
  26.5 0.8 %collective-permute-start.10 = (f32[128,128]{1,0:T(8,128)S(1)}, f32[128,128]{1,0:T(8,128)S(1)}, u32[]{:S(2)}, u32[]{:S(2)}) collective-permute-start(f32[128,128]{1,0:T(8,128)S(1)} %get-tuple-element.33), channel_id=1, source_target_pairs={{0,2},{1,7},{2,0},{3,5},{4,6},{5,3},{6,4},{7,1},{8,10},{9,15},{10,... | collective-permute-start | bytes 196616 | tf_op jit(solution)/shard_map/ppermute | solution.py:252
  27.3 1.9 %collective-permute-start.8 = (f32[128,128]{1,0:T(8,128)S(1)}, f32[128,128]{1,0:T(8,128)S(1)}, u32[]{:S(2)}, u32[]{:S(2)}) collective-permute-start(f32[128,128]{1,0:T(8,128)S(1)} %get-tuple-element.32), channel_id=1, source_target_pairs={{0,4},{1,5},{2,6},{3,7},{4,0},{5,1},{6,2},{7,3},{8,12},{9,13},{10,... | collective-permute-start | bytes 196616 | tf_op jit(solution)/shard_map/ppermute | solution.py:252
  29.1 1.8 %collective-permute-start.9 = (f32[128,128]{1,0:T(8,128)S(1)}, f32[128,128]{1,0:T(8,128)S(1)}, u32[]{:S(2)}, u32[]{:S(2)}) collective-permute-start(f32[128,128]{1,0:T(8,128)S(1)} %get-tuple-element.34), channel_id=1, source_target_pairs={{0,6},{1,3},{2,4},{3,1},{4,2},{5,7},{6,0},{7,5},{8,14},{9,11},{10,... | collective-permute-start | bytes 196616 | tf_op jit(solution)/shard_map/ppermute | solution.py:252
  30.9 4.4 %collective-permute-done.8 = f32[128,128]{1,0:T(8,128)S(1)} collective-permute-done((f32[128,128]{1,0:T(8,128)S(1)}, f32[128,128]{1,0:T(8,128)S(1)}, u32[]{:S(2)}, u32[]{:S(2)}) %collective-permute-start.8) | collective-permute-done | bytes 65568 | tf_op jit(solution)/shard_map/ppermute | solution.py:252
  35.4 0.9 %collective-permute-start.11 = (f32[128,128]{1,0:T(8,128)S(1)}, f32[128,128]{1,0:T(8,128)S(1)}, u32[]{:S(2)}, u32[]{:S(2)}) collective-permute-start(f32[128,128]{1,0:T(8,128)S(1)} %fusion.3.refs_0_), channel_id=1, source_target_pairs={{0,8},{8,0},{16,24},{24,16},{1,9},{9,1},{17,25},{25,17},{2,10},{10... | collective-permute-start | bytes 196616 | tf_op jit(solution)/shard_map/ppermute | solution.py:236
  36.3 1.4 %collective-permute-start.12 = (f32[128,128]{1,0:T(8,128)S(1)}, f32[128,128]{1,0:T(8,128)S(1)}, u32[]{:S(2)}, u32[]{:S(2)}) collective-permute-start(f32[128,128]{1,0:T(8,128)S(1)} %fusion.3.refs_0_), channel_id=1, source_target_pairs={{0,16},{8,24},{16,0},{24,8},{1,17},{9,25},{17,1},{25,9},{2,18},{10... | collective-permute-start | bytes 196616 | tf_op jit(solution)/shard_map/ppermute | solution.py:236
  37.7 1.3 %collective-permute-start.13 = (f32[128,128]{1,0:T(8,128)S(1)}, f32[128,128]{1,0:T(8,128)S(1)}, u32[]{:S(2)}, u32[]{:S(2)}) collective-permute-start(f32[128,128]{1,0:T(8,128)S(1)} %fusion.3.refs_0_), channel_id=1, source_target_pairs={{0,24},{8,16},{16,8},{24,0},{1,25},{9,17},{17,9},{25,1},{2,26},{10... | collective-permute-start | bytes 196616 | tf_op jit(solution)/shard_map/ppermute | solution.py:236
  38.9 3.4 %shard_map.55 = (bf16[512,512]{1,0:T(8,128)(2,1)S(1)}, bf16[512,512]{1,0:T(8,128)(2,1)S(1)}, bf16[512,512]{1,0:T(8,128)(2,1)S(1)}, bf16[512,512]{1,0:T(8,128)(2,1)S(1)}) custom-call(s32[3]{0:T(128)} %chain.5, s32[1,1,3]{2,1,0:T(1,128)} %counts.5, s32[3,2,256]{2,1,0:T(2,128)} %bitcast.10, f32[3,128,64,128]{3,2,1,0:T(8,128)} %bitcast.6), custom_call_target="tpu_custom_call" | custom-call | bytes 8388608 | tf_op jit(solution)/shard_map/pallas_call | solution.py:213
  43.9 1.0 %collective-permute-done.14 = f32[512,128]{1,0:T(8,128)S(1)} collective-permute-done((f32[512,128]{1,0:T(8,128)S(1)}, f32[512,128]{1,0:T(8,128)S(1)}, u32[]{:S(2)}, u32[]{:S(2)}) %collective-permute-start.14) | collective-permute-done | bytes 262176 | tf_op jit(solution)/shard_map/ppermute | solution.py:236
  45.0 1.6 %collective-permute-start.15 = (f32[128,128]{1,0:T(8,128)S(1)}, f32[128,128]{1,0:T(8,128)S(1)}, u32[]{:S(2)}, u32[]{:S(2)}) collective-permute-start(f32[128,128]{1,0:T(8,128)S(1)} %get-tuple-element.29), channel_id=1, source_target_pairs={{0,4},{1,5},{2,6},{3,7},{4,0},{5,1},{6,2},{7,3},{8,12},{9,13},{10,... | collective-permute-start | bytes 196616 | tf_op jit(solution)/shard_map/ppermute | solution.py:252
  46.6 1.7 %collective-permute-start.16 = (f32[128,128]{1,0:T(8,128)S(1)}, f32[128,128]{1,0:T(8,128)S(1)}, u32[]{:S(2)}, u32[]{:S(2)}) collective-permute-start(f32[128,128]{1,0:T(8,128)S(1)} %get-tuple-element.31), channel_id=1, source_target_pairs={{0,6},{1,3},{2,4},{3,1},{4,2},{5,7},{6,0},{7,5},{8,14},{9,11},{10,... | collective-permute-start | bytes 196616 | tf_op jit(solution)/shard_map/ppermute | solution.py:252
  48.5 4.8 %collective-permute-done.15 = f32[128,128]{1,0:T(8,128)S(1)} collective-permute-done((f32[128,128]{1,0:T(8,128)S(1)}, f32[128,128]{1,0:T(8,128)S(1)}, u32[]{:S(2)}, u32[]{:S(2)}) %collective-permute-start.15) | collective-permute-done | bytes 65568 | tf_op jit(solution)/shard_map/ppermute | solution.py:252
  53.8 10.5 %all_to_all.6 = f32[32,1,128]{2,1,0:T(1,128)S(1)} all-to-all(f32[32,1,128]{2,1,0:T(1,128)S(1)} %broadcast_in_dim.5), channel_id=1, replica_groups=mesh['row'=4,'col'=8] {'row','col'}, dimensions={0} | all-to-all | bytes 32768 | tf_op jit(solution)/shard_map/all_to_all | solution.py:263
  (34 shorter events, 5.6 us)
Async XLA Ops:
  3.2 1.6 %collective-permute-start = (f32[512,128]{1,0:T(8,128)S(1)}, f32[512,128]{1,0:T(8,128)S(1)}, u32[]{:S(2)}, u32[]{:S(2)}) collective-permute-start(f32[512,128]{1,0:T(8,128)S(1)} %get-tuple-element.22), channel_id=1, source_target_pairs={{0,1},{1,0},{2,3},{3,2},{4,5},{5,4},{6,7},{7,6},{8,9},{9,8},{10,11... | collective-permute-start | bytes 786440 | tf_op jit(solution)/shard_map/ppermute | solution.py:236
  4.8 8.0 %collective-permute-start.1 = (f32[128,128]{1,0:T(8,128)S(1)}, f32[128,128]{1,0:T(8,128)S(1)}, u32[]{:S(2)}, u32[]{:S(2)}) collective-permute-start(f32[128,128]{1,0:T(8,128)S(1)} %get-tuple-element.35), channel_id=1, source_target_pairs={{0,4},{1,5},{2,6},{3,7},{4,0},{5,1},{6,2},{7,3},{8,12},{9,13},{10,... | collective-permute-start | bytes 196616 | tf_op jit(solution)/shard_map/ppermute | solution.py:252
  9.0 6.6 %collective-permute-start.2 = (f32[128,128]{1,0:T(8,128)S(1)}, f32[128,128]{1,0:T(8,128)S(1)}, u32[]{:S(2)}, u32[]{:S(2)}) collective-permute-start(f32[128,128]{1,0:T(8,128)S(1)} %get-tuple-element.37), channel_id=1, source_target_pairs={{0,6},{1,3},{2,4},{3,1},{4,2},{5,7},{6,0},{7,5},{8,14},{9,11},{10,... | collective-permute-start | bytes 196616 | tf_op jit(solution)/shard_map/ppermute | solution.py:252
  10.3 5.7 %collective-permute-start.3 = (f32[128,128]{1,0:T(8,128)S(1)}, f32[128,128]{1,0:T(8,128)S(1)}, u32[]{:S(2)}, u32[]{:S(2)}) collective-permute-start(f32[128,128]{1,0:T(8,128)S(1)} %get-tuple-element.36), channel_id=1, source_target_pairs={{0,2},{1,7},{2,0},{3,5},{4,6},{5,3},{6,4},{7,1},{8,10},{9,15},{10,... | collective-permute-start | bytes 196616 | tf_op jit(solution)/shard_map/ppermute | solution.py:252
  16.0 6.6 %collective-permute-start.4 = (f32[128,128]{1,0:T(8,128)S(1)}, f32[128,128]{1,0:T(8,128)S(1)}, u32[]{:S(2)}, u32[]{:S(2)}) collective-permute-start(f32[128,128]{1,0:T(8,128)S(1)} %fusion.5.refs_0_), channel_id=1, source_target_pairs={{0,8},{8,0},{16,24},{24,16},{1,9},{9,1},{17,25},{25,17},{2,10},{10... | collective-permute-start | bytes 196616 | tf_op jit(solution)/shard_map/ppermute | solution.py:236
  17.6 5.0 %collective-permute-start.5 = (f32[128,128]{1,0:T(8,128)S(1)}, f32[128,128]{1,0:T(8,128)S(1)}, u32[]{:S(2)}, u32[]{:S(2)}) collective-permute-start(f32[128,128]{1,0:T(8,128)S(1)} %fusion.5.refs_0_), channel_id=1, source_target_pairs={{0,16},{8,24},{16,0},{24,8},{1,17},{9,25},{17,1},{25,9},{2,18},{10... | collective-permute-start | bytes 196616 | tf_op jit(solution)/shard_map/ppermute | solution.py:236
  19.2 5.2 %collective-permute-start.6 = (f32[128,128]{1,0:T(8,128)S(1)}, f32[128,128]{1,0:T(8,128)S(1)}, u32[]{:S(2)}, u32[]{:S(2)}) collective-permute-start(f32[128,128]{1,0:T(8,128)S(1)} %fusion.5.refs_0_), channel_id=1, source_target_pairs={{0,24},{8,16},{16,8},{24,0},{1,25},{9,17},{17,9},{25,1},{2,26},{10... | collective-permute-start | bytes 196616 | tf_op jit(solution)/shard_map/ppermute | solution.py:236
  24.8 1.6 %collective-permute-start.7 = (f32[512,128]{1,0:T(8,128)S(1)}, f32[512,128]{1,0:T(8,128)S(1)}, u32[]{:S(2)}, u32[]{:S(2)}) collective-permute-start(f32[512,128]{1,0:T(8,128)S(1)} %product.5), channel_id=1, source_target_pairs={{0,1},{1,0},{2,3},{3,2},{4,5},{5,4},{6,7},{7,6},{8,9},{9,8},{10,11... | collective-permute-start | bytes 786440 | tf_op jit(solution)/shard_map/ppermute | solution.py:236
  26.5 4.5 %collective-permute-start.10 = (f32[128,128]{1,0:T(8,128)S(1)}, f32[128,128]{1,0:T(8,128)S(1)}, u32[]{:S(2)}, u32[]{:S(2)}) collective-permute-start(f32[128,128]{1,0:T(8,128)S(1)} %get-tuple-element.33), channel_id=1, source_target_pairs={{0,2},{1,7},{2,0},{3,5},{4,6},{5,3},{6,4},{7,1},{8,10},{9,15},{10,... | collective-permute-start | bytes 196616 | tf_op jit(solution)/shard_map/ppermute | solution.py:252
  27.3 8.1 %collective-permute-start.8 = (f32[128,128]{1,0:T(8,128)S(1)}, f32[128,128]{1,0:T(8,128)S(1)}, u32[]{:S(2)}, u32[]{:S(2)}) collective-permute-start(f32[128,128]{1,0:T(8,128)S(1)} %get-tuple-element.32), channel_id=1, source_target_pairs={{0,4},{1,5},{2,6},{3,7},{4,0},{5,1},{6,2},{7,3},{8,12},{9,13},{10,... | collective-permute-start | bytes 196616 | tf_op jit(solution)/shard_map/ppermute | solution.py:252
  29.1 6.2 %collective-permute-start.9 = (f32[128,128]{1,0:T(8,128)S(1)}, f32[128,128]{1,0:T(8,128)S(1)}, u32[]{:S(2)}, u32[]{:S(2)}) collective-permute-start(f32[128,128]{1,0:T(8,128)S(1)} %get-tuple-element.34), channel_id=1, source_target_pairs={{0,6},{1,3},{2,4},{3,1},{4,2},{5,7},{6,0},{7,5},{8,14},{9,11},{10,... | collective-permute-start | bytes 196616 | tf_op jit(solution)/shard_map/ppermute | solution.py:252
  35.4 7.0 %collective-permute-start.11 = (f32[128,128]{1,0:T(8,128)S(1)}, f32[128,128]{1,0:T(8,128)S(1)}, u32[]{:S(2)}, u32[]{:S(2)}) collective-permute-start(f32[128,128]{1,0:T(8,128)S(1)} %fusion.3.refs_0_), channel_id=1, source_target_pairs={{0,8},{8,0},{16,24},{24,16},{1,9},{9,1},{17,25},{25,17},{2,10},{10... | collective-permute-start | bytes 196616 | tf_op jit(solution)/shard_map/ppermute | solution.py:236
  36.3 6.1 %collective-permute-start.12 = (f32[128,128]{1,0:T(8,128)S(1)}, f32[128,128]{1,0:T(8,128)S(1)}, u32[]{:S(2)}, u32[]{:S(2)}) collective-permute-start(f32[128,128]{1,0:T(8,128)S(1)} %fusion.3.refs_0_), channel_id=1, source_target_pairs={{0,16},{8,24},{16,0},{24,8},{1,17},{9,25},{17,1},{25,9},{2,18},{10... | collective-permute-start | bytes 196616 | tf_op jit(solution)/shard_map/ppermute | solution.py:236
  37.7 5.2 %collective-permute-start.13 = (f32[128,128]{1,0:T(8,128)S(1)}, f32[128,128]{1,0:T(8,128)S(1)}, u32[]{:S(2)}, u32[]{:S(2)}) collective-permute-start(f32[128,128]{1,0:T(8,128)S(1)} %fusion.3.refs_0_), channel_id=1, source_target_pairs={{0,24},{8,16},{16,8},{24,0},{1,25},{9,17},{17,9},{25,1},{2,26},{10... | collective-permute-start | bytes 196616 | tf_op jit(solution)/shard_map/ppermute | solution.py:236
  43.3 1.6 %collective-permute-start.14 = (f32[512,128]{1,0:T(8,128)S(1)}, f32[512,128]{1,0:T(8,128)S(1)}, u32[]{:S(2)}, u32[]{:S(2)}) collective-permute-start(f32[512,128]{1,0:T(8,128)S(1)} %product.7), channel_id=1, source_target_pairs={{0,1},{1,0},{2,3},{3,2},{4,5},{5,4},{6,7},{7,6},{8,9},{9,8},{10,11... | collective-permute-start | bytes 786440 | tf_op jit(solution)/shard_map/ppermute | solution.py:236
  45.0 8.4 %collective-permute-start.15 = (f32[128,128]{1,0:T(8,128)S(1)}, f32[128,128]{1,0:T(8,128)S(1)}, u32[]{:S(2)}, u32[]{:S(2)}) collective-permute-start(f32[128,128]{1,0:T(8,128)S(1)} %get-tuple-element.29), channel_id=1, source_target_pairs={{0,4},{1,5},{2,6},{3,7},{4,0},{5,1},{6,2},{7,3},{8,12},{9,13},{10,... | collective-permute-start | bytes 196616 | tf_op jit(solution)/shard_map/ppermute | solution.py:252
  46.6 6.8 %collective-permute-start.16 = (f32[128,128]{1,0:T(8,128)S(1)}, f32[128,128]{1,0:T(8,128)S(1)}, u32[]{:S(2)}, u32[]{:S(2)}) collective-permute-start(f32[128,128]{1,0:T(8,128)S(1)} %get-tuple-element.31), channel_id=1, source_target_pairs={{0,6},{1,3},{2,4},{3,1},{4,2},{5,7},{6,0},{7,5},{8,14},{9,11},{10,... | collective-permute-start | bytes 196616 | tf_op jit(solution)/shard_map/ppermute | solution.py:252
  48.3 5.4 %collective-permute-start.17 = (f32[128,128]{1,0:T(8,128)S(1)}, f32[128,128]{1,0:T(8,128)S(1)}, u32[]{:S(2)}, u32[]{:S(2)}) collective-permute-start(f32[128,128]{1,0:T(8,128)S(1)} %get-tuple-element.30), channel_id=1, source_target_pairs={{0,2},{1,7},{2,0},{3,5},{4,6},{5,3},{6,4},{7,1},{8,10},{9,15},{10,... | collective-permute-start | bytes 196616 | tf_op jit(solution)/shard_map/ppermute | solution.py:252

commit v5 on v4

--- a/solution.py
+++ b/solution.py
@@ -18,7 +18,7 @@
 
 
 def visits(chips):
-    return [0, *range(2, chips), 1], [0, 2, 1, *range(3, chips)]
+    return [*range(2, chips), 1, 0], [2, 1, *range(3, chips), 0]
 
 
 def place_tiles(step, in_pairs, chain, counts, coords, tiles, buf, coord_buf, spots, sems, acc):
@@ -95,28 +95,27 @@
             high[span], low[span] = split(acc[block] + pltpu.roll(acc[blocks + block], TILE, 1))
 
 
-def one_hot_product(acc, states, in_pairs, away, high, low, out):
-    for chip in range(out.shape[0] // ROWS_DEV):
-        span = pl.ds(chip * ROWS_DEV, ROWS_DEV)
-        block_rows(acc, in_pairs, (2 * chip + away) * BLOCKS_DEV, high, low, chip * ROWS_DEV)
+def one_hot_product(acc, states, in_pairs, turn, away, high, low, out):
+    for n in range(out.shape[0] // ROWS_DEV):
+        span = pl.ds(n * ROWS_DEV, ROWS_DEV)
+        block_rows(acc, in_pairs, (2 * (turn + n) + away) * BLOCKS_DEV, high, low, n * ROWS_DEV)
         out[span] = jnp.dot(high[span], states[...], preferred_element_type=jnp.float32) + jnp.dot(
             low[span], states[...], preferred_element_type=jnp.float32)
 
 
-def first_send_kernel(in_pairs, chain, counts, seeds, coords, tiles, send, acc, states,
-                      buf, coord_buf, spots, sems, high, low):
-    cols = send.shape[0] // ROWS_DEV * 2
+def first_kernel(in_pairs, cols, chain, counts, seeds, coords, tiles, send, acc, states,
+                 buf, coord_buf, spots, sems, high, low):
     block = seeds[...] // ROWS_DEV
     target = ((block // cols) ^ lax.axis_index("row")) * ROWS_DEV + seeds[...] % ROWS_DEV
     target = jnp.where(block % cols == lax.axis_index("col"), target, -1)
     entity = lax.broadcasted_iota(jnp.int32, states.shape, 0)
     states[...] = (entity == target).astype(jnp.float32).astype(jnp.bfloat16)
     place_tiles(0, in_pairs, chain, counts, coords, tiles, buf, coord_buf, spots, sems, acc)
-    one_hot_product(acc, states, in_pairs, 1, high, low, send)
-
-
-def first_keep_kernel(in_pairs, acc, states, keep, high, low):
-    one_hot_product(acc, states, in_pairs, 0, high, low, keep)
+    one_hot_product(acc, states, in_pairs, 0, 1, high, low, send)
+
+
+def one_hot_kernel(in_pairs, turn, away, acc, states, out, high, low):
+    one_hot_product(acc, states, in_pairs, turn, away, high, low, out)
 
 
 def dense_kernel(step, in_pairs, chain, counts, coords, tiles, keep_high, keep_low, send_high, send_low,
@@ -130,15 +129,24 @@
         block_rows(acc, in_pairs, (2 * chip + 1) * BLOCKS_DEV, send_high, send_low, at)
 
 
-def product_kernel(parts, high, low, *refs):
-    pieces, (out, weights) = refs[:parts], refs[parts:]
+def multiply(high, low, weights, start, out):
+    span = pl.ds(start, out.shape[0])
+    both = jnp.dot(high[span], weights[...], preferred_element_type=jnp.float32)
+    rest = jnp.dot(low[span], weights[:, :QUERIES], preferred_element_type=jnp.float32)
+    out[...] = both[:, :QUERIES] + (both[:, QUERIES:] + rest)
+
+
+def leading_kernel(high, low, *refs):
+    pieces, (out, weights) = refs[:-2], refs[-2:]
     for k, piece in enumerate(pieces):
         above, below = split(piece[...])
         weights[k * ROWS_DEV:(k + 1) * ROWS_DEV, :QUERIES] = above
         weights[k * ROWS_DEV:(k + 1) * ROWS_DEV, QUERIES:] = below
-    both = jnp.dot(high[...], weights[...], preferred_element_type=jnp.float32)
-    rest = jnp.dot(low[...], weights[:, :QUERIES], preferred_element_type=jnp.float32)
-    out[...] = both[:, :QUERIES] + (both[:, QUERIES:] + rest)
+    multiply(high, low, weights, 0, out)
+
+
+def product_kernel(start, high, low, weights, out):
+    multiply(high, low, weights, start, out)
 
 
 def shards(tiles, tile_coords, tile_count, seeds, chain):
@@ -169,7 +177,9 @@
     ]
     sums = pltpu.VMEM((2 * out_blocks * in_pairs, TILE, LANES), f32)
     half = pltpu.VMEM((rows_out, rows_in), bf16)
-    partial = pltpu.VMEM((rows_out, QUERIES), f32)
+    lead = pltpu.VMEM((ROWS_DEV, QUERIES), f32)
+    rest = pltpu.VMEM((rows_out - ROWS_DEV, QUERIES), f32)
+    halved = pltpu.VMEM((rows_in, 2 * QUERIES), bf16)
     one_hot = pltpu.VMEM((rows_in, QUERIES), bf16)
 
     def limit(size):
@@ -186,27 +196,28 @@
 
     given = [remain(x) for x in (chain, tile_count, seeds, coords, tiles)]
 
-    def first_send():
-        return pl.pallas_call(
-            functools.partial(first_send_kernel, in_pairs),
-            out_shape=[partial, sums, one_hot],
+    def first():
+        return pl.pallas_call(
+            functools.partial(first_kernel, in_pairs, col_total),
+            out_shape=[lead, sums, one_hot],
             in_specs=[smem, smem, vmem, hbm, hbm],
             out_specs=[vmem] * 3,
-            scratch_shapes=work + [half] * 2,
+            scratch_shapes=work + [pltpu.VMEM((ROWS_DEV, rows_in), bf16)] * 2,
             compiler_params=limit(tile_bytes + dense_bytes // 2),
-            name="first_send",
+            name="first",
         )(*given)
 
-    def first_keep(acc, states):
-        return pl.pallas_call(
-            functools.partial(first_keep_kernel, in_pairs),
-            out_shape=partial,
+    def one_hot_part(acc, states, away, shape):
+        turn = 0 if shape is lead else 1
+        return pl.pallas_call(
+            functools.partial(one_hot_kernel, in_pairs, turn, away),
+            out_shape=shape,
             in_specs=[vmem] * 2,
             out_specs=vmem,
-            scratch_shapes=[half] * 2,
+            scratch_shapes=[pltpu.VMEM((shape.shape[0], rows_in), bf16)] * 2,
             compiler_params=limit(dense_bytes // 2),
-            cost_estimate=cost(4 * rows_out * rows_in * QUERIES),
-            name="first_keep",
+            cost_estimate=cost(4 * shape.shape[0] * rows_in * QUERIES),
+            name="one_hot_part",
         )(local(acc), local(states))
 
     def densify(step):
@@ -220,42 +231,62 @@
             cost_estimate=pl.CostEstimate(flops=0, bytes_accessed=8 << 20, transcendentals=0),
         )(*given[:2], *given[3:])
 
-    def product(high, low, pieces):
-        return pl.pallas_call(
-            functools.partial(product_kernel, len(pieces)),
-            out_shape=partial,
+    def leading(high, low, pieces):
+        return pl.pallas_call(
+            leading_kernel,
+            out_shape=[lead, halved],
             in_specs=[vmem] * (2 + len(pieces)),
+            out_specs=[vmem] * 2,
+            compiler_params=limit(4 << 20),
+            cost_estimate=cost(6 * ROWS_DEV * rows_in * QUERIES),
+            name="leading",
+        )(local(high), local(low), *map(local, pieces))
+
+    def product(high, low, weights, shape):
+        return pl.pallas_call(
+            functools.partial(product_kernel, 0 if shape is lead else ROWS_DEV),
+            out_shape=shape,
+            in_specs=[vmem] * 3,
             out_specs=vmem,
-            scratch_shapes=[pltpu.VMEM((rows_in, 2 * QUERIES), bf16)],
             compiler_params=limit(4 << 20),
-            cost_estimate=cost(6 * rows_out * rows_in * QUERIES),
+            cost_estimate=cost(6 * shape.shape[0] * rows_in * QUERIES),
             name="product",
-        )(local(high), local(low), *map(local, pieces))
+        )(local(high), local(low), local(weights))
 
     def swap(x, axis, size, flip):
         return lax.ppermute(x, axis, [(i, i ^ flip) for i in range(size)])
 
+    def kept(away, shape):
+        if step == 0:
+            return one_hot_part(acc, states, away, shape)
+        return product(*relation[2 * away:2 * away + 2], weights, shape)
+
     for step in range(HOPS):
         if step == 0:
-            send, acc, states = first_send()
+            send, acc, states = first()
         else:
-            send = product(*relation[2:], pieces)
-        crossing = swap(send, "col", col_total, 1)
-        keep = first_keep(acc, states) if step == 0 else product(*relation[:2], pieces)
-        summed = keep + crossing
+            send, weights = leading(*relation[2:], pieces)
+        crossing = [swap(send, "col", col_total, 1)]
+        send = kept(1, rest)
+        crossing.append(swap(send, "col", col_total, 1))
+        head = kept(0, lead) + crossing[0]
+        tail = kept(0, rest) + crossing[1]
         arrived = []
         for turn, flips in enumerate(zip(*visits(depth_total))):
-            if turn:
-                pairs_there = [(2 * z + core, 2 * (z ^ flips[core]) + core)
-                               for z in range(depth_total) for core in range(2)]
-                arrived.append(
-                    lax.ppermute(summed[turn * ROWS_DEV:(turn + 1) * ROWS_DEV], "col", pairs_there))
+            part = tail[(turn - 1) * ROWS_DEV:turn * ROWS_DEV] if turn else head
+            if turn == depth_total - 1:
+                arrived.append(part)
+                continue
+            there = [(2 * z + core, 2 * (z ^ flips[core]) + core)
+                     for z in range(depth_total) for core in range(2)]
+            arrived.append(lax.ppermute(part, "col", there))
         if step + 1 < HOPS:
-            relation = densify(step + 1)
-        owned = summed[:ROWS_DEV]
-        for part in arrived:
+            following = densify(step + 1)
+        owned = arrived[-1]
+        for part in arrived[:-1]:
             owned = owned + part
         if step + 1 < HOPS:
+            relation = following
             pieces = [owned] + [swap(owned, "row", row_total, k) for k in range(1, row_total)]
 
     squares = jnp.sum(owned * owned, axis=0, keepdims=True)

time: 65.2 us -> 65.6 us (level)
  waiting for transfers between devices: 20.3 us -> 19.2 us
  Pallas kernels: 12.1 us -> 13 us
    ppermute x9 -> x12, waiting for transfers between devices: 5.06 us -> 2.87 us  [swap(): return lax.ppermute(x, axis, [(i, i ^ flip) for i in range(size)])]
    ppermute x9 -> x12, starting transfers between devices: 7.51 us -> 8.82 us  [swap(): return lax.ppermute(x, axis, [(i, i ^ flip) for i in range(size)])]
    ppermute x9, waiting for transfers between devices: 15.3 us -> 16.4 us  [shards(): arrived.append(lax.ppermute(part, 'col', there))]
    pallas_call x6 -> x12, Pallas kernels: 5.65 us -> 6.6 us  [the longest x1 2.92 us: first(): pl.pallas_call(functools.partial(first_kernel, in_pairs, col_total), out_...]
    ppermute x9, starting transfers between devices: 13.5 us -> 12.8 us  [shards(): arrived.append(lax.ppermute(part, 'col', there))]
  transfers between devices with their start and end apart: 18 -> 21, of which waited for: 11 -> 13; matrix products, arithmetic and copies ran while one was open for 0% -> 0% of each run, Pallas kernels for 12% -> 13%
where the time goes in v5:
time: 65.6 us; the launch traced here: 65.3 us
  starting transfers between devices  21.6 us (33%)
  waiting for transfers between devices  19.2 us (29%)
  Pallas kernels  13 us (20%)
  blocking collectives  10.4 us (16%)
  other arithmetic  0.84 us (1%)
    ppermute x9, waiting for transfers between devices, shards(): arrived.append(lax.ppermute(part, 'col', there))  16.4 us
    ppermute x9, starting transfers between devices, shards(): arrived.append(lax.ppermute(part, 'col', there))  12.8 us
    all_to_all x1, blocking collectives, shards(): lax.all_to_all(jnp.broadcast_to(squares, (devices, QUERIES)), ('row', 'co...  10.4 us
    ppermute x12, starting transfers between devices, swap(): return lax.ppermute(x, axis, [(i, i ^ flip) for i in range(size)])  8.82 us
    pallas_call x2, Pallas kernels, densify(): pl.pallas_call(functools.partial(dense_kernel, step, in_pairs), out_shape...  6.41 us
    pallas_call x1, Pallas kernels, first(): pl.pallas_call(functools.partial(first_kernel, in_pairs, col_total), out_...  2.92 us
    ppermute x12, waiting for transfers between devices, swap(): return lax.ppermute(x, axis, [(i, i ^ flip) for i in range(size)])  2.87 us
    pallas_call x6, Pallas kernels, product(): pl.pallas_call(functools.partial(product_kernel, 0 if shape is lead else...  1.92 us
  transfers between devices with their start and end apart: 21, of which 13 were waited for; matrix products, arithmetic and copies ran while one was open for 0% of the time, Pallas kernels for 13%

profile of v5, /device:TPU:0, one launch (start us, length us, event | category | flops | bytes accessed | tf_op | source)
XLA Modules:
  0.0 65.3 jit_solution(338056564148785147)
XLA Ops:
  0.0 2.9 %first.1 = (f32[128,128]{1,0:T(8,128)S(1)}, f32[128,64,128]{2,1,0:T(8,128)S(1)}, bf16[512,128]{1,0:T(8,128)(2,1)S(1)}) custom-call(s32[3]{0:T(128)} %chain.5, s32[1,1,3]{2,1,0:T(1,128)} %counts.5, s32[1,128]{1,0:T(1,128)} %bitcast.11, s32[3,2,256]{2,1,0:T(2,128)} %bitcast.8, f32[3,128,64,128]{3,2,1,0:T(8,128)} %bitcast.4), custom_call_target="tpu_custom_call" | custom-call | tf_op jit(solution)/shard_map/first/pallas_call | solution.py:200
  5.0 4.3 %collective-permute-start.2 = (f32[128,128]{1,0:T(8,128)S(1)}, f32[128,128]{1,0:T(8,128)S(1)}, u32[]{:S(2)}, u32[]{:S(2)}) collective-permute-start(f32[128,128]{1,0:T(8,128)S(1)} %add.56), channel_id=1, source_target_pairs={{0,4},{1,5},{2,6},{3,7},{4,0},{5,1},{6,2},{7,3},{8,12},{9,13},{10,... | collective-permute-start | bytes 196616 | tf_op jit(solution)/shard_map/ppermute | solution.py:282
  9.3 1.3 %collective-permute-start.3 = (f32[128,128]{1,0:T(8,128)S(1)}, f32[128,128]{1,0:T(8,128)S(1)}, u32[]{:S(2)}, u32[]{:S(2)}) collective-permute-start(f32[128,128]{1,0:T(8,128)S(1)} %get-tuple-element.41), channel_id=1, source_target_pairs={{0,6},{1,3},{2,4},{3,1},{4,2},{5,7},{6,0},{7,5},{8,14},{9,11},{10,... | collective-permute-start | bytes 196616 | tf_op jit(solution)/shard_map/ppermute | solution.py:282
  10.6 2.4 %collective-permute-done.2 = f32[128,128]{1,0:T(8,128)S(1)} collective-permute-done((f32[128,128]{1,0:T(8,128)S(1)}, f32[128,128]{1,0:T(8,128)S(1)}, u32[]{:S(2)}, u32[]{:S(2)}) %collective-permute-start.2) | collective-permute-done | bytes 65568 | tf_op jit(solution)/shard_map/ppermute | solution.py:282
  13.0 2.9 %collective-permute-done.3 = f32[128,128]{1,0:T(8,128)S(1)} collective-permute-done((f32[128,128]{1,0:T(8,128)S(1)}, f32[128,128]{1,0:T(8,128)S(1)}, u32[]{:S(2)}, u32[]{:S(2)}) %collective-permute-start.3) | collective-permute-done | bytes 65568 | tf_op jit(solution)/shard_map/ppermute | solution.py:282
  16.3 1.7 %collective-permute-start.5 = (f32[128,128]{1,0:T(8,128)S(1)}, f32[128,128]{1,0:T(8,128)S(1)}, u32[]{:S(2)}, u32[]{:S(2)}) collective-permute-start(f32[128,128]{1,0:T(8,128)S(1)} %fusion.5.refs_0_), channel_id=1, source_target_pairs={{0,8},{8,0},{16,24},{24,16},{1,9},{9,1},{17,25},{25,17},{2,10},{10... | collective-permute-start | bytes 196616 | tf_op jit(solution)/shard_map/ppermute | solution.py:257
  18.0 1.5 %collective-permute-start.6 = (f32[128,128]{1,0:T(8,128)S(1)}, f32[128,128]{1,0:T(8,128)S(1)}, u32[]{:S(2)}, u32[]{:S(2)}) collective-permute-start(f32[128,128]{1,0:T(8,128)S(1)} %fusion.5.refs_0_), channel_id=1, source_target_pairs={{0,16},{8,24},{16,0},{24,8},{1,17},{9,25},{17,1},{25,9},{2,18},{10... | collective-permute-start | bytes 196616 | tf_op jit(solution)/shard_map/ppermute | solution.py:257
  19.9 3.0 %shard_map.56 = (bf16[512,512]{1,0:T(8,128)(2,1)S(1)}, bf16[512,512]{1,0:T(8,128)(2,1)S(1)}, bf16[512,512]{1,0:T(8,128)(2,1)S(1)}, bf16[512,512]{1,0:T(8,128)(2,1)S(1)}) custom-call(s32[3]{0:T(128)} %chain.5, s32[1,1,3]{2,1,0:T(1,128)} %counts.5, s32[3,2,256]{2,1,0:T(2,128)} %bitcast.9, f32[3,128,64,128]{3,2,1,0:T(8,128)} %bitcast.5), custom_call_target="tpu_custom_call" | custom-call | bytes 8388608 | tf_op jit(solution)/shard_map/pallas_call | solution.py:224
  23.0 1.7 %collective-permute-done.7.refs_3_ = f32[128,128]{1,0:T(8,128)S(1)} collective-permute-done((f32[128,128]{1,0:T(8,128)S(1)}, f32[128,128]{1,0:T(8,128)S(1)}, u32[]{:S(2)}, u32[]{:S(2)}) %collective-permute-start.7) | collective-permute-done | bytes 65568 | tf_op jit(solution)/shard_map/ppermute | solution.py:257
  25.4 0.5 collective-permute-start.9
  26.9 1.8 %collective-permute-start.10 = (f32[128,128]{1,0:T(8,128)S(1)}, f32[128,128]{1,0:T(8,128)S(1)}, u32[]{:S(2)}, u32[]{:S(2)}) collective-permute-start(f32[128,128]{1,0:T(8,128)S(1)} %add.61), channel_id=1, source_target_pairs={{0,4},{1,5},{2,6},{3,7},{4,0},{5,1},{6,2},{7,3},{8,12},{9,13},{10,... | collective-permute-start | bytes 196616 | tf_op jit(solution)/shard_map/ppermute | solution.py:282
  28.7 1.4 %collective-permute-start.11 = (f32[128,128]{1,0:T(8,128)S(1)}, f32[128,128]{1,0:T(8,128)S(1)}, u32[]{:S(2)}, u32[]{:S(2)}) collective-permute-start(f32[128,128]{1,0:T(8,128)S(1)} %get-tuple-element.39), channel_id=1, source_target_pairs={{0,6},{1,3},{2,4},{3,1},{4,2},{5,7},{6,0},{7,5},{8,14},{9,11},{10,... | collective-permute-start | bytes 196616 | tf_op jit(solution)/shard_map/ppermute | solution.py:282
  30.6 3.1 %collective-permute-done.10 = f32[128,128]{1,0:T(8,128)S(1)} collective-permute-done((f32[128,128]{1,0:T(8,128)S(1)}, f32[128,128]{1,0:T(8,128)S(1)}, u32[]{:S(2)}, u32[]{:S(2)}) %collective-permute-start.10) | collective-permute-done | bytes 65568 | tf_op jit(solution)/shard_map/ppermute | solution.py:282
  33.7 1.5 %collective-permute-done.11 = f32[128,128]{1,0:T(8,128)S(1)} collective-permute-done((f32[128,128]{1,0:T(8,128)S(1)}, f32[128,128]{1,0:T(8,128)S(1)}, u32[]{:S(2)}, u32[]{:S(2)}) %collective-permute-start.11) | collective-permute-done | bytes 65568 | tf_op jit(solution)/shard_map/ppermute | solution.py:282
  35.2 0.6 collective-permute-done.12
  35.8 1.1 %collective-permute-start.13 = (f32[128,128]{1,0:T(8,128)S(1)}, f32[128,128]{1,0:T(8,128)S(1)}, u32[]{:S(2)}, u32[]{:S(2)}) collective-permute-start(f32[128,128]{1,0:T(8,128)S(1)} %fusion.3.refs_0_), channel_id=1, source_target_pairs={{0,8},{8,0},{16,24},{24,16},{1,9},{9,1},{17,25},{25,17},{2,10},{10... | collective-permute-start | bytes 196616 | tf_op jit(solution)/shard_map/ppermute | solution.py:257
  37.1 2.2 %collective-permute-start.15 = (f32[128,128]{1,0:T(8,128)S(1)}, f32[128,128]{1,0:T(8,128)S(1)}, u32[]{:S(2)}, u32[]{:S(2)}) collective-permute-start(f32[128,128]{1,0:T(8,128)S(1)} %fusion.3.refs_0_), channel_id=1, source_target_pairs={{0,24},{8,16},{16,8},{24,0},{1,25},{9,17},{17,9},{25,1},{2,26},{10... | collective-permute-start | bytes 196616 | tf_op jit(solution)/shard_map/ppermute | solution.py:257
  39.4 3.4 %shard_map.55 = (bf16[512,512]{1,0:T(8,128)(2,1)S(1)}, bf16[512,512]{1,0:T(8,128)(2,1)S(1)}, bf16[512,512]{1,0:T(8,128)(2,1)S(1)}, bf16[512,512]{1,0:T(8,128)(2,1)S(1)}) custom-call(s32[3]{0:T(128)} %chain.5, s32[1,1,3]{2,1,0:T(1,128)} %counts.5, s32[3,2,256]{2,1,0:T(2,128)} %bitcast.10, f32[3,128,64,128]{3,2,1,0:T(8,128)} %bitcast.6), custom_call_target="tpu_custom_call" | custom-call | bytes 8388608 | tf_op jit(solution)/shard_map/pallas_call | solution.py:224
  45.1 2.0 %collective-permute-start.18 = (f32[128,128]{1,0:T(8,128)S(1)}, f32[128,128]{1,0:T(8,128)S(1)}, u32[]{:S(2)}, u32[]{:S(2)}) collective-permute-start(f32[128,128]{1,0:T(8,128)S(1)} %add.66), channel_id=1, source_target_pairs={{0,4},{1,5},{2,6},{3,7},{4,0},{5,1},{6,2},{7,3},{8,12},{9,13},{10,... | collective-permute-start | bytes 196616 | tf_op jit(solution)/shard_map/ppermute | solution.py:282
  47.1 1.6 %collective-permute-start.19 = (f32[128,128]{1,0:T(8,128)S(1)}, f32[128,128]{1,0:T(8,128)S(1)}, u32[]{:S(2)}, u32[]{:S(2)}) collective-permute-start(f32[128,128]{1,0:T(8,128)S(1)} %get-tuple-element.37), channel_id=1, source_target_pairs={{0,6},{1,3},{2,4},{3,1},{4,2},{5,7},{6,0},{7,5},{8,14},{9,11},{10,... | collective-permute-start | bytes 196616 | tf_op jit(solution)/shard_map/ppermute | solution.py:282
  48.7 4.9 %collective-permute-done.18 = f32[128,128]{1,0:T(8,128)S(1)} collective-permute-done((f32[128,128]{1,0:T(8,128)S(1)}, f32[128,128]{1,0:T(8,128)S(1)}, u32[]{:S(2)}, u32[]{:S(2)}) %collective-permute-start.18) | collective-permute-done | bytes 65568 | tf_op jit(solution)/shard_map/ppermute | solution.py:282
  53.6 0.6 collective-permute-done.20
  54.3 10.4 %all_to_all.6 = f32[32,1,128]{2,1,0:T(1,128)S(1)} all-to-all(f32[32,1,128]{2,1,0:T(1,128)S(1)} %broadcast_in_dim.5), channel_id=1, replica_groups=mesh['row'=4,'col'=8] {'row','col'}, dimensions={0} | all-to-all | bytes 32768 | tf_op jit(solution)/shard_map/all_to_all | solution.py:294
  64.7 0.6 broadcast_multiply_fusion
  (49 shorter events, 7.7 us)
Async XLA Ops:
  3.4 5.9 %collective-permute-start = (f32[384,128]{1,0:T(8,128)S(1)}, f32[384,128]{1,0:T(8,128)S(1)}, u32[]{:S(2)}, u32[]{:S(2)}) collective-permute-start(f32[384,128]{1,0:T(8,128)S(1)} %one_hot_part.4), channel_id=1, source_target_pairs={{0,1},{1,0},{2,3},{3,2},{4,5},{5,4},{6,7},{7,6},{8,9},{9,8},{10,11... | collective-permute-start | bytes 589832 | tf_op jit(solution)/shard_map/ppermute | solution.py:257
  3.7 1.3 %collective-permute-start.1 = (f32[128,128]{1,0:T(8,128)S(1)}, f32[128,128]{1,0:T(8,128)S(1)}, u32[]{:S(2)}, u32[]{:S(2)}) collective-permute-start(f32[128,128]{1,0:T(8,128)S(1)} %get-tuple-element.30), channel_id=1, source_target_pairs={{0,1},{1,0},{2,3},{3,2},{4,5},{5,4},{6,7},{7,6},{8,9},{9,8},{10,11... | collective-permute-start | bytes 196616 | tf_op jit(solution)/shard_map/ppermute | solution.py:257
  5.0 8.0 %collective-permute-start.2 = (f32[128,128]{1,0:T(8,128)S(1)}, f32[128,128]{1,0:T(8,128)S(1)}, u32[]{:S(2)}, u32[]{:S(2)}) collective-permute-start(f32[128,128]{1,0:T(8,128)S(1)} %add.56), channel_id=1, source_target_pairs={{0,4},{1,5},{2,6},{3,7},{4,0},{5,1},{6,2},{7,3},{8,12},{9,13},{10,... | collective-permute-start | bytes 196616 | tf_op jit(solution)/shard_map/ppermute | solution.py:282
  9.3 6.6 %collective-permute-start.3 = (f32[128,128]{1,0:T(8,128)S(1)}, f32[128,128]{1,0:T(8,128)S(1)}, u32[]{:S(2)}, u32[]{:S(2)}) collective-permute-start(f32[128,128]{1,0:T(8,128)S(1)} %get-tuple-element.41), channel_id=1, source_target_pairs={{0,6},{1,3},{2,4},{3,1},{4,2},{5,7},{6,0},{7,5},{8,14},{9,11},{10,... | collective-permute-start | bytes 196616 | tf_op jit(solution)/shard_map/ppermute | solution.py:282
  10.6 5.7 %collective-permute-start.4 = (f32[128,128]{1,0:T(8,128)S(1)}, f32[128,128]{1,0:T(8,128)S(1)}, u32[]{:S(2)}, u32[]{:S(2)}) collective-permute-start(f32[128,128]{1,0:T(8,128)S(1)} %get-tuple-element.42), channel_id=1, source_target_pairs={{0,2},{1,7},{2,0},{3,5},{4,6},{5,3},{6,4},{7,1},{8,10},{9,15},{10,... | collective-permute-start | bytes 196616 | tf_op jit(solution)/shard_map/ppermute | solution.py:282
  16.3 6.6 %collective-permute-start.5 = (f32[128,128]{1,0:T(8,128)S(1)}, f32[128,128]{1,0:T(8,128)S(1)}, u32[]{:S(2)}, u32[]{:S(2)}) collective-permute-start(f32[128,128]{1,0:T(8,128)S(1)} %fusion.5.refs_0_), channel_id=1, source_target_pairs={{0,8},{8,0},{16,24},{24,16},{1,9},{9,1},{17,25},{25,17},{2,10},{10... | collective-permute-start | bytes 196616 | tf_op jit(solution)/shard_map/ppermute | solution.py:257
  18.0 5.0 %collective-permute-start.6 = (f32[128,128]{1,0:T(8,128)S(1)}, f32[128,128]{1,0:T(8,128)S(1)}, u32[]{:S(2)}, u32[]{:S(2)}) collective-permute-start(f32[128,128]{1,0:T(8,128)S(1)} %fusion.5.refs_0_), channel_id=1, source_target_pairs={{0,16},{8,24},{16,0},{24,8},{1,17},{9,25},{17,1},{25,9},{2,18},{10... | collective-permute-start | bytes 196616 | tf_op jit(solution)/shard_map/ppermute | solution.py:257
  19.5 5.2 %collective-permute-start.7 = (f32[128,128]{1,0:T(8,128)S(1)}, f32[128,128]{1,0:T(8,128)S(1)}, u32[]{:S(2)}, u32[]{:S(2)}) collective-permute-start(f32[128,128]{1,0:T(8,128)S(1)} %fusion.5.refs_0_), channel_id=1, source_target_pairs={{0,24},{8,16},{16,8},{24,0},{1,25},{9,17},{17,9},{25,1},{2,26},{10... | collective-permute-start | bytes 196616 | tf_op jit(solution)/shard_map/ppermute | solution.py:257
  25.3 3.4 %collective-permute-start.8 = (f32[384,128]{1,0:T(8,128)S(1)}, f32[384,128]{1,0:T(8,128)S(1)}, u32[]{:S(2)}, u32[]{:S(2)}) collective-permute-start(f32[384,128]{1,0:T(8,128)S(1)} %product.7), channel_id=1, source_target_pairs={{0,1},{1,0},{2,3},{3,2},{4,5},{5,4},{6,7},{7,6},{8,9},{9,8},{10,11... | collective-permute-start | bytes 589832 | tf_op jit(solution)/shard_map/ppermute | solution.py:257
  25.4 1.5 %collective-permute-start.9 = (f32[128,128]{1,0:T(8,128)S(1)}, f32[128,128]{1,0:T(8,128)S(1)}, u32[]{:S(2)}, u32[]{:S(2)}) collective-permute-start(f32[128,128]{1,0:T(8,128)S(1)} %get-tuple-element.32), channel_id=1, source_target_pairs={{0,1},{1,0},{2,3},{3,2},{4,5},{5,4},{6,7},{7,6},{8,9},{9,8},{10,11... | collective-permute-start | bytes 196616 | tf_op jit(solution)/shard_map/ppermute | solution.py:257
  26.9 6.8 %collective-permute-start.10 = (f32[128,128]{1,0:T(8,128)S(1)}, f32[128,128]{1,0:T(8,128)S(1)}, u32[]{:S(2)}, u32[]{:S(2)}) collective-permute-start(f32[128,128]{1,0:T(8,128)S(1)} %add.61), channel_id=1, source_target_pairs={{0,4},{1,5},{2,6},{3,7},{4,0},{5,1},{6,2},{7,3},{8,12},{9,13},{10,... | collective-permute-start | bytes 196616 | tf_op jit(solution)/shard_map/ppermute | solution.py:282
  28.7 6.5 %collective-permute-start.11 = (f32[128,128]{1,0:T(8,128)S(1)}, f32[128,128]{1,0:T(8,128)S(1)}, u32[]{:S(2)}, u32[]{:S(2)}) collective-permute-start(f32[128,128]{1,0:T(8,128)S(1)} %get-tuple-element.39), channel_id=1, source_target_pairs={{0,6},{1,3},{2,4},{3,1},{4,2},{5,7},{6,0},{7,5},{8,14},{9,11},{10,... | collective-permute-start | bytes 196616 | tf_op jit(solution)/shard_map/ppermute | solution.py:282
  30.1 5.7 %collective-permute-start.12 = (f32[128,128]{1,0:T(8,128)S(1)}, f32[128,128]{1,0:T(8,128)S(1)}, u32[]{:S(2)}, u32[]{:S(2)}) collective-permute-start(f32[128,128]{1,0:T(8,128)S(1)} %get-tuple-element.40), channel_id=1, source_target_pairs={{0,2},{1,7},{2,0},{3,5},{4,6},{5,3},{6,4},{7,1},{8,10},{9,15},{10,... | collective-permute-start | bytes 196616 | tf_op jit(solution)/shard_map/ppermute | solution.py:282
  35.8 7.0 %collective-permute-start.13 = (f32[128,128]{1,0:T(8,128)S(1)}, f32[128,128]{1,0:T(8,128)S(1)}, u32[]{:S(2)}, u32[]{:S(2)}) collective-permute-start(f32[128,128]{1,0:T(8,128)S(1)} %fusion.3.refs_0_), channel_id=1, source_target_pairs={{0,8},{8,0},{16,24},{24,16},{1,9},{9,1},{17,25},{25,17},{2,10},{10... | collective-permute-start | bytes 196616 | tf_op jit(solution)/shard_map/ppermute | solution.py:257
  36.9 5.9 %collective-permute-start.14 = (f32[128,128]{1,0:T(8,128)S(1)}, f32[128,128]{1,0:T(8,128)S(1)}, u32[]{:S(2)}, u32[]{:S(2)}) collective-permute-start(f32[128,128]{1,0:T(8,128)S(1)} %fusion.3.refs_0_), channel_id=1, source_target_pairs={{0,16},{8,24},{16,0},{24,8},{1,17},{9,25},{17,1},{25,9},{2,18},{10... | collective-permute-start | bytes 196616 | tf_op jit(solution)/shard_map/ppermute | solution.py:257
  37.1 5.7 %collective-permute-start.15 = (f32[128,128]{1,0:T(8,128)S(1)}, f32[128,128]{1,0:T(8,128)S(1)}, u32[]{:S(2)}, u32[]{:S(2)}) collective-permute-start(f32[128,128]{1,0:T(8,128)S(1)} %fusion.3.refs_0_), channel_id=1, source_target_pairs={{0,24},{8,16},{16,8},{24,0},{1,25},{9,17},{17,9},{25,1},{2,26},{10... | collective-permute-start | bytes 196616 | tf_op jit(solution)/shard_map/ppermute | solution.py:257
  43.4 3.6 %collective-permute-start.16 = (f32[384,128]{1,0:T(8,128)S(1)}, f32[384,128]{1,0:T(8,128)S(1)}, u32[]{:S(2)}, u32[]{:S(2)}) collective-permute-start(f32[384,128]{1,0:T(8,128)S(1)} %product.10), channel_id=1, source_target_pairs={{0,1},{1,0},{2,3},{3,2},{4,5},{5,4},{6,7},{7,6},{8,9},{9,8},{10,11... | collective-permute-start | bytes 589832 | tf_op jit(solution)/shard_map/ppermute | solution.py:257
  43.5 1.5 %collective-permute-start.17 = (f32[128,128]{1,0:T(8,128)S(1)}, f32[128,128]{1,0:T(8,128)S(1)}, u32[]{:S(2)}, u32[]{:S(2)}) collective-permute-start(f32[128,128]{1,0:T(8,128)S(1)} %get-tuple-element.34), channel_id=1, source_target_pairs={{0,1},{1,0},{2,3},{3,2},{4,5},{5,4},{6,7},{7,6},{8,9},{9,8},{10,11... | collective-permute-start | bytes 196616 | tf_op jit(solution)/shard_map/ppermute | solution.py:257
  45.1 8.6 %collective-permute-start.18 = (f32[128,128]{1,0:T(8,128)S(1)}, f32[128,128]{1,0:T(8,128)S(1)}, u32[]{:S(2)}, u32[]{:S(2)}) collective-permute-start(f32[128,128]{1,0:T(8,128)S(1)} %add.66), channel_id=1, source_target_pairs={{0,4},{1,5},{2,6},{3,7},{4,0},{5,1},{6,2},{7,3},{8,12},{9,13},{10,... | collective-permute-start | bytes 196616 | tf_op jit(solution)/shard_map/ppermute | solution.py:282
  47.1 6.5 %collective-permute-start.19 = (f32[128,128]{1,0:T(8,128)S(1)}, f32[128,128]{1,0:T(8,128)S(1)}, u32[]{:S(2)}, u32[]{:S(2)}) collective-permute-start(f32[128,128]{1,0:T(8,128)S(1)} %get-tuple-element.37), channel_id=1, source_target_pairs={{0,6},{1,3},{2,4},{3,1},{4,2},{5,7},{6,0},{7,5},{8,14},{9,11},{10,... | collective-permute-start | bytes 196616 | tf_op jit(solution)/shard_map/ppermute | solution.py:282
  48.7 5.5 %collective-permute-start.20 = (f32[128,128]{1,0:T(8,128)S(1)}, f32[128,128]{1,0:T(8,128)S(1)}, u32[]{:S(2)}, u32[]{:S(2)}) collective-permute-start(f32[128,128]{1,0:T(8,128)S(1)} %get-tuple-element.38), channel_id=1, source_target_pairs={{0,2},{1,7},{2,0},{3,5},{4,6},{5,3},{6,4},{7,1},{8,10},{9,15},{10,... | collective-permute-start | bytes 196616 | tf_op jit(solution)/shard_map/ppermute | solution.py:282

commit v6 on v5

--- a/solution.py
+++ b/solution.py
@@ -179,6 +179,7 @@
     half = pltpu.VMEM((rows_out, rows_in), bf16)
     lead = pltpu.VMEM((ROWS_DEV, QUERIES), f32)
     rest = pltpu.VMEM((rows_out - ROWS_DEV, QUERIES), f32)
+    last = pltpu.VMEM((rows_out - 2 * ROWS_DEV, QUERIES), f32)
     halved = pltpu.VMEM((rows_in, 2 * QUERIES), bf16)
     one_hot = pltpu.VMEM((rows_in, QUERIES), bf16)
 
@@ -207,8 +208,7 @@
             name="first",
         )(*given)
 
-    def one_hot_part(acc, states, away, shape):
-        turn = 0 if shape is lead else 1
+    def one_hot_part(acc, states, away, turn, shape):
         return pl.pallas_call(
             functools.partial(one_hot_kernel, in_pairs, turn, away),
             out_shape=shape,
@@ -242,9 +242,9 @@
             name="leading",
         )(local(high), local(low), *map(local, pieces))
 
-    def product(high, low, weights, shape):
-        return pl.pallas_call(
-            functools.partial(product_kernel, 0 if shape is lead else ROWS_DEV),
+    def product(high, low, weights, turn, shape):
+        return pl.pallas_call(
+            functools.partial(product_kernel, turn * ROWS_DEV),
             out_shape=shape,
             in_specs=[vmem] * 3,
             out_specs=vmem,
@@ -256,10 +256,10 @@
     def swap(x, axis, size, flip):
         return lax.ppermute(x, axis, [(i, i ^ flip) for i in range(size)])
 
-    def kept(away, shape):
+    def blocks_from(turn, away, shape):
         if step == 0:
-            return one_hot_part(acc, states, away, shape)
-        return product(*relation[2 * away:2 * away + 2], weights, shape)
+            return one_hot_part(acc, states, away, turn, shape)
+        return product(*relation[2 * away:2 * away + 2], weights, turn, shape)
 
     for step in range(HOPS):
         if step == 0:
@@ -267,13 +267,16 @@
         else:
             send, weights = leading(*relation[2:], pieces)
         crossing = [swap(send, "col", col_total, 1)]
-        send = kept(1, rest)
+        send = blocks_from(1, 1, rest)
         crossing.append(swap(send, "col", col_total, 1))
-        head = kept(0, lead) + crossing[0]
-        tail = kept(0, rest) + crossing[1]
+        ready = [blocks_from(0, 0, lead) + crossing[0]]
+        ready.append(blocks_from(1, 0, lead) + crossing[1][:ROWS_DEV])
+        if depth_total > 2:
+            tail = blocks_from(2, 0, last) + crossing[1][ROWS_DEV:]
+            ready += [tail[k * ROWS_DEV:(k + 1) * ROWS_DEV] for k in range(depth_total - 2)]
         arrived = []
         for turn, flips in enumerate(zip(*visits(depth_total))):
-            part = tail[(turn - 1) * ROWS_DEV:turn * ROWS_DEV] if turn else head
+            part = ready[turn]
             if turn == depth_total - 1:
                 arrived.append(part)
                 continue

time: 65.6 us -> 65.3 us (level)
  waiting for transfers between devices: 19.2 us -> 18.1 us
    pallas_call x6 -> x8, Pallas kernels: 1.92 us -> 2.23 us  [product(): pl.pallas_call(functools.partial(product_kernel, turn * ROWS_DEV), out_sh...]
    pallas_call x3 -> x4, Pallas kernels: 1.28 us -> 1.52 us  [one_hot_part(): pl.pallas_call(functools.partial(one_hot_kernel, in_pairs, turn, away), o...]
  transfers between devices with their start and end apart: 21 -> 21, of which waited for: 13 -> 12; matrix products, arithmetic and copies ran while one was open for 0% -> 0% of each run, Pallas kernels for 13% -> 14%
where the time goes in v6:
time: 65.3 us; the launch traced here: 65.1 us
  starting transfers between devices  22 us (34%)
  waiting for transfers between devices  18.1 us (28%)
  Pallas kernels  13.6 us (21%)
  blocking collectives  10.3 us (16%)
  other arithmetic  0.86 us (1%)
    ppermute x9, waiting for transfers between devices, shards(): arrived.append(lax.ppermute(part, 'col', there))  15.7 us
    ppermute x9, starting transfers between devices, shards(): arrived.append(lax.ppermute(part, 'col', there))  13.2 us
    all_to_all x1, blocking collectives, shards(): lax.all_to_all(jnp.broadcast_to(squares, (devices, QUERIES)), ('row', 'co...  10.3 us
    ppermute x12, starting transfers between devices, swap(): return lax.ppermute(x, axis, [(i, i ^ flip) for i in range(size)])  8.82 us
    pallas_call x2, Pallas kernels, densify(): pl.pallas_call(functools.partial(dense_kernel, step, in_pairs), out_shape...  6.41 us
    pallas_call x1, Pallas kernels, first(): pl.pallas_call(functools.partial(first_kernel, in_pairs, col_total), out_...  2.92 us
    ppermute x12, waiting for transfers between devices, swap(): return lax.ppermute(x, axis, [(i, i ^ flip) for i in range(size)])  2.38 us
    pallas_call x8, Pallas kernels, product(): pl.pallas_call(functools.partial(product_kernel, turn * ROWS_DEV), out_sh...  2.23 us
  transfers between devices with their start and end apart: 21, of which 12 were waited for; matrix products, arithmetic and copies ran while one was open for 0% of the time, Pallas kernels for 14%

profile of v6, /device:TPU:0, one launch (start us, length us, event | category | flops | bytes accessed | tf_op | source)
XLA Modules:
  0.0 65.1 jit_solution(14683019461847211259)
XLA Ops:
  0.0 2.9 %first.1 = (f32[128,128]{1,0:T(8,128)S(1)}, f32[128,64,128]{2,1,0:T(8,128)S(1)}, bf16[512,128]{1,0:T(8,128)(2,1)S(1)}) custom-call(s32[3]{0:T(128)} %chain.5, s32[1,1,3]{2,1,0:T(1,128)} %counts.5, s32[1,128]{1,0:T(1,128)} %bitcast.11, s32[3,2,256]{2,1,0:T(2,128)} %bitcast.8, f32[3,128,64,128]{3,2,1,0:T(8,128)} %bitcast.4), custom_call_target="tpu_custom_call" | custom-call | tf_op jit(solution)/shard_map/first/pallas_call | solution.py:201
  5.1 4.2 %collective-permute-start.2 = (f32[128,128]{1,0:T(8,128)S(1)}, f32[128,128]{1,0:T(8,128)S(1)}, u32[]{:S(2)}, u32[]{:S(2)}) collective-permute-start(f32[128,128]{1,0:T(8,128)S(1)} %add.65), channel_id=1, source_target_pairs={{0,4},{1,5},{2,6},{3,7},{4,0},{5,1},{6,2},{7,3},{8,12},{9,13},{10,... | collective-permute-start | bytes 196616 | tf_op jit(solution)/shard_map/ppermute | solution.py:285
  9.3 1.1 %collective-permute-start.4 = (f32[128,128]{1,0:T(8,128)S(1)}, f32[128,128]{1,0:T(8,128)S(1)}, u32[]{:S(2)}, u32[]{:S(2)}) collective-permute-start(f32[128,128]{1,0:T(8,128)S(1)} %slice.51), channel_id=1, source_target_pairs={{0,2},{1,7},{2,0},{3,5},{4,6},{5,3},{6,4},{7,1},{8,10},{9,15},{10,... | collective-permute-start | bytes 196616 | tf_op jit(solution)/shard_map/ppermute | solution.py:285
  11.0 2.7 %collective-permute-done.2 = f32[128,128]{1,0:T(8,128)S(1)} collective-permute-done((f32[128,128]{1,0:T(8,128)S(1)}, f32[128,128]{1,0:T(8,128)S(1)}, u32[]{:S(2)}, u32[]{:S(2)}) %collective-permute-start.2) | collective-permute-done | bytes 65568 | tf_op jit(solution)/shard_map/ppermute | solution.py:285
  13.7 1.8 %collective-permute-done.4 = f32[128,128]{1,0:T(8,128)S(1)} collective-permute-done((f32[128,128]{1,0:T(8,128)S(1)}, f32[128,128]{1,0:T(8,128)S(1)}, u32[]{:S(2)}, u32[]{:S(2)}) %collective-permute-start.4) | collective-permute-done | bytes 65568 | tf_op jit(solution)/shard_map/ppermute | solution.py:285
  15.4 1.2 %collective-permute-done.3 = f32[128,128]{1,0:T(8,128)S(1)} collective-permute-done((f32[128,128]{1,0:T(8,128)S(1)}, f32[128,128]{1,0:T(8,128)S(1)}, u32[]{:S(2)}, u32[]{:S(2)}) %collective-permute-start.3) | collective-permute-done | bytes 65568 | tf_op jit(solution)/shard_map/ppermute | solution.py:285
  16.6 2.0 %collective-permute-start.5 = (f32[128,128]{1,0:T(8,128)S(1)}, f32[128,128]{1,0:T(8,128)S(1)}, u32[]{:S(2)}, u32[]{:S(2)}) collective-permute-start(f32[128,128]{1,0:T(8,128)S(1)} %fusion.5.refs_0_), channel_id=1, source_target_pairs={{0,8},{8,0},{16,24},{24,16},{1,9},{9,1},{17,25},{25,17},{2,10},{10... | collective-permute-start | bytes 196616 | tf_op jit(solution)/shard_map/ppermute | solution.py:257
  18.6 1.2 %collective-permute-start.6 = (f32[128,128]{1,0:T(8,128)S(1)}, f32[128,128]{1,0:T(8,128)S(1)}, u32[]{:S(2)}, u32[]{:S(2)}) collective-permute-start(f32[128,128]{1,0:T(8,128)S(1)} %fusion.5.refs_0_), channel_id=1, source_target_pairs={{0,16},{8,24},{16,0},{24,8},{1,17},{9,25},{17,1},{25,9},{2,18},{10... | collective-permute-start | bytes 196616 | tf_op jit(solution)/shard_map/ppermute | solution.py:257
  20.2 3.0 %shard_map.56 = (bf16[512,512]{1,0:T(8,128)(2,1)S(1)}, bf16[512,512]{1,0:T(8,128)(2,1)S(1)}, bf16[512,512]{1,0:T(8,128)(2,1)S(1)}, bf16[512,512]{1,0:T(8,128)(2,1)S(1)}) custom-call(s32[3]{0:T(128)} %chain.5, s32[1,1,3]{2,1,0:T(1,128)} %counts.5, s32[3,2,256]{2,1,0:T(2,128)} %bitcast.9, f32[3,128,64,128]{3,2,1,0:T(8,128)} %bitcast.5), custom_call_target="tpu_custom_call" | custom-call | bytes 8388608 | tf_op jit(solution)/shard_map/pallas_call | solution.py:224
  23.2 1.8 %collective-permute-done.7.refs_3_ = f32[128,128]{1,0:T(8,128)S(1)} collective-permute-done((f32[128,128]{1,0:T(8,128)S(1)}, f32[128,128]{1,0:T(8,128)S(1)}, u32[]{:S(2)}, u32[]{:S(2)}) %collective-permute-start.7) | collective-permute-done | bytes 65568 | tf_op jit(solution)/shard_map/ppermute | solution.py:257
  27.2 1.5 %collective-permute-start.10 = (f32[128,128]{1,0:T(8,128)S(1)}, f32[128,128]{1,0:T(8,128)S(1)}, u32[]{:S(2)}, u32[]{:S(2)}) collective-permute-start(f32[128,128]{1,0:T(8,128)S(1)} %add.71), channel_id=1, source_target_pairs={{0,4},{1,5},{2,6},{3,7},{4,0},{5,1},{6,2},{7,3},{8,12},{9,13},{10,... | collective-permute-start | bytes 196616 | tf_op jit(solution)/shard_map/ppermute | solution.py:285
  28.8 0.6 collective-permute-start.11
  29.4 1.6 %collective-permute-start.12 = (f32[128,128]{1,0:T(8,128)S(1)}, f32[128,128]{1,0:T(8,128)S(1)}, u32[]{:S(2)}, u32[]{:S(2)}) collective-permute-start(f32[128,128]{1,0:T(8,128)S(1)} %slice.55), channel_id=1, source_target_pairs={{0,2},{1,7},{2,0},{3,5},{4,6},{5,3},{6,4},{7,1},{8,10},{9,15},{10,... | collective-permute-start | bytes 196616 | tf_op jit(solution)/shard_map/ppermute | solution.py:285
  31.0 2.2 %collective-permute-done.10 = f32[128,128]{1,0:T(8,128)S(1)} collective-permute-done((f32[128,128]{1,0:T(8,128)S(1)}, f32[128,128]{1,0:T(8,128)S(1)}, u32[]{:S(2)}, u32[]{:S(2)}) %collective-permute-start.10) | collective-permute-done | bytes 65568 | tf_op jit(solution)/shard_map/ppermute | solution.py:285
  33.2 1.8 %collective-permute-done.11 = f32[128,128]{1,0:T(8,128)S(1)} collective-permute-done((f32[128,128]{1,0:T(8,128)S(1)}, f32[128,128]{1,0:T(8,128)S(1)}, u32[]{:S(2)}, u32[]{:S(2)}) %collective-permute-start.11) | collective-permute-done | bytes 65568 | tf_op jit(solution)/shard_map/ppermute | solution.py:285
  35.6 1.3 %collective-permute-start.13 = (f32[128,128]{1,0:T(8,128)S(1)}, f32[128,128]{1,0:T(8,128)S(1)}, u32[]{:S(2)}, u32[]{:S(2)}) collective-permute-start(f32[128,128]{1,0:T(8,128)S(1)} %fusion.3.refs_0_), channel_id=1, source_target_pairs={{0,8},{8,0},{16,24},{24,16},{1,9},{9,1},{17,25},{25,17},{2,10},{10... | collective-permute-start | bytes 196616 | tf_op jit(solution)/shard_map/ppermute | solution.py:257
  37.1 2.0 %collective-permute-start.15 = (f32[128,128]{1,0:T(8,128)S(1)}, f32[128,128]{1,0:T(8,128)S(1)}, u32[]{:S(2)}, u32[]{:S(2)}) collective-permute-start(f32[128,128]{1,0:T(8,128)S(1)} %fusion.3.refs_0_), channel_id=1, source_target_pairs={{0,24},{8,16},{16,8},{24,0},{1,25},{9,17},{17,9},{25,1},{2,26},{10... | collective-permute-start | bytes 196616 | tf_op jit(solution)/shard_map/ppermute | solution.py:257
  39.1 3.4 %shard_map.55 = (bf16[512,512]{1,0:T(8,128)(2,1)S(1)}, bf16[512,512]{1,0:T(8,128)(2,1)S(1)}, bf16[512,512]{1,0:T(8,128)(2,1)S(1)}, bf16[512,512]{1,0:T(8,128)(2,1)S(1)}) custom-call(s32[3]{0:T(128)} %chain.5, s32[1,1,3]{2,1,0:T(1,128)} %counts.5, s32[3,2,256]{2,1,0:T(2,128)} %bitcast.10, f32[3,128,64,128]{3,2,1,0:T(8,128)} %bitcast.6), custom_call_target="tpu_custom_call" | custom-call | bytes 8388608 | tf_op jit(solution)/shard_map/pallas_call | solution.py:224
  44.8 2.2 %collective-permute-start.18 = (f32[128,128]{1,0:T(8,128)S(1)}, f32[128,128]{1,0:T(8,128)S(1)}, u32[]{:S(2)}, u32[]{:S(2)}) collective-permute-start(f32[128,128]{1,0:T(8,128)S(1)} %add.77), channel_id=1, source_target_pairs={{0,4},{1,5},{2,6},{3,7},{4,0},{5,1},{6,2},{7,3},{8,12},{9,13},{10,... | collective-permute-start | bytes 196616 | tf_op jit(solution)/shard_map/ppermute | solution.py:285
  47.1 1.2 %collective-permute-start.19 = (f32[128,128]{1,0:T(8,128)S(1)}, f32[128,128]{1,0:T(8,128)S(1)}, u32[]{:S(2)}, u32[]{:S(2)}) collective-permute-start(f32[128,128]{1,0:T(8,128)S(1)} %slice_add_fusion.3), channel_id=1, source_target_pairs={{0,6},{1,3},{2,4},{3,1},{4,2},{5,7},{6,0},{7,5},{8,14},{9,11},{10,... | collective-permute-start | bytes 196616 | tf_op jit(solution)/shard_map/ppermute | solution.py:285
  48.6 3.3 %collective-permute-done.18 = f32[128,128]{1,0:T(8,128)S(1)} collective-permute-done((f32[128,128]{1,0:T(8,128)S(1)}, f32[128,128]{1,0:T(8,128)S(1)}, u32[]{:S(2)}, u32[]{:S(2)}) %collective-permute-start.18) | collective-permute-done | bytes 65568 | tf_op jit(solution)/shard_map/ppermute | solution.py:285
  51.9 1.7 %collective-permute-done.19 = f32[128,128]{1,0:T(8,128)S(1)} collective-permute-done((f32[128,128]{1,0:T(8,128)S(1)}, f32[128,128]{1,0:T(8,128)S(1)}, u32[]{:S(2)}, u32[]{:S(2)}) %collective-permute-start.19) | collective-permute-done | bytes 65568 | tf_op jit(solution)/shard_map/ppermute | solution.py:285
  54.1 10.3 %all_to_all.6 = f32[32,1,128]{2,1,0:T(1,128)S(1)} all-to-all(f32[32,1,128]{2,1,0:T(1,128)S(1)} %broadcast_in_dim.5), channel_id=1, replica_groups=mesh['row'=4,'col'=8] {'row','col'}, dimensions={0} | all-to-all | bytes 32768 | tf_op jit(solution)/shard_map/all_to_all | solution.py:297
  64.4 0.6 broadcast_multiply_fusion
  (55 shorter events, 9.2 us)
Async XLA Ops:
  3.4 5.9 %collective-permute-start = (f32[384,128]{1,0:T(8,128)S(1)}, f32[384,128]{1,0:T(8,128)S(1)}, u32[]{:S(2)}, u32[]{:S(2)}) collective-permute-start(f32[384,128]{1,0:T(8,128)S(1)} %one_hot_part.5), channel_id=1, source_target_pairs={{0,1},{1,0},{2,3},{3,2},{4,5},{5,4},{6,7},{7,6},{8,9},{9,8},{10,11... | collective-permute-start | bytes 589832 | tf_op jit(solution)/shard_map/ppermute | solution.py:257
  3.7 1.4 %collective-permute-start.1 = (f32[128,128]{1,0:T(8,128)S(1)}, f32[128,128]{1,0:T(8,128)S(1)}, u32[]{:S(2)}, u32[]{:S(2)}) collective-permute-start(f32[128,128]{1,0:T(8,128)S(1)} %get-tuple-element.30), channel_id=1, source_target_pairs={{0,1},{1,0},{2,3},{3,2},{4,5},{5,4},{6,7},{7,6},{8,9},{9,8},{10,11... | collective-permute-start | bytes 196616 | tf_op jit(solution)/shard_map/ppermute | solution.py:257
  5.1 8.6 %collective-permute-start.2 = (f32[128,128]{1,0:T(8,128)S(1)}, f32[128,128]{1,0:T(8,128)S(1)}, u32[]{:S(2)}, u32[]{:S(2)}) collective-permute-start(f32[128,128]{1,0:T(8,128)S(1)} %add.65), channel_id=1, source_target_pairs={{0,4},{1,5},{2,6},{3,7},{4,0},{5,1},{6,2},{7,3},{8,12},{9,13},{10,... | collective-permute-start | bytes 196616 | tf_op jit(solution)/shard_map/ppermute | solution.py:285
  9.3 6.1 %collective-permute-start.4 = (f32[128,128]{1,0:T(8,128)S(1)}, f32[128,128]{1,0:T(8,128)S(1)}, u32[]{:S(2)}, u32[]{:S(2)}) collective-permute-start(f32[128,128]{1,0:T(8,128)S(1)} %slice.51), channel_id=1, source_target_pairs={{0,2},{1,7},{2,0},{3,5},{4,6},{5,3},{6,4},{7,1},{8,10},{9,15},{10,... | collective-permute-start | bytes 196616 | tf_op jit(solution)/shard_map/ppermute | solution.py:285
  10.5 6.1 %collective-permute-start.3 = (f32[128,128]{1,0:T(8,128)S(1)}, f32[128,128]{1,0:T(8,128)S(1)}, u32[]{:S(2)}, u32[]{:S(2)}) collective-permute-start(f32[128,128]{1,0:T(8,128)S(1)} %slice_add_fusion.7), channel_id=1, source_target_pairs={{0,6},{1,3},{2,4},{3,1},{4,2},{5,7},{6,0},{7,5},{8,14},{9,11},{10,... | collective-permute-start | bytes 196616 | tf_op jit(solution)/shard_map/ppermute | solution.py:285
  16.6 6.6 %collective-permute-start.5 = (f32[128,128]{1,0:T(8,128)S(1)}, f32[128,128]{1,0:T(8,128)S(1)}, u32[]{:S(2)}, u32[]{:S(2)}) collective-permute-start(f32[128,128]{1,0:T(8,128)S(1)} %fusion.5.refs_0_), channel_id=1, source_target_pairs={{0,8},{8,0},{16,24},{24,16},{1,9},{9,1},{17,25},{25,17},{2,10},{10... | collective-permute-start | bytes 196616 | tf_op jit(solution)/shard_map/ppermute | solution.py:257
  18.6 4.6 %collective-permute-start.6 = (f32[128,128]{1,0:T(8,128)S(1)}, f32[128,128]{1,0:T(8,128)S(1)}, u32[]{:S(2)}, u32[]{:S(2)}) collective-permute-start(f32[128,128]{1,0:T(8,128)S(1)} %fusion.5.refs_0_), channel_id=1, source_target_pairs={{0,16},{8,24},{16,0},{24,8},{1,17},{9,25},{17,1},{25,9},{2,18},{10... | collective-permute-start | bytes 196616 | tf_op jit(solution)/shard_map/ppermute | solution.py:257
  19.8 5.2 %collective-permute-start.7 = (f32[128,128]{1,0:T(8,128)S(1)}, f32[128,128]{1,0:T(8,128)S(1)}, u32[]{:S(2)}, u32[]{:S(2)}) collective-permute-start(f32[128,128]{1,0:T(8,128)S(1)} %fusion.5.refs_0_), channel_id=1, source_target_pairs={{0,24},{8,16},{16,8},{24,0},{1,25},{9,17},{17,9},{25,1},{2,26},{10... | collective-permute-start | bytes 196616 | tf_op jit(solution)/shard_map/ppermute | solution.py:257
  25.6 3.1 %collective-permute-start.8 = (f32[384,128]{1,0:T(8,128)S(1)}, f32[384,128]{1,0:T(8,128)S(1)}, u32[]{:S(2)}, u32[]{:S(2)}) collective-permute-start(f32[384,128]{1,0:T(8,128)S(1)} %product.9), channel_id=1, source_target_pairs={{0,1},{1,0},{2,3},{3,2},{4,5},{5,4},{6,7},{7,6},{8,9},{9,8},{10,11... | collective-permute-start | bytes 589832 | tf_op jit(solution)/shard_map/ppermute | solution.py:257
  25.7 1.5 %collective-permute-start.9 = (f32[128,128]{1,0:T(8,128)S(1)}, f32[128,128]{1,0:T(8,128)S(1)}, u32[]{:S(2)}, u32[]{:S(2)}) collective-permute-start(f32[128,128]{1,0:T(8,128)S(1)} %get-tuple-element.32), channel_id=1, source_target_pairs={{0,1},{1,0},{2,3},{3,2},{4,5},{5,4},{6,7},{7,6},{8,9},{9,8},{10,11... | collective-permute-start | bytes 196616 | tf_op jit(solution)/shard_map/ppermute | solution.py:257
  27.2 6.0 %collective-permute-start.10 = (f32[128,128]{1,0:T(8,128)S(1)}, f32[128,128]{1,0:T(8,128)S(1)}, u32[]{:S(2)}, u32[]{:S(2)}) collective-permute-start(f32[128,128]{1,0:T(8,128)S(1)} %add.71), channel_id=1, source_target_pairs={{0,4},{1,5},{2,6},{3,7},{4,0},{5,1},{6,2},{7,3},{8,12},{9,13},{10,... | collective-permute-start | bytes 196616 | tf_op jit(solution)/shard_map/ppermute | solution.py:285
  28.8 6.2 %collective-permute-start.11 = (f32[128,128]{1,0:T(8,128)S(1)}, f32[128,128]{1,0:T(8,128)S(1)}, u32[]{:S(2)}, u32[]{:S(2)}) collective-permute-start(f32[128,128]{1,0:T(8,128)S(1)} %slice_add_fusion.5), channel_id=1, source_target_pairs={{0,6},{1,3},{2,4},{3,1},{4,2},{5,7},{6,0},{7,5},{8,14},{9,11},{10,... | collective-permute-start | bytes 196616 | tf_op jit(solution)/shard_map/ppermute | solution.py:285
  29.4 6.2 %collective-permute-start.12 = (f32[128,128]{1,0:T(8,128)S(1)}, f32[128,128]{1,0:T(8,128)S(1)}, u32[]{:S(2)}, u32[]{:S(2)}) collective-permute-start(f32[128,128]{1,0:T(8,128)S(1)} %slice.55), channel_id=1, source_target_pairs={{0,2},{1,7},{2,0},{3,5},{4,6},{5,3},{6,4},{7,1},{8,10},{9,15},{10,... | collective-permute-start | bytes 196616 | tf_op jit(solution)/shard_map/ppermute | solution.py:285
  35.6 7.0 %collective-permute-start.13 = (f32[128,128]{1,0:T(8,128)S(1)}, f32[128,128]{1,0:T(8,128)S(1)}, u32[]{:S(2)}, u32[]{:S(2)}) collective-permute-start(f32[128,128]{1,0:T(8,128)S(1)} %fusion.3.refs_0_), channel_id=1, source_target_pairs={{0,8},{8,0},{16,24},{24,16},{1,9},{9,1},{17,25},{25,17},{2,10},{10... | collective-permute-start | bytes 196616 | tf_op jit(solution)/shard_map/ppermute | solution.py:257
  36.9 5.7 %collective-permute-start.14 = (f32[128,128]{1,0:T(8,128)S(1)}, f32[128,128]{1,0:T(8,128)S(1)}, u32[]{:S(2)}, u32[]{:S(2)}) collective-permute-start(f32[128,128]{1,0:T(8,128)S(1)} %fusion.3.refs_0_), channel_id=1, source_target_pairs={{0,16},{8,24},{16,0},{24,8},{1,17},{9,25},{17,1},{25,9},{2,18},{10... | collective-permute-start | bytes 196616 | tf_op jit(solution)/shard_map/ppermute | solution.py:257
  37.1 5.5 %collective-permute-start.15 = (f32[128,128]{1,0:T(8,128)S(1)}, f32[128,128]{1,0:T(8,128)S(1)}, u32[]{:S(2)}, u32[]{:S(2)}) collective-permute-start(f32[128,128]{1,0:T(8,128)S(1)} %fusion.3.refs_0_), channel_id=1, source_target_pairs={{0,24},{8,16},{16,8},{24,0},{1,25},{9,17},{17,9},{25,1},{2,26},{10... | collective-permute-start | bytes 196616 | tf_op jit(solution)/shard_map/ppermute | solution.py:257
  43.2 3.8 %collective-permute-start.16 = (f32[384,128]{1,0:T(8,128)S(1)}, f32[384,128]{1,0:T(8,128)S(1)}, u32[]{:S(2)}, u32[]{:S(2)}) collective-permute-start(f32[384,128]{1,0:T(8,128)S(1)} %product.13), channel_id=1, source_target_pairs={{0,1},{1,0},{2,3},{3,2},{4,5},{5,4},{6,7},{7,6},{8,9},{9,8},{10,11... | collective-permute-start | bytes 589832 | tf_op jit(solution)/shard_map/ppermute | solution.py:257
  43.3 1.5 %collective-permute-start.17 = (f32[128,128]{1,0:T(8,128)S(1)}, f32[128,128]{1,0:T(8,128)S(1)}, u32[]{:S(2)}, u32[]{:S(2)}) collective-permute-start(f32[128,128]{1,0:T(8,128)S(1)} %get-tuple-element.34), channel_id=1, source_target_pairs={{0,1},{1,0},{2,3},{3,2},{4,5},{5,4},{6,7},{7,6},{8,9},{9,8},{10,11... | collective-permute-start | bytes 196616 | tf_op jit(solution)/shard_map/ppermute | solution.py:257
  44.8 7.0 %collective-permute-start.18 = (f32[128,128]{1,0:T(8,128)S(1)}, f32[128,128]{1,0:T(8,128)S(1)}, u32[]{:S(2)}, u32[]{:S(2)}) collective-permute-start(f32[128,128]{1,0:T(8,128)S(1)} %add.77), channel_id=1, source_target_pairs={{0,4},{1,5},{2,6},{3,7},{4,0},{5,1},{6,2},{7,3},{8,12},{9,13},{10,... | collective-permute-start | bytes 196616 | tf_op jit(solution)/shard_map/ppermute | solution.py:285
  47.1 6.5 %collective-permute-start.19 = (f32[128,128]{1,0:T(8,128)S(1)}, f32[128,128]{1,0:T(8,128)S(1)}, u32[]{:S(2)}, u32[]{:S(2)}) collective-permute-start(f32[128,128]{1,0:T(8,128)S(1)} %slice_add_fusion.3), channel_id=1, source_target_pairs={{0,6},{1,3},{2,4},{3,1},{4,2},{5,7},{6,0},{7,5},{8,14},{9,11},{10,... | collective-permute-start | bytes 196616 | tf_op jit(solution)/shard_map/ppermute | solution.py:285
  48.3 5.7 %collective-permute-start.20 = (f32[128,128]{1,0:T(8,128)S(1)}, f32[128,128]{1,0:T(8,128)S(1)}, u32[]{:S(2)}, u32[]{:S(2)}) collective-permute-start(f32[128,128]{1,0:T(8,128)S(1)} %slice.59), channel_id=1, source_target_pairs={{0,2},{1,7},{2,0},{3,5},{4,6},{5,3},{6,4},{7,1},{8,10},{9,15},{10,... | collective-permute-start | bytes 196616 | tf_op jit(solution)/shard_map/ppermute | solution.py:285
